TPU v7x, 512 devices: a whole 4x4x16 slice. The times are simulated.
512 devices in a mesh: lists: 128 (over z, x, core), help: 4 (over y).
Axes of the slice: x: 4, y: 4, z: 16, core: 2. Of those that a mesh axis runs over, the one named last changes fastest.
Arguments:
- vectors: float32 [256, 1024, 768], P('lists', 'help'), may hold values from -6 to 6
- labels: int32 [256, 1024], P('lists', 'help'), may hold values from 0 to 1, as said below
- list_sizes: int32 [256], P('lists'), may hold values from 64 to 1024, as said below
- centroids: float32 [256, 768], P('lists'), may hold values from -4 to 4
- split_ids: int32 [64], replicated, may hold values from 0 to 255, as said below
- nearby: int32 [64, 8], replicated, may hold values from 0 to 255, as said below
- owner_map: int32 [256], replicated, may hold values from 0 to 255, as said below
- mover_source: int32 [65536], P(('lists', 'help')), may hold values from 0 to 511, as said below
- mover_dest: int32 [65536], P(('lists', 'help')), may hold values from -1 to 255, as said below
Outputs:
- gains: float32 [256, 1024], P('lists', 'help')
- arrivals: float32 [256, 512, 768], P('lists')
Inputs may be any that keep to these rules, and one draw needn't show every extreme that they name: `split_ids`: distinct list ids. `nearby`: for each split, 8 distinct list ids, none equal to the split list. `owner_map`: a permutation of the slots. `list_sizes`: every list has at least two live rows; every split list has at least 576 live rows; the first slot of every index of lists that does not hold a split list holds at least 832 live rows. `labels`: row 0 of every list has label 0 and row 1 label 1. `mover_source`: distinct rows of the source device's block, live ones first. `mover_dest`: -1 exactly where the mover's source row is not live; from one device at most 2 live movers go to lists stored on one index of lists; every list slot receives at most 512 rows in all. Numbers of movers counted from these ids (per device and slot, or running totals of them) are small exact integers and may cross devices in any exact integer encoding, several to a word.
All inputs are finite; a program needn't handle non-finite values.
Results may differ from a plain program's by a relative error of at most 0.0003.
Values sent between devices are 32-bit elements; how exact they have to be, the bound alone decides.
No kernel may reach another device: no remote copies, remote signals or barrier semaphores. Data moves between devices by JAX's collectives and lax.ppermute only.
A program may use at most 64 MiB of HBM per device.

v0:
```python
import jax
import jax.numpy as jnp
from jax import lax
from jax.experimental import pallas as pl
from jax.experimental.pallas import tpu as pltpu
from jax.sharding import Mesh
from jax.sharding import PartitionSpec as P

NEAR = ("z_lo", "x", "core")
LISTS = ("z_hi", *NEAR)
LANES = 128
HIGH = lax.Precision.HIGHEST


def exchanged(pieces, axis):
    return lax.all_to_all(pieces, axis, 0, 0, tiled=True)


def copies(shard, axis):
    length = lax.axis_size(axis)
    return exchanged(jnp.broadcast_to(shard[None], (length, *shard.shape)), axis)


def turned(block, axis, step):
    length = lax.axis_size(axis)
    return lax.ppermute(block, axis, [(i, (i + step) % length) for i in range(length)])


def select_kernel(cols, depth, key, tail, out):
    lines = tail.shape[0]
    pairs = key.shape[1]
    rows = tail[:, 0, :].T
    line = lax.broadcasted_iota(jnp.int32, (lines, pairs), 0)
    pick = (line == key[...]).astype(jnp.float32)
    chosen = jnp.dot(rows, pick, precision=HIGH, preferred_element_type=jnp.float32)
    each = LANES // 4
    splits = pairs // 2
    own = [
        chosen[a * each : (a + 1) * each, :splits]
        + chosen[(a + 2) * each : (a + 3) * each, splits:]
        for a in range(2)
    ]
    for y in range(out.shape[0]):
        for a in range(2):
            out[y, :, a * splits : (a + 1) * splits] = own[a]
        for r in range(depth):
            at = cols + 1 + r
            out[y, at : at + 1, :] = rows[at : at + 1, :]


def selected(key, tail, cols, depth, helpers):
    vmem = pl.BlockSpec(memory_space=pltpu.VMEM)
    return pl.pallas_call(
        lambda *refs: select_kernel(cols, depth, *refs),
        out_shape=jax.ShapeDtypeStruct((helpers, LANES // 4, LANES), jnp.float32),
        in_specs=[vmem, vmem],
        out_specs=vmem,
        name="select",
    )(key, tail)


def put_rows(image, place, ref, base, start, width):
    def body(i, carry):
        for r in range(2):
            p = place[base + r, start + i]
            image[pl.ds(p, 1), :] = ref[i, :, r * width : (r + 1) * width]
        return carry

    lax.fori_loop(0, ref.shape[0], body, 0, unroll=4)


def near_kernel(width, total, skip, me, codes, own, below, above, image, place, spot, scalars, sem):
    lines = own.shape[0]
    code = jnp.concatenate([codes[y, skip : skip + 2, :] for y in range(4)], axis=0)
    before = (
        lax.broadcasted_iota(jnp.int32, (lines, lines), 0)
        < lax.broadcasted_iota(jnp.int32, (lines, lines), 1)
    ).astype(jnp.float32)
    places = jnp.full(code.shape, float(total), jnp.float32)
    for t in range(2):
        mark = (code == float(t + 1)).astype(jnp.float32)
        per_line = jnp.sum(mark, axis=0, keepdims=True)
        seen = jnp.dot(
            jnp.broadcast_to(per_line, code.shape), before, preferred_element_type=jnp.float32
        )[0:1]
        ahead = []
        for row in range(code.shape[0]):
            ahead.append(seen)
            seen = seen + mark[row : row + 1]
        ahead = jnp.concatenate(ahead, axis=0)
        places = jnp.where(mark > 0.0, ahead + float(t * total // 2), places)
    spot[...] = places.astype(jnp.int32)
    copy = pltpu.make_async_copy(spot, scalars, sem)
    copy.start()
    place[...] = spot[...]
    image[...] = jnp.zeros_like(image)
    copy.wait()
    for ref, turn in ((own, 0), (below, 3), (above, 1)):
        put_rows(image, scalars, ref, lax.rem(me[0] + turn, 4) * 2, 0, width)


def near_rows(me, codes, parts, width, total, skip):
    vmem = pl.BlockSpec(memory_space=pltpu.VMEM)
    return pl.pallas_call(
        lambda *refs: near_kernel(width, total, skip, *refs),
        out_shape=(
            pltpu.VMEM((total + 8, width), jnp.float32),
            jax.ShapeDtypeStruct((8, LANES), jnp.int32),
        ),
        in_specs=[pl.BlockSpec(memory_space=pltpu.SMEM), vmem] + [vmem] * len(parts),
        out_specs=(vmem, vmem),
        scratch_shapes=[
            pltpu.VMEM((8, LANES), jnp.int32),
            pltpu.SMEM((8, LANES), jnp.int32),
            pltpu.SemaphoreType.DMA,
        ],
        name="near",
    )(me, codes, *parts)


def far_kernel(width, total, me, place, low, high, old, image, out, sem):
    base = lax.rem(me[0] + 2, 4) * 2
    put_rows(image, place, low, base, 0, width)
    put_rows(image, place, high, base, low.shape[0], width)
    copy = pltpu.make_async_copy(image.at[pl.ds(0, total)], out, sem)
    copy.start()
    copy.wait()


def far_rows(me, place, parts, image, width, total):
    vmem = pl.BlockSpec(memory_space=pltpu.VMEM)
    smem = pl.BlockSpec(memory_space=pltpu.SMEM)
    return pl.pallas_call(
        lambda *refs: far_kernel(width, total, *refs),
        out_shape=(
            pltpu.VMEM(image.shape, jnp.float32),
            jax.ShapeDtypeStruct((total, width), jnp.float32),
        ),
        in_specs=[smem, smem] + [vmem] * (len(parts) + 1),
        out_specs=(vmem, pl.BlockSpec(memory_space=pl.ANY)),
        scratch_shapes=[pltpu.SemaphoreType.DMA],
        input_output_aliases={2 + len(parts): 0},
        name="far",
    )(me, place, *parts, image)[1]


def local(
    vectors, labels, list_sizes, centroids, split_ids, nearby, owner_map, mover_source, mover_dest
):
    list_dev, rows, width = vectors.shape
    lists_count = lax.axis_size(LISTS)
    help_count = lax.axis_size("help")
    my_line = lax.axis_index(LISTS)
    my_help = lax.axis_index("help")
    first = my_line * list_dev
    start_row = my_help * rows
    splits = split_ids.shape[0]
    local_slots = first + jnp.arange(list_dev, dtype=jnp.int32)
    row_index = start_row + jnp.arange(rows, dtype=jnp.int32)
    valid = row_index[None, :] < list_sizes[:, None]
    moves = mover_source.shape[0]
    ids = jnp.arange(owner_map.shape[0], dtype=jnp.int32)
    devs = jnp.arange(lists_count, dtype=jnp.int32)
    depth = 2

    live = mover_dest >= 0
    slot = jnp.sum(
        jnp.where(mover_dest[:, None] == ids[None, :], owner_map[None, :], 0), axis=1
    )
    dev = jnp.where(live, slot // list_dev, -1)
    order = jnp.arange(moves, dtype=jnp.int32)
    same = (dev[:, None] == dev[None, :]) & (order[:, None] > order[None, :])
    rank = jnp.sum(same.astype(jnp.int32), axis=1)
    to = dev[:, None] == devs[None, :]
    picked = [to & (rank == r)[:, None] for r in range(depth)]
    codes = [
        jnp.sum(jnp.where(p, (slot % list_dev + 1)[:, None], 0), axis=0) for p in picked
    ]
    takes = [jnp.sum(jnp.where(p, mover_source[:, None], 0), axis=0) for p in picked]
    flat_rows = vectors.reshape(list_dev * rows, width)
    sent = [flat_rows[t] for t in takes]

    halves = jnp.stack([(labels == 0) & valid, (labels == 1) & valid], axis=1).astype(jnp.float32)
    partial_value = jnp.einsum("kar,krd->kad", halves, vectors, precision=HIGH)
    counts = jnp.sum(halves, axis=2)
    chunks = lax.axis_size(NEAR)
    cols = width // chunks
    half = list_dev * 2
    lanes = jnp.moveaxis(partial_value.reshape(half, chunks, cols), 1, 0)
    lanes = jnp.concatenate(
        [
            lanes,
            jnp.broadcast_to(counts.reshape(1, half, 1), (chunks, half, 1)),
            jnp.zeros((chunks, half, LANES // half - cols - 1), jnp.float32),
        ],
        axis=2,
    ).reshape(chunks, LANES)
    lanes = jnp.tile(lanes, (lists_count // chunks, 1))
    lane = jnp.arange(LANES, dtype=jnp.int32)
    for r in range(depth):
        lanes = jnp.where(
            lane[None, :] == cols + 1 + r, codes[r].astype(jnp.float32)[:, None], lanes
        )
    bucket = jnp.concatenate([*sent, lanes], axis=1)[:, None, :]
    got = exchanged(bucket, LISTS)

    split_slots = owner_map[split_ids]
    k_ids = jnp.arange(list_dev, dtype=jnp.int32)[:, None]
    key = jnp.where(split_slots[None] % list_dev == k_ids, split_slots[None] // list_dev, -1)
    tail = got[:, :, depth * width :]
    chosen = selected(key.reshape(1, list_dev * splits), tail, cols, depth, help_count)
    over_help = exchanged(chosen, "help")
    sums = jnp.sum(over_help[:, : cols + 1], axis=0)
    means = sums[:cols] / sums[cols:]
    cents = copies(means, NEAR).reshape(width, 2 * splits)

    sq_cent = jnp.sum(cents * cents, axis=0)
    near_slots = owner_map[nearby]
    hit = jnp.any(near_slots[None, :, :] == local_slots[:, None, None], axis=2)
    paired = jnp.tile(hit, (1, 2))
    cross = jnp.einsum("krd,dc->krc", vectors, cents, precision=HIGH)
    far = jnp.min(jnp.where(paired[:, None, :], sq_cent[None, None, :] - 2.0 * cross, 1e30), axis=2)
    own_cross = jnp.einsum("krd,kd->kr", vectors, centroids, precision=HIGH)
    own_dist = jnp.sum(centroids * centroids, axis=1)[:, None] - 2.0 * own_cross
    touched = valid & jnp.any(hit, axis=1)[:, None]
    gains = jnp.where(touched, (own_dist - far) / width, 0.0)

    cut = lists_count // 2
    own = got[:, :, : depth * width]
    below = turned(own, "help", 1)
    above = turned(own, "help", -1)
    far_low = turned(below[:cut], "help", 1)
    far_high = turned(above[cut:], "help", -1)
    arrive_cap = lists_count * help_count * ((depth + list_dev - 1) // list_dev)
    total = list_dev * arrive_cap
    me = my_help[None]
    image, place = near_rows(me, over_help, [own, below, above], width, total, cols + 1)
    out = far_rows(me, place, [far_low, far_high], image, width, total)
    return gains, out.reshape(list_dev, arrive_cap, width)


def solution(mesh):
    split = Mesh(
        mesh.devices.reshape(4, 4, 4, 2, mesh.shape["help"]), (*LISTS, "help")
    )
    placed = (
        P(LISTS, "help", None),
        P(LISTS, "help"),
        P(LISTS),
        P(LISTS, None),
        P(),
        P(),
        P(),
        P((*LISTS, "help")),
        P((*LISTS, "help")),
    )

    return jax.shard_map(
        local,
        mesh=split,
        in_specs=placed,
        out_specs=(P(LISTS, "help"), P(LISTS, None, None)),
        check_vma=False,
    )
```

profile of v0, /device:TPU:1, one launch (start us, length us, event | category | flops | bytes accessed | tf_op | source)
XLA Modules:
  0.0 145.6 jit_solution(2539423418138214041)
XLA Ops:
  0.7 1.0 select_reduce_fusion
  2.5 0.8 select_reduce_fusion.4
  4.3 2.0 %fusion.19 = f32[2,2,768]{2,1,0:T(2,128)S(1)} fusion(pred[2,2,256]{2,1,0:T(4,128)(4,1)S(1)} %get-tuple-element.15, f32[2,256,768]{2,1,0:T(8,128)} %param.9), kind=kOutput, calls=%fused_computation.75 | convolution fusion | flops 9437184 | bytes 1586176 | tf_op jit(solution)/shard_map/kar,krd->kad/dot_general | solution.py:184
  6.9 0.8 gather_fusion.3
  8.7 1.5 %broadcast_in_dim.170 = f32[128,1,1664]{2,1,0:T(1,128)} reshape(f32[128,1664]{1,0:T(8,128)S(1)} %pad_maximum_fusion) | data formatting | bytes 1703936 | tf_op jit(solution)/shard_map/broadcast_in_dim | solution.py:204
  10.2 20.4 %all-to-all-start = ((f32[128,1,1664]{2,1,0:T(1,128)}), f32[128,1,1664]{2,1,0:T(1,128)S(1)}, u32[]{:S(2)}, u32[]{:S(2)}) async-start(f32[128,1,1664]{2,1,0:T(1,128)} %broadcast_in_dim.170), calls=%async_computation | async-start | bytes 1703936 | tf_op jit(solution)/shard_map/all_to_all | solution.py:16
  32.0 43.2 %all-to-all-done = f32[128,1,1664]{2,1,0:T(1,128)S(1)} async-done(((f32[128,1,1664]{2,1,0:T(1,128)}), f32[128,1,1664]{2,1,0:T(1,128)S(1)}, u32[]{:S(2)}, u32[]{:S(2)}) %all-to-all-start) | async-done | bytes 852000 | tf_op jit(solution)/shard_map/all_to_all | solution.py:16
  75.9 1.9 %select.42 = f32[4,32,128]{2,1,0:T(8,128)} custom-call(s32[1,128]{1,0:T(1,128)} %select_n.120.refs_0_, f32[128,1,128]{2,1,0:T(1,128)} %slice.36.refs_1_), custom_call_target="tpu_custom_call" | custom-call | tf_op jit(solution)/shard_map/select/pallas_call | solution.py:53
  77.8 8.7 %all_to_all.15.refs_1_ = f32[4,32,128]{2,1,0:T(8,128)S(1)} all-to-all(f32[4,32,128]{2,1,0:T(8,128)} %select.42), channel_id=1, replica_groups=mesh['z_hi'=4,'z_lo'=4,'x'=4,'core'=2,'help'=4] {'help'}, dimensions={0} | all-to-all | bytes 131072 | tf_op jit(solution)/shard_map/all_to_all | solution.py:16
  87.3 9.2 %all-to-all-start.2 = ((f32[32,24,128]{2,1,0:T(8,128)}), f32[32,24,128]{2,1,0:T(8,128)}, u32[]{:S(2)}, u32[]{:S(2)}) async-start(f32[32,24,128]{2,1,0:T(8,128)} %broadcast_in_dim.171), calls=%async_computation.2 | async-start | bytes 786432 | tf_op jit(solution)/shard_map/all_to_all | solution.py:16
  96.6 2.8 %collective-permute-start.1 = (f32[128,1,1536]{2,1,0:T(1,128)S(1)}, f32[128,1,1536]{2,1,0:T(1,128)S(1)}, u32[]{:S(2)}, u32[]{:S(2)}) collective-permute-start(f32[128,1,1536]{2,1,0:T(1,128)S(1)} %slice.40.refs_2_), channel_id=1, source_target_pairs={{0,3},{1,0},{2,1},{3,2},{4,7},{5,4},{6,5},{7,6},{8,11},{9,8},{10,9... | collective-permute-start | bytes 2359304 | tf_op jit(solution)/shard_map/ppermute | solution.py:26
  99.4 2.5 %collective-permute-start = (f32[128,1,1536]{2,1,0:T(1,128)S(1)}, f32[128,1,1536]{2,1,0:T(1,128)}, u32[]{:S(2)}, u32[]{:S(2)}) collective-permute-start(f32[128,1,1536]{2,1,0:T(1,128)S(1)} %slice.40.refs_2_), channel_id=1, source_target_pairs={{0,1},{1,2},{2,3},{3,0},{4,5},{5,6},{6,7},{7,4},{8,9},{9,10},{10,1... | collective-permute-start | bytes 2359304 | tf_op jit(solution)/shard_map/ppermute | solution.py:26
  102.1 3.5 %gather_fusion = s32[512]{0:T(512)S(1)} fusion(s32[256]{0:T(256)S(1)} %copy-done, s32[1024]{0:T(1024)S(1)} %pad_clamp_fusion.3), kind=kCustom, calls=%fused_computation | custom fusion | bytes 6144 | tf_op jit(solution)/shard_map/gather | solution.py:218
  105.8 11.6 %collective-permute-done.1.refs_4_ = f32[128,1,1536]{2,1,0:T(1,128)S(1)} collective-permute-done((f32[128,1,1536]{2,1,0:T(1,128)S(1)}, f32[128,1,1536]{2,1,0:T(1,128)S(1)}, u32[]{:S(2)}, u32[]{:S(2)}) %collective-permute-start.1) | collective-permute-done | bytes 786464 | tf_op jit(solution)/shard_map/ppermute | solution.py:26
  117.4 0.8 slice.42
  118.2 3.9 %collective-permute-start.3 = (f32[64,1,1536]{2,1,0:T(1,128)}, f32[64,1,1536]{2,1,0:T(1,128)}, u32[]{:S(2)}, u32[]{:S(2)}) collective-permute-start(f32[64,1,1536]{2,1,0:T(1,128)} %slice.42), channel_id=1, source_target_pairs={{0,3},{1,0},{2,1},{3,2},{4,7},{5,4},{6,5},{7,6},{8,11},{9,8},{10,9... | collective-permute-start | bytes 1179656 | tf_op jit(solution)/shard_map/ppermute | solution.py:26
  122.1 1.8 %slice.41 = f32[64,1,1536]{2,1,0:T(1,128)} slice(f32[128,1,1536]{2,1,0:T(1,128)} %collective-permute-done.refs_3_), slice={[0:64], [0:1], [0:1536]} | slice | bytes 786432 | tf_op jit(solution)/shard_map/slice | solution.py:232
  123.9 1.9 %collective-permute-start.2 = (f32[64,1,1536]{2,1,0:T(1,128)}, f32[64,1,1536]{2,1,0:T(1,128)}, u32[]{:S(2)}, u32[]{:S(2)}) collective-permute-start(f32[64,1,1536]{2,1,0:T(1,128)} %slice.41), channel_id=1, source_target_pairs={{0,1},{1,2},{2,3},{3,0},{4,5},{5,6},{6,7},{7,4},{8,9},{9,10},{10,1... | collective-permute-start | bytes 1179656 | tf_op jit(solution)/shard_map/ppermute | solution.py:26
  126.3 1.4 fusion.8
  127.7 6.2 %near.1 = (f32[1032,768]{1,0:T(8,128)S(1)}, s32[8,128]{1,0:T(8,128)}) custom-call(s32[1]{0:T(128)} %bitcast.15.refs_0_, f32[4,32,128]{2,1,0:T(8,128)} %copy-done.4, f32[128,1,1536]{2,1,0:T(1,128)} %copy-done.2, f32[128,1,1536]{2,1,0:T(1,128)} %collective-permute-done.refs_3_, f32[128,1,1536]{2,1,0:T(1,128)} %copy-done.3), custom_call_target="tpu_custom_call" | custom-call | tf_op jit(solution)/shard_map/near/pallas_call | solution.py:104
  133.9 2.7 %collective-permute-done.2.refs_2_ = f32[64,1,1536]{2,1,0:T(1,128)} collective-permute-done((f32[64,1,1536]{2,1,0:T(1,128)}, f32[64,1,1536]{2,1,0:T(1,128)}, u32[]{:S(2)}, u32[]{:S(2)}) %collective-permute-start.2) | collective-permute-done | bytes 393248 | tf_op jit(solution)/shard_map/ppermute | solution.py:26
  136.6 3.8 %far.1 = (f32[1032,768]{1,0:T(8,128)S(1)}, f32[1024,768]{1,0:T(8,128)}) custom-call(s32[1]{0:T(128)} %bitcast.15.refs_0_, s32[8,128]{1,0:T(8,128)} %get-tuple-element.5.refs_1_, f32[64,1,1536]{2,1,0:T(1,128)} %collective-permute-done.2.refs_2_, f32[64,1,1536]{2,1,0:T(1,128)} %collective-permute-done.3.refs_3_, ...), custom_call_target="tpu_custom_call", output_to_operand_aliasing={{0}: (4, {})} | custom-call | tf_op jit(solution)/shard_map/far/pallas_call | solution.py:133
  140.4 1.1 multiply_reduce_fusion
  141.5 3.4 %fusion.3 = f32[2,256]{1,0:T(2,128)S(1)} fusion(f32[768,128,1]{1,0,2:T(8,128)} %bitcast.13, f32[2,256,768]{2,1,0:T(8,128)} %param.9, f32[128]{0:T(128)S(1)} %multiply_reduce_fusion, pred[2,128]{1,0:T(4,128)(4,1)S(1)} %tile.19), kind=kOutput, calls=%fused_computation.8 | convolution fusion | flops 604241408 | bytes 1968896 | tf_op jit(solution)/shard_map/krd,dc->krc/dot_general | solution.py:221
  (70 shorter events, 7.7 us)
Async XLA Ops:
  0.6 6.2 %copy-start.1 = (f32[2,256,768]{2,1,0:T(8,128)S(1)}, f32[2,256,768]{2,1,0:T(8,128)}, u32[]{:S(2)}) copy-start(f32[2,256,768]{2,1,0:T(8,128)} %param.9) | copy-start | bytes 4718596
  8.7 21.9 %copy-start.8 = (s32[64]{0:T(128)S(1)}, s32[64]{0:T(128)}, u32[]{:S(2)}) copy-start(s32[64]{0:T(128)} %param.13) | copy-start | bytes 772
  8.7 21.9 %copy-start = (s32[256]{0:T(256)S(1)}, s32[256]{0:T(256)}, u32[]{:S(2)}) copy-start(s32[256]{0:T(256)} %param.15) | copy-start | bytes 3076
  10.2 65.1 %all-to-all-start = ((f32[128,1,1664]{2,1,0:T(1,128)}), f32[128,1,1664]{2,1,0:T(1,128)S(1)}, u32[]{:S(2)}, u32[]{:S(2)}) async-start(f32[128,1,1664]{2,1,0:T(1,128)} %broadcast_in_dim.170), calls=%async_computation | async-start | bytes 1703936 | tf_op jit(solution)/shard_map/all_to_all | solution.py:16
  75.9 26.0 %copy-start.6 = (s32[64,8]{0,1:T(8,128)S(1)}, s32[64,8]{0,1:T(8,128)}, u32[]{:S(2)}) copy-start(s32[64,8]{0,1:T(8,128)} %param.14) | copy-start | bytes 6148
  86.5 19.1 %copy-start.4 = (f32[4,32,128]{2,1,0:T(8,128)}, f32[4,32,128]{2,1,0:T(8,128)S(1)}, u32[]{:S(2)}) copy-start(f32[4,32,128]{2,1,0:T(8,128)S(1)} %all_to_all.15.refs_1_) | copy-start | bytes 196612
  87.3 53.1 %all-to-all-start.2 = ((f32[32,24,128]{2,1,0:T(8,128)}), f32[32,24,128]{2,1,0:T(8,128)}, u32[]{:S(2)}, u32[]{:S(2)}) async-start(f32[32,24,128]{2,1,0:T(8,128)} %broadcast_in_dim.171), calls=%async_computation.2 | async-start | bytes 786432 | tf_op jit(solution)/shard_map/all_to_all | solution.py:16
  96.6 9.1 %copy-start.2 = (f32[128,1,1536]{2,1,0:T(1,128)}, f32[128,1,1536]{2,1,0:T(1,128)S(1)}, u32[]{:S(2)}) copy-start(f32[128,1,1536]{2,1,0:T(1,128)S(1)} %slice.40.refs_2_) | copy-start | bytes 2359300
  96.6 20.8 %collective-permute-start.1 = (f32[128,1,1536]{2,1,0:T(1,128)S(1)}, f32[128,1,1536]{2,1,0:T(1,128)S(1)}, u32[]{:S(2)}, u32[]{:S(2)}) collective-permute-start(f32[128,1,1536]{2,1,0:T(1,128)S(1)} %slice.40.refs_2_), channel_id=1, source_target_pairs={{0,3},{1,0},{2,1},{3,2},{4,7},{5,4},{6,5},{7,6},{8,11},{9,8},{10,9... | collective-permute-start | bytes 2359304 | tf_op jit(solution)/shard_map/ppermute | solution.py:26
  99.4 22.7 %collective-permute-start = (f32[128,1,1536]{2,1,0:T(1,128)S(1)}, f32[128,1,1536]{2,1,0:T(1,128)}, u32[]{:S(2)}, u32[]{:S(2)}) collective-permute-start(f32[128,1,1536]{2,1,0:T(1,128)S(1)} %slice.40.refs_2_), channel_id=1, source_target_pairs={{0,1},{1,2},{2,3},{3,0},{4,5},{5,6},{6,7},{7,4},{8,9},{9,10},{10,1... | collective-permute-start | bytes 2359304 | tf_op jit(solution)/shard_map/ppermute | solution.py:26
  105.7 20.5 %copy-start.5 = (f32[2,768]{1,0:T(2,128)S(1)}, f32[2,768]{1,0:T(2,128)}, u32[]{:S(2)}) copy-start(f32[2,768]{1,0:T(2,128)} %param.12) | copy-start | bytes 18436
  117.4 10.3 %copy-start.3 = (f32[128,1,1536]{2,1,0:T(1,128)}, f32[128,1,1536]{2,1,0:T(1,128)S(1)}, u32[]{:S(2)}) copy-start(f32[128,1,1536]{2,1,0:T(1,128)S(1)} %collective-permute-done.1.refs_4_) | copy-start | bytes 2359300
  118.2 15.6 %collective-permute-start.3 = (f32[64,1,1536]{2,1,0:T(1,128)}, f32[64,1,1536]{2,1,0:T(1,128)}, u32[]{:S(2)}, u32[]{:S(2)}) collective-permute-start(f32[64,1,1536]{2,1,0:T(1,128)} %slice.42), channel_id=1, source_target_pairs={{0,3},{1,0},{2,1},{3,2},{4,7},{5,4},{6,5},{7,6},{8,11},{9,8},{10,9... | collective-permute-start | bytes 1179656 | tf_op jit(solution)/shard_map/ppermute | solution.py:26
  123.9 12.6 %collective-permute-start.2 = (f32[64,1,1536]{2,1,0:T(1,128)}, f32[64,1,1536]{2,1,0:T(1,128)}, u32[]{:S(2)}, u32[]{:S(2)}) collective-permute-start(f32[64,1,1536]{2,1,0:T(1,128)} %slice.41), channel_id=1, source_target_pairs={{0,1},{1,2},{2,3},{3,0},{4,5},{5,6},{6,7},{7,4},{8,9},{9,10},{10,1... | collective-permute-start | bytes 1179656 | tf_op jit(solution)/shard_map/ppermute | solution.py:26
  140.4 4.5 %copy-start.7 = (s32[2]{0:T(128)S(1)}, s32[2]{0:T(128)}, u32[]{:S(2)}) copy-start(s32[2]{0:T(128)} %param.11) | copy-start | bytes 28
where the time goes:
time: 147 us; the launch traced here: 146 us
  waiting for transfers between devices  57.5 us (39%)
  starting transfers between devices  40.6 us (28%)
  local copies, waits for them, and re-layouts  13.1 us (9%)
  Pallas kernels  11.9 us (8%)
  blocking collectives  8.66 us (6%)
  matrix products  6.8 us (5%)
  other arithmetic  5.91 us (4%)
    all_to_all x2, waiting for transfers between devices, exchanged(): return lax.all_to_all(pieces, axis, 0, 0, tiled=True)  43.2 us
    all_to_all x2, starting transfers between devices, exchanged(): return lax.all_to_all(pieces, axis, 0, 0, tiled=True)  29.5 us
    ppermute x4, waiting for transfers between devices, turned(): lax.ppermute(block, axis, [(i, (i + step) % length) for i in range(length)])  14.3 us
    ppermute x4, starting transfers between devices, turned(): lax.ppermute(block, axis, [(i, (i + step) % length) for i in range(length)])  11.1 us
    all_to_all x1, blocking collectives, exchanged(): return lax.all_to_all(pieces, axis, 0, 0, tiled=True)  8.66 us
    pallas_call x1, Pallas kernels, near_rows(): pl.pallas_call(lambda *refs: near_kernel(width, total, skip, *refs), out_...  6.17 us
    pallas_call x1, Pallas kernels, far_rows(): pl.pallas_call(lambda *refs: far_kernel(width, total, *refs), out_shape=(...  3.82 us
    gather x3, local copies, waits for them, and re-layouts, local(): near_slots = owner_map[nearby]  3.65 us
  transfers between devices with their start and end apart: 6, of which 3 were waited for; matrix products, arithmetic and copies ran while one was open for 7% of the time, Pallas kernels for 7%

commit v1 on v0

--- a/solution.py
+++ b/solution.py
@@ -55,14 +55,15 @@
         out_shape=jax.ShapeDtypeStruct((helpers, LANES // 4, LANES), jnp.float32),
         in_specs=[vmem, vmem],
         out_specs=vmem,
+        compiler_params=pltpu.CompilerParams(vmem_limit_bytes=4 * 2**20),
         name="select",
     )(key, tail)
 
 
-def put_rows(image, place, ref, base, start, width):
+def put_rows(image, place, ref, base, width):
     def body(i, carry):
         for r in range(2):
-            p = place[base + r, start + i]
+            p = place[base + r, i]
             image[pl.ds(p, 1), :] = ref[i, :, r * width : (r + 1) * width]
         return carry
 
@@ -96,7 +97,7 @@
     image[...] = jnp.zeros_like(image)
     copy.wait()
     for ref, turn in ((own, 0), (below, 3), (above, 1)):
-        put_rows(image, scalars, ref, lax.rem(me[0] + turn, 4) * 2, 0, width)
+        put_rows(image, scalars, ref, lax.rem(me[0] + turn, 4) * 2, width)
 
 
 def near_rows(me, codes, parts, width, total, skip):
@@ -114,14 +115,13 @@
             pltpu.SMEM((8, LANES), jnp.int32),
             pltpu.SemaphoreType.DMA,
         ],
+        compiler_params=pltpu.CompilerParams(vmem_limit_bytes=16 * 2**20),
         name="near",
     )(me, codes, *parts)
 
 
-def far_kernel(width, total, me, place, low, high, old, image, out, sem):
-    base = lax.rem(me[0] + 2, 4) * 2
-    put_rows(image, place, low, base, 0, width)
-    put_rows(image, place, high, base, low.shape[0], width)
+def far_kernel(width, total, me, place, far, old, image, out, sem):
+    put_rows(image, place, far, lax.rem(me[0] + 2, 4) * 2, width)
     copy = pltpu.make_async_copy(image.at[pl.ds(0, total)], out, sem)
     copy.start()
     copy.wait()
@@ -140,6 +140,7 @@
         out_specs=(vmem, pl.BlockSpec(memory_space=pl.ANY)),
         scratch_shapes=[pltpu.SemaphoreType.DMA],
         input_output_aliases={2 + len(parts): 0},
+        compiler_params=pltpu.CompilerParams(vmem_limit_bytes=16 * 2**20),
         name="far",
     )(me, place, *parts, image)[1]
 
@@ -217,25 +218,23 @@
     sq_cent = jnp.sum(cents * cents, axis=0)
     near_slots = owner_map[nearby]
     hit = jnp.any(near_slots[None, :, :] == local_slots[:, None, None], axis=2)
+    own_cross = jnp.einsum("krd,kd->kr", vectors, centroids, precision=HIGH)
+    own_dist = jnp.sum(centroids * centroids, axis=1)[:, None] - 2.0 * own_cross
     paired = jnp.tile(hit, (1, 2))
     cross = jnp.einsum("krd,dc->krc", vectors, cents, precision=HIGH)
     far = jnp.min(jnp.where(paired[:, None, :], sq_cent[None, None, :] - 2.0 * cross, 1e30), axis=2)
-    own_cross = jnp.einsum("krd,kd->kr", vectors, centroids, precision=HIGH)
-    own_dist = jnp.sum(centroids * centroids, axis=1)[:, None] - 2.0 * own_cross
     touched = valid & jnp.any(hit, axis=1)[:, None]
     gains = jnp.where(touched, (own_dist - far) / width, 0.0)
 
-    cut = lists_count // 2
     own = got[:, :, : depth * width]
     below = turned(own, "help", 1)
     above = turned(own, "help", -1)
-    far_low = turned(below[:cut], "help", 1)
-    far_high = turned(above[cut:], "help", -1)
+    far = turned(own, "help", 2)
     arrive_cap = lists_count * help_count * ((depth + list_dev - 1) // list_dev)
     total = list_dev * arrive_cap
     me = my_help[None]
     image, place = near_rows(me, over_help, [own, below, above], width, total, cols + 1)
-    out = far_rows(me, place, [far_low, far_high], image, width, total)
+    out = far_rows(me, place, [far], image, width, total)
     return gains, out.reshape(list_dev, arrive_cap, width)
 
 

time: 147 us -> 148 us (level)
  waiting for transfers between devices: 57.5 us -> 69.4 us
  Pallas kernels: 11.9 us -> 9.02 us
  starting transfers between devices: 40.6 us -> 38 us
  matrix products: 6.8 us -> 4.85 us
  local copies, waits for them, and re-layouts: 13.1 us -> 11.4 us
    ppermute x4 -> x3, waiting for transfers between devices: 14.3 us -> 25.6 us  [turned(): lax.ppermute(block, axis, [(i, (i + step) % length) for i in range(length)])]
    ppermute x4 -> x3, starting transfers between devices: 11.1 us -> 8.42 us  [turned(): lax.ppermute(block, axis, [(i, (i + step) % length) for i in range(length)])]
    slice x2 -> x0, local copies, waits for them, and re-layouts: 2.61 us -> none  [the longest x1 1.78 us: local(): far_low = turned(below[:cut], 'help', 1)]
    pallas_call x1, Pallas kernels: 1.9 us -> 0.4 us  [selected(): pl.pallas_call(lambda *refs: select_kernel(cols, depth, *refs), out_shape...]
  transfers between devices with their start and end apart: 6 -> 5, of which waited for: 3 -> 3; matrix products, arithmetic and copies ran while one was open for 7% -> 5% of each run, Pallas kernels for 7% -> 6%
where the time goes in v1:
time: 148 us
  waiting for transfers between devices  69.4 us (47%)
  starting transfers between devices  38 us (26%)
  local copies, waits for them, and re-layouts  11.4 us (8%)
  Pallas kernels  9.02 us (6%)
  blocking collectives  8.46 us (6%)
  other arithmetic  5.92 us (4%)
  matrix products  4.85 us (3%)
    all_to_all x2, waiting for transfers between devices, exchanged(): return lax.all_to_all(pieces, axis, 0, 0, tiled=True)  43.7 us
    all_to_all x2, starting transfers between devices, exchanged(): return lax.all_to_all(pieces, axis, 0, 0, tiled=True)  29.5 us
    ppermute x3, waiting for transfers between devices, turned(): lax.ppermute(block, axis, [(i, (i + step) % length) for i in range(length)])  25.6 us
    all_to_all x1, blocking collectives, exchanged(): return lax.all_to_all(pieces, axis, 0, 0, tiled=True)  8.46 us
    ppermute x3, starting transfers between devices, turned(): lax.ppermute(block, axis, [(i, (i + step) % length) for i in range(length)])  8.42 us
    pallas_call x1, Pallas kernels, near_rows(): pl.pallas_call(lambda *refs: near_kernel(width, total, skip, *refs), out_...  5.28 us
    gather x3, local copies, waits for them, and re-layouts, local(): near_slots = owner_map[nearby]  3.65 us
    pallas_call x1, Pallas kernels, far_rows(): pl.pallas_call(lambda *refs: far_kernel(width, total, *refs), out_shape=(...  3.33 us
  transfers between devices with their start and end apart: 5, of which 3 were waited for; matrix products, arithmetic and copies ran while one was open for 5% of the time, Pallas kernels for 6%

profile of v1, /device:TPU:1, one launch (start us, length us, event | category | flops | bytes accessed | tf_op | source)
XLA Modules:
  0.0 147.9 jit_solution(16320861958153407672)
XLA Ops:
  0.7 1.0 select_reduce_fusion
  2.5 0.8 select_reduce_fusion.4
  5.5 0.8 gather_fusion.3
  6.3 0.8 gather_fusion.2
  7.3 1.5 %broadcast_in_dim.170 = f32[128,1,1664]{2,1,0:T(1,128)} reshape(f32[128,1664]{1,0:T(8,128)S(1)} %pad_maximum_fusion) | data formatting | bytes 1703936 | tf_op jit(solution)/shard_map/broadcast_in_dim | solution.py:205
  8.8 20.4 %all-to-all-start = ((f32[128,1,1664]{2,1,0:T(1,128)}), f32[128,1,1664]{2,1,0:T(1,128)S(1)}, u32[]{:S(2)}, u32[]{:S(2)}) async-start(f32[128,1,1664]{2,1,0:T(1,128)} %broadcast_in_dim.170), calls=%async_computation | async-start | bytes 1703936 | tf_op jit(solution)/shard_map/all_to_all | solution.py:16
  29.2 0.8 gather_fusion.1
  30.1 43.7 %all-to-all-done = f32[128,1,1664]{2,1,0:T(1,128)S(1)} async-done(((f32[128,1,1664]{2,1,0:T(1,128)}), f32[128,1,1664]{2,1,0:T(1,128)S(1)}, u32[]{:S(2)}, u32[]{:S(2)}) %all-to-all-start) | async-done | bytes 852000 | tf_op jit(solution)/shard_map/all_to_all | solution.py:16
  73.9 0.8 copy-done.2
  75.2 8.5 %all_to_all.15.refs_1_ = f32[4,32,128]{2,1,0:T(8,128)S(1)} all-to-all(f32[4,32,128]{2,1,0:T(8,128)S(1)} %select.42), channel_id=1, replica_groups=mesh['z_hi'=4,'z_lo'=4,'x'=4,'core'=2,'help'=4] {'help'}, dimensions={0} | all-to-all | bytes 131072 | tf_op jit(solution)/shard_map/all_to_all | solution.py:16
  83.7 0.8 broadcast_in_dim.171
  84.5 9.2 %all-to-all-start.2 = ((f32[32,24,128]{2,1,0:T(8,128)}), f32[32,24,128]{2,1,0:T(8,128)}, u32[]{:S(2)}, u32[]{:S(2)}) async-start(f32[32,24,128]{2,1,0:T(8,128)} %broadcast_in_dim.171), calls=%async_computation.2 | async-start | bytes 786432 | tf_op jit(solution)/shard_map/all_to_all | solution.py:16
  93.6 1.2 slice.32.refs_2_
  94.8 2.6 %collective-permute-start.2 = (f32[128,1,1536]{2,1,0:T(1,128)S(1)}, f32[128,1,1536]{2,1,0:T(1,128)S(1)}, u32[]{:S(2)}, u32[]{:S(2)}) collective-permute-start(f32[128,1,1536]{2,1,0:T(1,128)S(1)} %slice.32.refs_2_), channel_id=1, source_target_pairs={{0,2},{1,3},{2,0},{3,1},{4,6},{5,7},{6,4},{7,5},{8,10},{9,11},{10,... | collective-permute-start | bytes 2359304 | tf_op jit(solution)/shard_map/ppermute | solution.py:26
  97.5 3.9 %collective-permute-start.1 = (f32[128,1,1536]{2,1,0:T(1,128)S(1)}, f32[128,1,1536]{2,1,0:T(1,128)}, u32[]{:S(2)}, u32[]{:S(2)}) collective-permute-start(f32[128,1,1536]{2,1,0:T(1,128)S(1)} %slice.32.refs_2_), channel_id=1, source_target_pairs={{0,3},{1,0},{2,1},{3,2},{4,7},{5,4},{6,5},{7,6},{8,11},{9,8},{10,9... | collective-permute-start | bytes 2359304 | tf_op jit(solution)/shard_map/ppermute | solution.py:26
  101.4 1.9 %collective-permute-start = (f32[128,1,1536]{2,1,0:T(1,128)S(1)}, f32[128,1,1536]{2,1,0:T(1,128)}, u32[]{:S(2)}, u32[]{:S(2)}) collective-permute-start(f32[128,1,1536]{2,1,0:T(1,128)S(1)} %slice.32.refs_2_), channel_id=1, source_target_pairs={{0,1},{1,2},{2,3},{3,0},{4,5},{5,6},{6,7},{7,4},{8,9},{9,10},{10,1... | collective-permute-start | bytes 2359304 | tf_op jit(solution)/shard_map/ppermute | solution.py:26
  103.5 3.5 %gather_fusion = s32[512]{0:T(512)S(1)} fusion(s32[256]{0:T(256)S(1)} %copy-done.1, s32[1024]{0:T(1024)S(1)} %pad_clamp_fusion.3), kind=kCustom, calls=%fused_computation | custom fusion | bytes 6144 | tf_op jit(solution)/shard_map/gather | solution.py:219
  107.6 1.4 fusion.8
  109.0 23.5 %collective-permute-done.1.refs_4_ = f32[128,1,1536]{2,1,0:T(1,128)} collective-permute-done((f32[128,1,1536]{2,1,0:T(1,128)S(1)}, f32[128,1,1536]{2,1,0:T(1,128)}, u32[]{:S(2)}, u32[]{:S(2)}) %collective-permute-start.1) | collective-permute-done | bytes 786464 | tf_op jit(solution)/shard_map/ppermute | solution.py:26
  132.5 2.1 %collective-permute-done.refs_3_ = f32[128,1,1536]{2,1,0:T(1,128)} collective-permute-done((f32[128,1,1536]{2,1,0:T(1,128)S(1)}, f32[128,1,1536]{2,1,0:T(1,128)}, u32[]{:S(2)}, u32[]{:S(2)}) %collective-permute-start) | collective-permute-done | bytes 786464 | tf_op jit(solution)/shard_map/ppermute | solution.py:26
  134.7 5.3 %near.1 = (f32[1032,768]{1,0:T(8,128)S(1)}, s32[8,128]{1,0:T(8,128)S(1)}) custom-call(s32[1]{0:T(128)} %bitcast.15.refs_0_, f32[4,32,128]{2,1,0:T(8,128)S(1)} %all_to_all.15.refs_1_, f32[128,1,1536]{2,1,0:T(1,128)S(1)} %slice.32.refs_2_, f32[128,1,1536]{2,1,0:T(1,128)} %collective-permute-done.refs_3_, f32[128,1,1536]{2,1,0:T(1,128)} %collective-permute-done.1.refs_4_), custom_call_target="tpu_custom_call" | custom-call | tf_op jit(solution)/shard_map/near/pallas_call | solution.py:105
  140.0 3.3 %far.1 = (f32[1032,768]{1,0:T(8,128)S(1)}, f32[1024,768]{1,0:T(8,128)}) custom-call(s32[1]{0:T(128)} %bitcast.15.refs_0_, s32[8,128]{1,0:T(8,128)S(1)} %get-tuple-element.5.refs_1_, f32[128,1,1536]{2,1,0:T(1,128)S(1)} %collective-permute-done.2.refs_2_, f32[1032,768]{1,0:T(8,128)S(1)} %get-tuple-element.6.refs_3_), custom_call_target="tpu_custom_call", output_to_operand_aliasing={{0}: (3, {})} | custom-call | tf_op jit(solution)/shard_map/far/pallas_call | solution.py:133
  143.3 1.1 multiply_reduce_fusion
  144.4 2.8 %fusion.3 = f32[2,256]{1,0:T(2,128)S(1)} fusion(f32[768,128,1]{1,0,2:T(8,128)} %bitcast.13, f32[2,256,768]{2,1,0:T(8,128)S(1)} %copy-done, f32[128]{0:T(128)S(1)} %multiply_reduce_fusion, pred[2,128]{1,0:T(4,128)(4,1)S(1)} %tile.19), kind=kOutput, calls=%fused_computation.8 | convolution fusion | flops 604241408 | bytes 1968896 | tf_op jit(solution)/shard_map/krd,dc->krc/dot_general | solution.py:224
  (62 shorter events, 5.1 us)
Async XLA Ops:
  0.6 3.7 %copy-start = (f32[2,256,768]{2,1,0:T(8,128)S(1)}, f32[2,256,768]{2,1,0:T(8,128)}, u32[]{:S(2)}) copy-start(f32[2,256,768]{2,1,0:T(8,128)} %param.9) | copy-start | bytes 4718596
  7.3 21.9 %copy-start.6 = (s32[64]{0:T(128)S(1)}, s32[64]{0:T(128)}, u32[]{:S(2)}) copy-start(s32[64]{0:T(128)} %param.13) | copy-start | bytes 772
  7.3 21.9 %copy-start.1 = (s32[256]{0:T(256)S(1)}, s32[256]{0:T(256)}, u32[]{:S(2)}) copy-start(s32[256]{0:T(256)} %param.15) | copy-start | bytes 3076
  8.8 65.1 %all-to-all-start = ((f32[128,1,1664]{2,1,0:T(1,128)}), f32[128,1,1664]{2,1,0:T(1,128)S(1)}, u32[]{:S(2)}, u32[]{:S(2)}) async-start(f32[128,1,1664]{2,1,0:T(1,128)} %broadcast_in_dim.170), calls=%async_computation | async-start | bytes 1703936 | tf_op jit(solution)/shard_map/all_to_all | solution.py:16
  73.9 0.9 copy-start.2
  74.8 28.5 %copy-start.4 = (s32[64,8]{0,1:T(8,128)S(1)}, s32[64,8]{0,1:T(8,128)}, u32[]{:S(2)}) copy-start(s32[64,8]{0,1:T(8,128)} %param.14) | copy-start | bytes 6148
  84.5 58.9 %all-to-all-start.2 = ((f32[32,24,128]{2,1,0:T(8,128)}), f32[32,24,128]{2,1,0:T(8,128)}, u32[]{:S(2)}, u32[]{:S(2)}) async-start(f32[32,24,128]{2,1,0:T(8,128)} %broadcast_in_dim.171), calls=%async_computation.2 | async-start | bytes 786432 | tf_op jit(solution)/shard_map/all_to_all | solution.py:16
  94.8 45.1 %collective-permute-start.2 = (f32[128,1,1536]{2,1,0:T(1,128)S(1)}, f32[128,1,1536]{2,1,0:T(1,128)S(1)}, u32[]{:S(2)}, u32[]{:S(2)}) collective-permute-start(f32[128,1,1536]{2,1,0:T(1,128)S(1)} %slice.32.refs_2_), channel_id=1, source_target_pairs={{0,2},{1,3},{2,0},{3,1},{4,6},{5,7},{6,4},{7,5},{8,10},{9,11},{10,... | collective-permute-start | bytes 2359304 | tf_op jit(solution)/shard_map/ppermute | solution.py:26
  97.5 35.1 %collective-permute-start.1 = (f32[128,1,1536]{2,1,0:T(1,128)S(1)}, f32[128,1,1536]{2,1,0:T(1,128)}, u32[]{:S(2)}, u32[]{:S(2)}) collective-permute-start(f32[128,1,1536]{2,1,0:T(1,128)S(1)} %slice.32.refs_2_), channel_id=1, source_target_pairs={{0,3},{1,0},{2,1},{3,2},{4,7},{5,4},{6,5},{7,6},{8,11},{9,8},{10,9... | collective-permute-start | bytes 2359304 | tf_op jit(solution)/shard_map/ppermute | solution.py:26
  101.4 33.3 %collective-permute-start = (f32[128,1,1536]{2,1,0:T(1,128)S(1)}, f32[128,1,1536]{2,1,0:T(1,128)}, u32[]{:S(2)}, u32[]{:S(2)}) collective-permute-start(f32[128,1,1536]{2,1,0:T(1,128)S(1)} %slice.32.refs_2_), channel_id=1, source_target_pairs={{0,1},{1,2},{2,3},{3,0},{4,5},{5,6},{6,7},{7,4},{8,9},{9,10},{10,1... | collective-permute-start | bytes 2359304 | tf_op jit(solution)/shard_map/ppermute | solution.py:26
  103.5 4.0 %copy-start.3 = (f32[2,768]{1,0:T(2,128)S(1)}, f32[2,768]{1,0:T(2,128)}, u32[]{:S(2)}) copy-start(f32[2,768]{1,0:T(2,128)} %param.12) | copy-start | bytes 18436
  143.3 4.0 %copy-start.5 = (s32[2]{0:T(128)S(1)}, s32[2]{0:T(128)}, u32[]{:S(2)}) copy-start(s32[2]{0:T(128)} %param.11) | copy-start | bytes 28

commit v2 on v0

--- a/solution.py
+++ b/solution.py
@@ -55,6 +55,7 @@
         out_shape=jax.ShapeDtypeStruct((helpers, LANES // 4, LANES), jnp.float32),
         in_specs=[vmem, vmem],
         out_specs=vmem,
+        compiler_params=pltpu.CompilerParams(vmem_limit_bytes=4 * 2**20),
         name="select",
     )(key, tail)
 
@@ -69,8 +70,9 @@
     lax.fori_loop(0, ref.shape[0], body, 0, unroll=4)
 
 
-def near_kernel(width, total, skip, me, codes, own, below, above, image, place, spot, scalars, sem):
-    lines = own.shape[0]
+def near_kernel(width, total, skip, me, codes, *refs):
+    *parts, image, place, spot, scalars, sem = refs
+    lines = codes.shape[2]
     code = jnp.concatenate([codes[y, skip : skip + 2, :] for y in range(4)], axis=0)
     before = (
         lax.broadcasted_iota(jnp.int32, (lines, lines), 0)
@@ -95,8 +97,9 @@
     place[...] = spot[...]
     image[...] = jnp.zeros_like(image)
     copy.wait()
-    for ref, turn in ((own, 0), (below, 3), (above, 1)):
-        put_rows(image, scalars, ref, lax.rem(me[0] + turn, 4) * 2, 0, width)
+    for at, ref in enumerate(parts):
+        base = lax.rem(me[0] + (0, 3, 1)[at // 2], 4) * 2
+        put_rows(image, scalars, ref, base, at % 2 * (lines // 2), width)
 
 
 def near_rows(me, codes, parts, width, total, skip):
@@ -114,6 +117,7 @@
             pltpu.SMEM((8, LANES), jnp.int32),
             pltpu.SemaphoreType.DMA,
         ],
+        compiler_params=pltpu.CompilerParams(vmem_limit_bytes=16 * 2**20),
         name="near",
     )(me, codes, *parts)
 
@@ -140,6 +144,7 @@
         out_specs=(vmem, pl.BlockSpec(memory_space=pl.ANY)),
         scratch_shapes=[pltpu.SemaphoreType.DMA],
         input_output_aliases={2 + len(parts): 0},
+        compiler_params=pltpu.CompilerParams(vmem_limit_bytes=16 * 2**20),
         name="far",
     )(me, place, *parts, image)[1]
 
@@ -214,27 +219,29 @@
     means = sums[:cols] / sums[cols:]
     cents = copies(means, NEAR).reshape(width, 2 * splits)
 
-    sq_cent = jnp.sum(cents * cents, axis=0)
     near_slots = owner_map[nearby]
     hit = jnp.any(near_slots[None, :, :] == local_slots[:, None, None], axis=2)
-    paired = jnp.tile(hit, (1, 2))
-    cross = jnp.einsum("krd,dc->krc", vectors, cents, precision=HIGH)
-    far = jnp.min(jnp.where(paired[:, None, :], sq_cent[None, None, :] - 2.0 * cross, 1e30), axis=2)
     own_cross = jnp.einsum("krd,kd->kr", vectors, centroids, precision=HIGH)
     own_dist = jnp.sum(centroids * centroids, axis=1)[:, None] - 2.0 * own_cross
+    paired = jnp.tile(hit, (1, 2))
+    sq_cent = jnp.sum(cents * cents, axis=0)
+    cross = jnp.einsum("krd,dc->krc", vectors, cents, precision=lax.Precision.HIGH)
+    far = jnp.min(jnp.where(paired[:, None, :], sq_cent[None, None, :] - 2.0 * cross, 1e30), axis=2)
     touched = valid & jnp.any(hit, axis=1)[:, None]
     gains = jnp.where(touched, (own_dist - far) / width, 0.0)
 
     cut = lists_count // 2
-    own = got[:, :, : depth * width]
-    below = turned(own, "help", 1)
-    above = turned(own, "help", -1)
-    far_low = turned(below[:cut], "help", 1)
-    far_high = turned(above[cut:], "help", -1)
+    low, high = got[:cut, :, : depth * width], got[cut:, :, : depth * width]
+    below_low = turned(low, "help", 1)
+    above_high = turned(high, "help", -1)
+    below_high = turned(high, "help", 1)
+    above_low = turned(low, "help", -1)
+    far_low = turned(below_low, "help", 1)
+    far_high = turned(above_high, "help", -1)
     arrive_cap = lists_count * help_count * ((depth + list_dev - 1) // list_dev)
     total = list_dev * arrive_cap
     me = my_help[None]
-    image, place = near_rows(me, over_help, [own, below, above], width, total, cols + 1)
+    image, place = near_rows(me, over_help, [low, high, below_low, below_high, above_low, above_high], width, total, cols + 1)
     out = far_rows(me, place, [far_low, far_high], image, width, total)
     return gains, out.reshape(list_dev, arrive_cap, width)
 

time: 147 us -> 134 us (0.912)
  waiting for transfers between devices: 57.5 us -> 48.1 us
  starting transfers between devices: 40.6 us -> 46.6 us
  local copies, waits for them, and re-layouts: 13.1 us -> 9.35 us
  Pallas kernels: 11.9 us -> 9.1 us
  matrix products: 6.8 us -> 4.02 us
    ppermute x4 -> x6, waiting for transfers between devices: 14.3 us -> 4.39 us  [turned(): lax.ppermute(block, axis, [(i, (i + step) % length) for i in range(length)])]
    ppermute x4 -> x6, starting transfers between devices: 11.1 us -> 17.1 us  [turned(): lax.ppermute(block, axis, [(i, (i + step) % length) for i in range(length)])]
    slice x3 -> x1, local copies, waits for them, and re-layouts: 2.69 us -> 0.08 us  [local(): low, high = (got[:cut, :, :depth * width], got[cut:, :, :depth * width])]
    pallas_call x1, Pallas kernels: 1.9 us -> 0.4 us  [selected(): pl.pallas_call(lambda *refs: select_kernel(cols, depth, *refs), out_shape...]
  transfers between devices with their start and end apart: 6 -> 8, of which waited for: 3 -> 4; matrix products, arithmetic and copies ran while one was open for 7% -> 5% of each run, Pallas kernels for 7% -> 7%
where the time goes in v2:
time: 134 us; the launch traced here: 133 us
  waiting for transfers between devices  48.1 us (36%)
  starting transfers between devices  46.6 us (35%)
  local copies, waits for them, and re-layouts  9.35 us (7%)
  Pallas kernels  9.1 us (7%)
  blocking collectives  8.46 us (6%)
  other arithmetic  5.9 us (4%)
  matrix products  4.02 us (3%)
    all_to_all x2, waiting for transfers between devices, exchanged(): return lax.all_to_all(pieces, axis, 0, 0, tiled=True)  43.7 us
    all_to_all x2, starting transfers between devices, exchanged(): return lax.all_to_all(pieces, axis, 0, 0, tiled=True)  29.5 us
    ppermute x6, starting transfers between devices, turned(): lax.ppermute(block, axis, [(i, (i + step) % length) for i in range(length)])  17.1 us
    all_to_all x1, blocking collectives, exchanged(): return lax.all_to_all(pieces, axis, 0, 0, tiled=True)  8.46 us
    pallas_call x1, Pallas kernels, near_rows(): pl.pallas_call(lambda *refs: near_kernel(width, total, skip, *refs), out_...  5.4 us
    ppermute x6, waiting for transfers between devices, turned(): lax.ppermute(block, axis, [(i, (i + step) % length) for i in range(length)])  4.39 us
    gather x3, local copies, waits for them, and re-layouts, local(): near_slots = owner_map[nearby]  3.65 us
    pallas_call x1, Pallas kernels, far_rows(): pl.pallas_call(lambda *refs: far_kernel(width, total, *refs), out_shape=(...  3.3 us
  transfers between devices with their start and end apart: 8, of which 4 were waited for; matrix products, arithmetic and copies ran while one was open for 5% of the time, Pallas kernels for 7%

profile of v2, /device:TPU:1, one launch (start us, length us, event | category | flops | bytes accessed | tf_op | source)
XLA Modules:
  0.0 132.6 jit_solution(2333662297788473806)
XLA Ops:
  0.7 1.0 select_reduce_fusion
  2.5 0.8 select_reduce_fusion.4
  5.5 0.8 gather_fusion.3
  6.3 0.8 gather_fusion.2
  7.3 1.5 %broadcast_in_dim.170 = f32[128,1,1664]{2,1,0:T(1,128)} reshape(f32[128,1664]{1,0:T(8,128)S(1)} %pad_maximum_fusion) | data formatting | bytes 1703936 | tf_op jit(solution)/shard_map/broadcast_in_dim | solution.py:209
  8.8 20.4 %all-to-all-start = ((f32[128,1,1664]{2,1,0:T(1,128)}), f32[128,1,1664]{2,1,0:T(1,128)S(1)}, u32[]{:S(2)}, u32[]{:S(2)}) async-start(f32[128,1,1664]{2,1,0:T(1,128)} %broadcast_in_dim.170), calls=%async_computation | async-start | bytes 1703936 | tf_op jit(solution)/shard_map/all_to_all | solution.py:16
  30.1 43.7 %all-to-all-done = f32[128,1,1664]{2,1,0:T(1,128)S(1)} async-done(((f32[128,1,1664]{2,1,0:T(1,128)}), f32[128,1,1664]{2,1,0:T(1,128)S(1)}, u32[]{:S(2)}, u32[]{:S(2)}) %all-to-all-start) | async-done | bytes 852000 | tf_op jit(solution)/shard_map/all_to_all | solution.py:16
  74.3 8.5 %all_to_all.15.refs_1_ = f32[4,32,128]{2,1,0:T(8,128)S(1)} all-to-all(f32[4,32,128]{2,1,0:T(8,128)S(1)} %select.42), channel_id=1, replica_groups=mesh['z_hi'=4,'z_lo'=4,'x'=4,'core'=2,'help'=4] {'help'}, dimensions={0} | all-to-all | bytes 131072 | tf_op jit(solution)/shard_map/all_to_all | solution.py:16
  83.6 9.2 %all-to-all-start.2 = ((f32[32,24,128]{2,1,0:T(8,128)}), f32[32,24,128]{2,1,0:T(8,128)}, u32[]{:S(2)}, u32[]{:S(2)}) async-start(f32[32,24,128]{2,1,0:T(8,128)} %broadcast_in_dim.171), calls=%async_computation.2 | async-start | bytes 786432 | tf_op jit(solution)/shard_map/all_to_all | solution.py:16
  92.9 2.8 %collective-permute-start.3 = (f32[64,1,1536]{2,1,0:T(1,128)S(1)}, f32[64,1,1536]{2,1,0:T(1,128)}, u32[]{:S(2)}, u32[]{:S(2)}) collective-permute-start(f32[64,1,1536]{2,1,0:T(1,128)S(1)} %get-tuple-element.16.refs_3_), channel_id=1, source_target_pairs={{0,3},{1,0},{2,1},{3,2},{4,7},{5,4},{6,5},{7,6},{8,11},{9,8},{10,9... | collective-permute-start | bytes 1179656 | tf_op jit(solution)/shard_map/ppermute | solution.py:26
  95.7 2.5 %collective-permute-start = (f32[64,1,1536]{2,1,0:T(1,128)S(1)}, f32[64,1,1536]{2,1,0:T(1,128)}, u32[]{:S(2)}, u32[]{:S(2)}) collective-permute-start(f32[64,1,1536]{2,1,0:T(1,128)S(1)} %get-tuple-element.17.refs_2_), channel_id=1, source_target_pairs={{0,1},{1,2},{2,3},{3,0},{4,5},{5,6},{6,7},{7,4},{8,9},{9,10},{10,1... | collective-permute-start | bytes 1179656 | tf_op jit(solution)/shard_map/ppermute | solution.py:26
  98.4 3.5 %gather_fusion = s32[512]{0:T(512)S(1)} fusion(s32[256]{0:T(256)S(1)} %copy-done.1, s32[1024]{0:T(1024)S(1)} %pad_clamp_fusion.3), kind=kCustom, calls=%fused_computation | custom fusion | bytes 6144 | tf_op jit(solution)/shard_map/gather | solution.py:222
  102.0 2.2 %collective-permute-start.1 = (f32[64,1,1536]{2,1,0:T(1,128)S(1)}, f32[64,1,1536]{2,1,0:T(1,128)}, u32[]{:S(2)}, u32[]{:S(2)}) collective-permute-start(f32[64,1,1536]{2,1,0:T(1,128)S(1)} %get-tuple-element.16.refs_3_), channel_id=1, source_target_pairs={{0,1},{1,2},{2,3},{3,0},{4,5},{5,6},{6,7},{7,4},{8,9},{9,10},{10,1... | collective-permute-start | bytes 1179656 | tf_op jit(solution)/shard_map/ppermute | solution.py:26
  104.3 4.3 %collective-permute-start.2 = (f32[64,1,1536]{2,1,0:T(1,128)S(1)}, f32[64,1,1536]{2,1,0:T(1,128)}, u32[]{:S(2)}, u32[]{:S(2)}) collective-permute-start(f32[64,1,1536]{2,1,0:T(1,128)S(1)} %get-tuple-element.17.refs_2_), channel_id=1, source_target_pairs={{0,3},{1,0},{2,1},{3,2},{4,7},{5,4},{6,5},{7,6},{8,11},{9,8},{10,9... | collective-permute-start | bytes 1179656 | tf_op jit(solution)/shard_map/ppermute | solution.py:26
  108.6 2.8 %collective-permute-start.5 = (f32[64,1,1536]{2,1,0:T(1,128)}, f32[64,1,1536]{2,1,0:T(1,128)S(1)}, u32[]{:S(2)}, u32[]{:S(2)}) collective-permute-start(f32[64,1,1536]{2,1,0:T(1,128)} %collective-permute-done.3.refs_7_), channel_id=1, source_target_pairs={{0,3},{1,0},{2,1},{3,2},{4,7},{5,4},{6,5},{7,6},{8,11},{9,8},{10,9... | collective-permute-start | bytes 1179656 | tf_op jit(solution)/shard_map/ppermute | solution.py:26
  111.4 2.5 %collective-permute-start.4 = (f32[64,1,1536]{2,1,0:T(1,128)}, f32[64,1,1536]{2,1,0:T(1,128)S(1)}, u32[]{:S(2)}, u32[]{:S(2)}) collective-permute-start(f32[64,1,1536]{2,1,0:T(1,128)} %collective-permute-done.refs_4_), channel_id=1, source_target_pairs={{0,1},{1,2},{2,3},{3,0},{4,5},{5,6},{6,7},{7,4},{8,9},{9,10},{10,1... | collective-permute-start | bytes 1179656 | tf_op jit(solution)/shard_map/ppermute | solution.py:26
  114.3 1.4 %fusion.8 = f32[2,1,256]{2,1,0:T(1,128)S(1)} fusion(f32[2,256,768]{2,1,0:T(8,128)S(1)} %copy-done, f32[2,768,1]{1,0,2:T(2,128)S(1)} %bitcast.50), kind=kOutput, calls=%fused_computation.32 | convolution fusion | flops 4718592 | bytes 1581056 | tf_op jit(solution)/shard_map/krd,kd->kr/dot_general | solution.py:224
  115.7 1.7 %collective-permute-done.1.refs_5_ = f32[64,1,1536]{2,1,0:T(1,128)} collective-permute-done((f32[64,1,1536]{2,1,0:T(1,128)S(1)}, f32[64,1,1536]{2,1,0:T(1,128)}, u32[]{:S(2)}, u32[]{:S(2)}) %collective-permute-start.1) | collective-permute-done | bytes 393248 | tf_op jit(solution)/shard_map/ppermute | solution.py:26
  117.4 5.4 %near.1 = (f32[1032,768]{1,0:T(8,128)S(1)}, s32[8,128]{1,0:T(8,128)S(1)}) custom-call(s32[1]{0:T(128)} %bitcast.15.refs_0_, f32[4,32,128]{2,1,0:T(8,128)S(1)} %all_to_all.15.refs_1_, f32[64,1,1536]{2,1,0:T(1,128)S(1)} %get-tuple-element.17.refs_2_, f32[64,1,1536]{2,1,0:T(1,128)S(1)} %get-tuple-element.16.refs_3_, ...), custom_call_target="tpu_custom_call" | custom-call | tf_op jit(solution)/shard_map/near/pallas_call | solution.py:107
  122.8 1.6 %collective-permute-done.5.refs_3_ = f32[64,1,1536]{2,1,0:T(1,128)S(1)} collective-permute-done((f32[64,1,1536]{2,1,0:T(1,128)}, f32[64,1,1536]{2,1,0:T(1,128)S(1)}, u32[]{:S(2)}, u32[]{:S(2)}) %collective-permute-start.5) | collective-permute-done | bytes 393248 | tf_op jit(solution)/shard_map/ppermute | solution.py:26
  124.4 1.1 collective-permute-done.4.refs_2_
  125.5 3.3 %far.1 = (f32[1032,768]{1,0:T(8,128)S(1)}, f32[1024,768]{1,0:T(8,128)}) custom-call(s32[1]{0:T(128)} %bitcast.15.refs_0_, s32[8,128]{1,0:T(8,128)S(1)} %get-tuple-element.5.refs_1_, f32[64,1,1536]{2,1,0:T(1,128)S(1)} %collective-permute-done.4.refs_2_, f32[64,1,1536]{2,1,0:T(1,128)S(1)} %collective-permute-done.5.refs_3_, ...), custom_call_target="tpu_custom_call", output_to_operand_aliasing={{0}: (4, {})} | custom-call | tf_op jit(solution)/shard_map/far/pallas_call | solution.py:137
  128.8 1.1 multiply_reduce_fusion
  130.0 2.0 %fusion.3 = f32[2,256]{1,0:T(2,128)S(1)} fusion(f32[768,128,1]{1,0,2:T(8,128)} %bitcast.13, f32[2,256,768]{2,1,0:T(8,128)S(1)} %copy-done, f32[128]{0:T(128)S(1)} %multiply_reduce_fusion, pred[2,128]{1,0:T(4,128)(4,1)S(1)} %tile.19), kind=kOutput, calls=%fused_computation.8 | convolution fusion | flops 302251520 | bytes 1968896 | tf_op jit(solution)/shard_map/krd,dc->krc/dot_general | solution.py:228
  (66 shorter events, 6.8 us)
Async XLA Ops:
  0.6 3.7 %copy-start = (f32[2,256,768]{2,1,0:T(8,128)S(1)}, f32[2,256,768]{2,1,0:T(8,128)}, u32[]{:S(2)}) copy-start(f32[2,256,768]{2,1,0:T(8,128)} %param.9) | copy-start | bytes 4718596
  7.3 21.9 %copy-start.5 = (s32[64]{0:T(128)S(1)}, s32[64]{0:T(128)}, u32[]{:S(2)}) copy-start(s32[64]{0:T(128)} %param.13) | copy-start | bytes 772
  7.3 21.9 %copy-start.1 = (s32[256]{0:T(256)S(1)}, s32[256]{0:T(256)}, u32[]{:S(2)}) copy-start(s32[256]{0:T(256)} %param.15) | copy-start | bytes 3076
  8.8 65.1 %all-to-all-start = ((f32[128,1,1664]{2,1,0:T(1,128)}), f32[128,1,1664]{2,1,0:T(1,128)S(1)}, u32[]{:S(2)}, u32[]{:S(2)}) async-start(f32[128,1,1664]{2,1,0:T(1,128)} %broadcast_in_dim.170), calls=%async_computation | async-start | bytes 1703936 | tf_op jit(solution)/shard_map/all_to_all | solution.py:16
  73.9 24.2 %copy-start.3 = (s32[64,8]{0,1:T(8,128)S(1)}, s32[64,8]{0,1:T(8,128)}, u32[]{:S(2)}) copy-start(s32[64,8]{0,1:T(8,128)} %param.14) | copy-start | bytes 6148
  83.6 45.2 %all-to-all-start.2 = ((f32[32,24,128]{2,1,0:T(8,128)}), f32[32,24,128]{2,1,0:T(8,128)}, u32[]{:S(2)}, u32[]{:S(2)}) async-start(f32[32,24,128]{2,1,0:T(8,128)} %broadcast_in_dim.171), calls=%async_computation.2 | async-start | bytes 786432 | tf_op jit(solution)/shard_map/all_to_all | solution.py:16
  92.9 15.7 %collective-permute-start.3 = (f32[64,1,1536]{2,1,0:T(1,128)S(1)}, f32[64,1,1536]{2,1,0:T(1,128)}, u32[]{:S(2)}, u32[]{:S(2)}) collective-permute-start(f32[64,1,1536]{2,1,0:T(1,128)S(1)} %get-tuple-element.16.refs_3_), channel_id=1, source_target_pairs={{0,3},{1,0},{2,1},{3,2},{4,7},{5,4},{6,5},{7,6},{8,11},{9,8},{10,9... | collective-permute-start | bytes 1179656 | tf_op jit(solution)/shard_map/ppermute | solution.py:26
  95.7 15.7 %collective-permute-start = (f32[64,1,1536]{2,1,0:T(1,128)S(1)}, f32[64,1,1536]{2,1,0:T(1,128)}, u32[]{:S(2)}, u32[]{:S(2)}) collective-permute-start(f32[64,1,1536]{2,1,0:T(1,128)S(1)} %get-tuple-element.17.refs_2_), channel_id=1, source_target_pairs={{0,1},{1,2},{2,3},{3,0},{4,5},{5,6},{6,7},{7,4},{8,9},{9,10},{10,1... | collective-permute-start | bytes 1179656 | tf_op jit(solution)/shard_map/ppermute | solution.py:26
  98.4 15.8 %copy-start.2 = (f32[2,768]{1,0:T(2,128)S(1)}, f32[2,768]{1,0:T(2,128)}, u32[]{:S(2)}) copy-start(f32[2,768]{1,0:T(2,128)} %param.12) | copy-start | bytes 18436
  102.0 15.3 %collective-permute-start.1 = (f32[64,1,1536]{2,1,0:T(1,128)S(1)}, f32[64,1,1536]{2,1,0:T(1,128)}, u32[]{:S(2)}, u32[]{:S(2)}) collective-permute-start(f32[64,1,1536]{2,1,0:T(1,128)S(1)} %get-tuple-element.16.refs_3_), channel_id=1, source_target_pairs={{0,1},{1,2},{2,3},{3,0},{4,5},{5,6},{6,7},{7,4},{8,9},{9,10},{10,1... | collective-permute-start | bytes 1179656 | tf_op jit(solution)/shard_map/ppermute | solution.py:26
  104.3 13.1 %collective-permute-start.2 = (f32[64,1,1536]{2,1,0:T(1,128)S(1)}, f32[64,1,1536]{2,1,0:T(1,128)}, u32[]{:S(2)}, u32[]{:S(2)}) collective-permute-start(f32[64,1,1536]{2,1,0:T(1,128)S(1)} %get-tuple-element.17.refs_2_), channel_id=1, source_target_pairs={{0,3},{1,0},{2,1},{3,2},{4,7},{5,4},{6,5},{7,6},{8,11},{9,8},{10,9... | collective-permute-start | bytes 1179656 | tf_op jit(solution)/shard_map/ppermute | solution.py:26
  108.6 15.8 %collective-permute-start.5 = (f32[64,1,1536]{2,1,0:T(1,128)}, f32[64,1,1536]{2,1,0:T(1,128)S(1)}, u32[]{:S(2)}, u32[]{:S(2)}) collective-permute-start(f32[64,1,1536]{2,1,0:T(1,128)} %collective-permute-done.3.refs_7_), channel_id=1, source_target_pairs={{0,3},{1,0},{2,1},{3,2},{4,7},{5,4},{6,5},{7,6},{8,11},{9,8},{10,9... | collective-permute-start | bytes 1179656 | tf_op jit(solution)/shard_map/ppermute | solution.py:26
  111.4 14.1 %collective-permute-start.4 = (f32[64,1,1536]{2,1,0:T(1,128)}, f32[64,1,1536]{2,1,0:T(1,128)S(1)}, u32[]{:S(2)}, u32[]{:S(2)}) collective-permute-start(f32[64,1,1536]{2,1,0:T(1,128)} %collective-permute-done.refs_4_), channel_id=1, source_target_pairs={{0,1},{1,2},{2,3},{3,0},{4,5},{5,6},{6,7},{7,4},{8,9},{9,10},{10,1... | collective-permute-start | bytes 1179656 | tf_op jit(solution)/shard_map/ppermute | solution.py:26
  128.8 3.1 %copy-start.4 = (s32[2]{0:T(128)S(1)}, s32[2]{0:T(128)}, u32[]{:S(2)}) copy-start(s32[2]{0:T(128)} %param.11) | copy-start | bytes 28

commit v3 on v2

--- a/solution.py
+++ b/solution.py
@@ -58,6 +58,40 @@
         compiler_params=pltpu.CompilerParams(vmem_limit_bytes=4 * 2**20),
         name="select",
     )(key, tail)
+
+
+def halved(values):
+    high = values.astype(jnp.bfloat16)
+    return high, (values - high.astype(jnp.float32)).astype(jnp.bfloat16)
+
+
+def score_kernel(vectors, cents, penalty, own, touched, out):
+    table = cents[...]
+    base = jnp.sum(table * table, axis=0, keepdims=True)
+    high, low = halved(table)
+    for k in range(vectors.shape[0]):
+        rows_high, rows_low = halved(vectors[k])
+
+        def product(left, right):
+            return jnp.dot(left, right, preferred_element_type=jnp.float32)
+
+        cross = product(rows_high, low) + product(rows_low, high) + product(rows_high, high)
+        dist = base + penalty[k : k + 1, :] - 2.0 * cross
+        least = jnp.min(dist.T, axis=0, keepdims=True)
+        gain = (own[k : k + 1, :] - least) / vectors.shape[2]
+        out[k : k + 1, :] = jnp.where(touched[k : k + 1, :] > 0.0, gain, 0.0)
+
+
+def scored(vectors, cents, penalty, own, touched):
+    vmem = pl.BlockSpec(memory_space=pltpu.VMEM)
+    return pl.pallas_call(
+        score_kernel,
+        out_shape=jax.ShapeDtypeStruct(own.shape, jnp.float32),
+        in_specs=[vmem] * 5,
+        out_specs=vmem,
+        compiler_params=pltpu.CompilerParams(vmem_limit_bytes=16 * 2**20),
+        name="score",
+    )(vectors, cents, penalty, own, touched)
 
 
 def put_rows(image, place, ref, base, start, width):
@@ -221,14 +255,11 @@
 
     near_slots = owner_map[nearby]
     hit = jnp.any(near_slots[None, :, :] == local_slots[:, None, None], axis=2)
+    penalty = jnp.tile(jnp.where(hit, 0.0, 1e30), (1, 2))
     own_cross = jnp.einsum("krd,kd->kr", vectors, centroids, precision=HIGH)
     own_dist = jnp.sum(centroids * centroids, axis=1)[:, None] - 2.0 * own_cross
-    paired = jnp.tile(hit, (1, 2))
-    sq_cent = jnp.sum(cents * cents, axis=0)
-    cross = jnp.einsum("krd,dc->krc", vectors, cents, precision=lax.Precision.HIGH)
-    far = jnp.min(jnp.where(paired[:, None, :], sq_cent[None, None, :] - 2.0 * cross, 1e30), axis=2)
-    touched = valid & jnp.any(hit, axis=1)[:, None]
-    gains = jnp.where(touched, (own_dist - far) / width, 0.0)
+    touched = (valid & jnp.any(hit, axis=1)[:, None]).astype(jnp.float32)
+    gains = scored(vectors, cents, penalty, own_dist, touched)
 
     cut = lists_count // 2
     low, high = got[:cut, :, : depth * width], got[cut:, :, : depth * width]

time: 134 us -> 138 us (1.030)
  waiting for transfers between devices: 48.1 us -> 52.5 us
  local copies, waits for them, and re-layouts: 9.35 us -> 11.4 us
  matrix products: 4.02 us -> 2.03 us
  Pallas kernels: 9.1 us -> 11 us
  other arithmetic: 5.9 us -> 4.13 us
    ppermute x6, waiting for transfers between devices: 4.39 us -> 8.75 us  [turned(): lax.ppermute(block, axis, [(i, (i + step) % length) for i in range(length)])]
    dot_general x1 -> x0, matrix products: 1.98 us -> none  [local(): jnp.einsum('krd,dc->krc', vectors, cents, precision=lax.Precision.HIGH)]
    pallas_call x0 -> x1, Pallas kernels: none -> 1.47 us  [scored(): pl.pallas_call(score_kernel, out_shape=jax.ShapeDtypeStruct(own.shape, jn...]
  transfers between devices with their start and end apart: 8 -> 8, of which waited for: 4 -> 3; matrix products, arithmetic and copies ran while one was open for 5% -> 3% of each run, Pallas kernels for 7% -> 7%
where the time goes in v3:
time: 138 us; the launch traced here: 137 us
  waiting for transfers between devices  52.5 us (38%)
  starting transfers between devices  46.6 us (34%)
  local copies, waits for them, and re-layouts  11.4 us (8%)
  Pallas kernels  11 us (8%)
  blocking collectives  8.46 us (6%)
  other arithmetic  4.13 us (3%)
  matrix products  2.03 us (1%)
    all_to_all x2, waiting for transfers between devices, exchanged(): return lax.all_to_all(pieces, axis, 0, 0, tiled=True)  43.7 us
    all_to_all x2, starting transfers between devices, exchanged(): return lax.all_to_all(pieces, axis, 0, 0, tiled=True)  29.5 us
    ppermute x6, starting transfers between devices, turned(): lax.ppermute(block, axis, [(i, (i + step) % length) for i in range(length)])  17.1 us
    ppermute x6, waiting for transfers between devices, turned(): lax.ppermute(block, axis, [(i, (i + step) % length) for i in range(length)])  8.75 us
    all_to_all x1, blocking collectives, exchanged(): return lax.all_to_all(pieces, axis, 0, 0, tiled=True)  8.46 us
    pallas_call x1, Pallas kernels, near_rows(): pl.pallas_call(lambda *refs: near_kernel(width, total, skip, *refs), out_...  5.4 us
    pallas_call x1, Pallas kernels, far_rows(): pl.pallas_call(lambda *refs: far_kernel(width, total, *refs), out_shape=(...  3.7 us
    gather x3, local copies, waits for them, and re-layouts, local(): near_slots = owner_map[nearby]  3.64 us
  transfers between devices with their start and end apart: 8, of which 3 were waited for; matrix products, arithmetic and copies ran while one was open for 3% of the time, Pallas kernels for 7%

profile of v3, /device:TPU:1, one launch (start us, length us, event | category | flops | bytes accessed | tf_op | source)
XLA Modules:
  0.0 137.1 jit_solution(13991721368029319919)
XLA Ops:
  0.7 0.9 select_reduce_fusion
  2.4 0.8 select_reduce_fusion.4
  4.2 3.5 %gather_fusion.3 = s32[512]{0:T(512)S(1)} fusion(s32[256]{0:T(256)S(1)} %copy-done.1, s32[1024]{0:T(1024)S(1)} %pad_clamp_fusion), kind=kCustom, calls=%fused_computation.3 | custom fusion | bytes 6144 | tf_op jit(solution)/shard_map/gather | solution.py:256
  9.6 0.8 gather_fusion.2
  10.4 0.8 gather_fusion.1
  11.4 1.5 %broadcast_in_dim.159 = f32[128,1,1664]{2,1,0:T(1,128)} reshape(f32[128,1664]{1,0:T(8,128)S(1)} %pad_maximum_fusion) | data formatting | bytes 1703936 | tf_op jit(solution)/shard_map/broadcast_in_dim | solution.py:243
  12.9 20.4 %all-to-all-start = ((f32[128,1,1664]{2,1,0:T(1,128)}), f32[128,1,1664]{2,1,0:T(1,128)S(1)}, u32[]{:S(2)}, u32[]{:S(2)}) async-start(f32[128,1,1664]{2,1,0:T(1,128)} %broadcast_in_dim.159), calls=%async_computation | async-start | bytes 1703936 | tf_op jit(solution)/shard_map/all_to_all | solution.py:16
  34.2 43.7 %all-to-all-done = f32[128,1,1664]{2,1,0:T(1,128)S(1)} async-done(((f32[128,1,1664]{2,1,0:T(1,128)}), f32[128,1,1664]{2,1,0:T(1,128)S(1)}, u32[]{:S(2)}, u32[]{:S(2)}) %all-to-all-start) | async-done | bytes 852000 | tf_op jit(solution)/shard_map/all_to_all | solution.py:16
  78.0 0.8 copy-done.2
  79.3 8.5 %all_to_all.15.refs_1_ = f32[4,32,128]{2,1,0:T(8,128)S(1)} all-to-all(f32[4,32,128]{2,1,0:T(8,128)S(1)} %select.42), channel_id=1, replica_groups=mesh['z_hi'=4,'z_lo'=4,'x'=4,'core'=2,'help'=4] {'help'}, dimensions={0} | all-to-all | bytes 131072 | tf_op jit(solution)/shard_map/all_to_all | solution.py:16
  88.5 9.1 %all-to-all-start.2 = ((f32[32,24,128]{2,1,0:T(8,128)}), f32[32,24,128]{2,1,0:T(8,128)S(1)}, u32[]{:S(2)}, u32[]{:S(2)}) async-start(f32[32,24,128]{2,1,0:T(8,128)} %broadcast_in_dim.160), calls=%async_computation.2 | async-start | bytes 786432 | tf_op jit(solution)/shard_map/all_to_all | solution.py:16
  97.6 1.2 fusion.15
  98.8 2.8 %collective-permute-start.3 = (f32[64,1,1536]{2,1,0:T(1,128)S(1)}, f32[64,1,1536]{2,1,0:T(1,128)}, u32[]{:S(2)}, u32[]{:S(2)}) collective-permute-start(f32[64,1,1536]{2,1,0:T(1,128)S(1)} %get-tuple-element.16.refs_3_), channel_id=1, source_target_pairs={{0,3},{1,0},{2,1},{3,2},{4,7},{5,4},{6,5},{7,6},{8,11},{9,8},{10,9... | collective-permute-start | bytes 1179656 | tf_op jit(solution)/shard_map/ppermute | solution.py:26
  101.6 2.5 %collective-permute-start = (f32[64,1,1536]{2,1,0:T(1,128)S(1)}, f32[64,1,1536]{2,1,0:T(1,128)}, u32[]{:S(2)}, u32[]{:S(2)}) collective-permute-start(f32[64,1,1536]{2,1,0:T(1,128)S(1)} %get-tuple-element.17.refs_2_), channel_id=1, source_target_pairs={{0,1},{1,2},{2,3},{3,0},{4,5},{5,6},{6,7},{7,4},{8,9},{9,10},{10,1... | collective-permute-start | bytes 1179656 | tf_op jit(solution)/shard_map/ppermute | solution.py:26
  104.2 1.4 %fusion.6 = f32[2,1,256]{2,1,0:T(1,128)S(1)} fusion(f32[2,256,768]{2,1,0:T(8,128)S(1)} %copy-done, f32[2,768,1]{1,0,2:T(2,128)S(1)} %bitcast.34), kind=kOutput, calls=%fused_computation.28 | convolution fusion | flops 4718592 | bytes 1581056 | tf_op jit(solution)/shard_map/krd,kd->kr/dot_general | solution.py:259
  105.6 2.2 %collective-permute-start.1 = (f32[64,1,1536]{2,1,0:T(1,128)S(1)}, f32[64,1,1536]{2,1,0:T(1,128)}, u32[]{:S(2)}, u32[]{:S(2)}) collective-permute-start(f32[64,1,1536]{2,1,0:T(1,128)S(1)} %get-tuple-element.16.refs_3_), channel_id=1, source_target_pairs={{0,1},{1,2},{2,3},{3,0},{4,5},{5,6},{6,7},{7,4},{8,9},{9,10},{10,1... | collective-permute-start | bytes 1179656 | tf_op jit(solution)/shard_map/ppermute | solution.py:26
  107.8 4.3 %collective-permute-start.2 = (f32[64,1,1536]{2,1,0:T(1,128)S(1)}, f32[64,1,1536]{2,1,0:T(1,128)}, u32[]{:S(2)}, u32[]{:S(2)}) collective-permute-start(f32[64,1,1536]{2,1,0:T(1,128)S(1)} %get-tuple-element.17.refs_2_), channel_id=1, source_target_pairs={{0,3},{1,0},{2,1},{3,2},{4,7},{5,4},{6,5},{7,6},{8,11},{9,8},{10,9... | collective-permute-start | bytes 1179656 | tf_op jit(solution)/shard_map/ppermute | solution.py:26
  112.1 3.2 %collective-permute-start.5 = (f32[64,1,1536]{2,1,0:T(1,128)}, f32[64,1,1536]{2,1,0:T(1,128)S(1)}, u32[]{:S(2)}, u32[]{:S(2)}) collective-permute-start(f32[64,1,1536]{2,1,0:T(1,128)} %collective-permute-done.3.refs_7_), channel_id=1, source_target_pairs={{0,3},{1,0},{2,1},{3,2},{4,7},{5,4},{6,5},{7,6},{8,11},{9,8},{10,9... | collective-permute-start | bytes 1179656 | tf_op jit(solution)/shard_map/ppermute | solution.py:26
  115.3 2.1 %collective-permute-start.4 = (f32[64,1,1536]{2,1,0:T(1,128)}, f32[64,1,1536]{2,1,0:T(1,128)}, u32[]{:S(2)}, u32[]{:S(2)}) collective-permute-start(f32[64,1,1536]{2,1,0:T(1,128)} %collective-permute-done.refs_4_), channel_id=1, source_target_pairs={{0,1},{1,2},{2,3},{3,0},{4,5},{5,6},{6,7},{7,4},{8,9},{9,10},{10,1... | collective-permute-start | bytes 1179656 | tf_op jit(solution)/shard_map/ppermute | solution.py:26
  117.7 5.7 %collective-permute-done.1.refs_5_ = f32[64,1,1536]{2,1,0:T(1,128)} collective-permute-done((f32[64,1,1536]{2,1,0:T(1,128)S(1)}, f32[64,1,1536]{2,1,0:T(1,128)}, u32[]{:S(2)}, u32[]{:S(2)}) %collective-permute-start.1) | collective-permute-done | bytes 393248 | tf_op jit(solution)/shard_map/ppermute | solution.py:26
  123.4 5.4 %near.1 = (f32[1032,768]{1,0:T(8,128)S(1)}, s32[8,128]{1,0:T(8,128)S(1)}) custom-call(s32[1]{0:T(128)} %bitcast.13.refs_0_, f32[4,32,128]{2,1,0:T(8,128)S(1)} %all_to_all.15.refs_1_, f32[64,1,1536]{2,1,0:T(1,128)S(1)} %get-tuple-element.17.refs_2_, f32[64,1,1536]{2,1,0:T(1,128)S(1)} %get-tuple-element.16.refs_3_, ...), custom_call_target="tpu_custom_call" | custom-call | tf_op jit(solution)/shard_map/near/pallas_call | solution.py:141
  128.9 3.0 %collective-permute-done.4.refs_2_ = f32[64,1,1536]{2,1,0:T(1,128)} collective-permute-done((f32[64,1,1536]{2,1,0:T(1,128)}, f32[64,1,1536]{2,1,0:T(1,128)}, u32[]{:S(2)}, u32[]{:S(2)}) %collective-permute-start.4) | collective-permute-done | bytes 393248 | tf_op jit(solution)/shard_map/ppermute | solution.py:26
  131.9 3.7 %far.1 = (f32[1032,768]{1,0:T(8,128)S(1)}, f32[1024,768]{1,0:T(8,128)}) custom-call(s32[1]{0:T(128)} %bitcast.13.refs_0_, s32[8,128]{1,0:T(8,128)S(1)} %get-tuple-element.5.refs_1_, f32[64,1,1536]{2,1,0:T(1,128)} %collective-permute-done.4.refs_2_, f32[64,1,1536]{2,1,0:T(1,128)S(1)} %collective-permute-done.5.refs_3_, ...), custom_call_target="tpu_custom_call", output_to_operand_aliasing={{0}: (4, {})} | custom-call | tf_op jit(solution)/shard_map/far/pallas_call | solution.py:171
  135.6 1.5 %score.1 = f32[2,256]{1,0:T(2,128)} custom-call(f32[2,256,768]{2,1,0:T(8,128)S(1)} %copy-done, f32[768,128]{1,0:T(8,128)S(1)} %bitcast.32, f32[2,128]{1,0:T(2,128)S(1)} %tile.23.penalty, f32[2,256]{1,0:T(2,128)S(1)} %fusion.11.own, f32[2,256]{1,0:T(2,128)S(1)} %get-tuple-element.20.touched), custom_call_target="tpu_custom_call" | custom-call | tf_op jit(solution)/shard_map/score/pallas_call | solution.py:87
  (67 shorter events, 6.2 us)
Async XLA Ops:
  0.6 3.6 %copy-start.1 = (s32[256]{0:T(256)S(1)}, s32[256]{0:T(256)}, u32[]{:S(2)}) copy-start(s32[256]{0:T(256)} %param.15) | copy-start | bytes 3076
  4.2 3.9 %copy-start.4 = (s32[2,256]{1,0:T(2,128)S(1)}, s32[2,256]{1,0:T(2,128)}, u32[]{:S(2)}) copy-start(s32[2,256]{1,0:T(2,128)} %param.10) | copy-start | bytes 6148
  4.2 3.9 %copy-start.5 = (s32[2]{0:T(128)S(1)}, s32[2]{0:T(128)}, u32[]{:S(2)}) copy-start(s32[2]{0:T(128)} %param.11) | copy-start | bytes 28
  4.2 4.2 %copy-start = (f32[2,256,768]{2,1,0:T(8,128)S(1)}, f32[2,256,768]{2,1,0:T(8,128)}, u32[]{:S(2)}) copy-start(f32[2,256,768]{2,1,0:T(8,128)} %vectors.1) | copy-start | bytes 4718596
  11.4 21.9 %copy-start.6 = (s32[64]{0:T(128)S(1)}, s32[64]{0:T(128)}, u32[]{:S(2)}) copy-start(s32[64]{0:T(128)} %param.13) | copy-start | bytes 772
  12.9 65.1 %all-to-all-start = ((f32[128,1,1664]{2,1,0:T(1,128)}), f32[128,1,1664]{2,1,0:T(1,128)S(1)}, u32[]{:S(2)}, u32[]{:S(2)}) async-start(f32[128,1,1664]{2,1,0:T(1,128)} %broadcast_in_dim.159), calls=%async_computation | async-start | bytes 1703936 | tf_op jit(solution)/shard_map/all_to_all | solution.py:16
  78.0 0.9 copy-start.2
  78.9 25.3 %copy-start.3 = (f32[2,768]{1,0:T(2,128)S(1)}, f32[2,768]{1,0:T(2,128)}, u32[]{:S(2)}) copy-start(f32[2,768]{1,0:T(2,128)} %param.12) | copy-start | bytes 18436
  88.5 47.1 %all-to-all-start.2 = ((f32[32,24,128]{2,1,0:T(8,128)}), f32[32,24,128]{2,1,0:T(8,128)S(1)}, u32[]{:S(2)}, u32[]{:S(2)}) async-start(f32[32,24,128]{2,1,0:T(8,128)} %broadcast_in_dim.160), calls=%async_computation.2 | async-start | bytes 786432 | tf_op jit(solution)/shard_map/all_to_all | solution.py:16
  98.8 13.2 %collective-permute-start.3 = (f32[64,1,1536]{2,1,0:T(1,128)S(1)}, f32[64,1,1536]{2,1,0:T(1,128)}, u32[]{:S(2)}, u32[]{:S(2)}) collective-permute-start(f32[64,1,1536]{2,1,0:T(1,128)S(1)} %get-tuple-element.16.refs_3_), channel_id=1, source_target_pairs={{0,3},{1,0},{2,1},{3,2},{4,7},{5,4},{6,5},{7,6},{8,11},{9,8},{10,9... | collective-permute-start | bytes 1179656 | tf_op jit(solution)/shard_map/ppermute | solution.py:26
  101.6 13.6 %collective-permute-start = (f32[64,1,1536]{2,1,0:T(1,128)S(1)}, f32[64,1,1536]{2,1,0:T(1,128)}, u32[]{:S(2)}, u32[]{:S(2)}) collective-permute-start(f32[64,1,1536]{2,1,0:T(1,128)S(1)} %get-tuple-element.17.refs_2_), channel_id=1, source_target_pairs={{0,1},{1,2},{2,3},{3,0},{4,5},{5,6},{6,7},{7,4},{8,9},{9,10},{10,1... | collective-permute-start | bytes 1179656 | tf_op jit(solution)/shard_map/ppermute | solution.py:26
  105.6 17.9 %collective-permute-start.1 = (f32[64,1,1536]{2,1,0:T(1,128)S(1)}, f32[64,1,1536]{2,1,0:T(1,128)}, u32[]{:S(2)}, u32[]{:S(2)}) collective-permute-start(f32[64,1,1536]{2,1,0:T(1,128)S(1)} %get-tuple-element.16.refs_3_), channel_id=1, source_target_pairs={{0,1},{1,2},{2,3},{3,0},{4,5},{5,6},{6,7},{7,4},{8,9},{9,10},{10,1... | collective-permute-start | bytes 1179656 | tf_op jit(solution)/shard_map/ppermute | solution.py:26
  107.8 15.7 %collective-permute-start.2 = (f32[64,1,1536]{2,1,0:T(1,128)S(1)}, f32[64,1,1536]{2,1,0:T(1,128)}, u32[]{:S(2)}, u32[]{:S(2)}) collective-permute-start(f32[64,1,1536]{2,1,0:T(1,128)S(1)} %get-tuple-element.17.refs_2_), channel_id=1, source_target_pairs={{0,3},{1,0},{2,1},{3,2},{4,7},{5,4},{6,5},{7,6},{8,11},{9,8},{10,9... | collective-permute-start | bytes 1179656 | tf_op jit(solution)/shard_map/ppermute | solution.py:26
  112.1 16.8 %collective-permute-start.5 = (f32[64,1,1536]{2,1,0:T(1,128)}, f32[64,1,1536]{2,1,0:T(1,128)S(1)}, u32[]{:S(2)}, u32[]{:S(2)}) collective-permute-start(f32[64,1,1536]{2,1,0:T(1,128)} %collective-permute-done.3.refs_7_), channel_id=1, source_target_pairs={{0,3},{1,0},{2,1},{3,2},{4,7},{5,4},{6,5},{7,6},{8,11},{9,8},{10,9... | collective-permute-start | bytes 1179656 | tf_op jit(solution)/shard_map/ppermute | solution.py:26
  115.3 16.6 %collective-permute-start.4 = (f32[64,1,1536]{2,1,0:T(1,128)}, f32[64,1,1536]{2,1,0:T(1,128)}, u32[]{:S(2)}, u32[]{:S(2)}) collective-permute-start(f32[64,1,1536]{2,1,0:T(1,128)} %collective-permute-done.refs_4_), channel_id=1, source_target_pairs={{0,1},{1,2},{2,3},{3,0},{4,5},{5,6},{6,7},{7,4},{8,9},{9,10},{10,1... | collective-permute-start | bytes 1179656 | tf_op jit(solution)/shard_map/ppermute | solution.py:26

commit v4 on v3

--- a/solution.py
+++ b/solution.py
@@ -9,6 +9,7 @@
 NEAR = ("z_lo", "x", "core")
 LISTS = ("z_hi", *NEAR)
 LANES = 128
+FAR = 1e30
 HIGH = lax.Precision.HIGHEST
 
 
@@ -65,7 +66,7 @@
     return high, (values - high.astype(jnp.float32)).astype(jnp.bfloat16)
 
 
-def score_kernel(vectors, cents, penalty, own, touched, out):
+def score_kernel(vectors, cents, penalty, own, live, out):
     table = cents[...]
     base = jnp.sum(table * table, axis=0, keepdims=True)
     high, low = halved(table)
@@ -79,10 +80,11 @@
         dist = base + penalty[k : k + 1, :] - 2.0 * cross
         least = jnp.min(dist.T, axis=0, keepdims=True)
         gain = (own[k : k + 1, :] - least) / vectors.shape[2]
-        out[k : k + 1, :] = jnp.where(touched[k : k + 1, :] > 0.0, gain, 0.0)
-
-
-def scored(vectors, cents, penalty, own, touched):
+        near = least < 0.5 * FAR
+        out[k : k + 1, :] = jnp.where((live[k : k + 1, :] > 0.0) & near, gain, 0.0)
+
+
+def scored(vectors, cents, penalty, own, live):
     vmem = pl.BlockSpec(memory_space=pltpu.VMEM)
     return pl.pallas_call(
         score_kernel,
@@ -91,7 +93,7 @@
         out_specs=vmem,
         compiler_params=pltpu.CompilerParams(vmem_limit_bytes=16 * 2**20),
         name="score",
-    )(vectors, cents, penalty, own, touched)
+    )(vectors, cents, penalty, own, live)
 
 
 def put_rows(image, place, ref, base, start, width):
@@ -255,11 +257,10 @@
 
     near_slots = owner_map[nearby]
     hit = jnp.any(near_slots[None, :, :] == local_slots[:, None, None], axis=2)
-    penalty = jnp.tile(jnp.where(hit, 0.0, 1e30), (1, 2))
+    penalty = jnp.tile(jnp.where(hit, 0.0, FAR), (1, 2))
     own_cross = jnp.einsum("krd,kd->kr", vectors, centroids, precision=HIGH)
     own_dist = jnp.sum(centroids * centroids, axis=1)[:, None] - 2.0 * own_cross
-    touched = (valid & jnp.any(hit, axis=1)[:, None]).astype(jnp.float32)
-    gains = scored(vectors, cents, penalty, own_dist, touched)
+    gains = scored(vectors, cents, penalty, own_dist, valid.astype(jnp.float32))
 
     cut = lists_count // 2
     low, high = got[:cut, :, : depth * width], got[cut:, :, : depth * width]

time: 138 us -> 136 us (0.986)
  blocking collectives: 8.46 us -> 0 us
  starting transfers between devices: 46.6 us -> 50.7 us
  matrix products: 2.03 us -> 3.43 us
    all_to_all x1 -> x0, blocking collectives: 8.46 us -> none  [exchanged(): return lax.all_to_all(pieces, axis, 0, 0, tiled=True)]
    all_to_all x2 -> x3, waiting for transfers between devices: 43.7 us -> 48 us  [exchanged(): return lax.all_to_all(pieces, axis, 0, 0, tiled=True)]
    all_to_all x2 -> x3, starting transfers between devices: 29.5 us -> 33.7 us  [exchanged(): return lax.all_to_all(pieces, axis, 0, 0, tiled=True)]
    ppermute x6, waiting for transfers between devices: 8.75 us -> 4.88 us  [turned(): lax.ppermute(block, axis, [(i, (i + step) % length) for i in range(length)])]
    dot_general x1, matrix products: 0.61 us -> 2.01 us  [local(): partial_value = jnp.einsum('kar,krd->kad', halves, vectors, precision=HIGH)]
  transfers between devices with their start and end apart: 8 -> 9, of which waited for: 3 -> 4; matrix products, arithmetic and copies ran while one was open for 3% -> 6% of each run, Pallas kernels for 7% -> 7%
where the time goes in v4:
time: 136 us; the launch traced here: 134 us
  waiting for transfers between devices  52.9 us (39%)
  starting transfers between devices  50.7 us (37%)
  Pallas kernels  11.6 us (9%)
  local copies, waits for them, and re-layouts  10.5 us (8%)
  other arithmetic  4.11 us (3%)
  matrix products  3.43 us (3%)
    all_to_all x3, waiting for transfers between devices, exchanged(): return lax.all_to_all(pieces, axis, 0, 0, tiled=True)  48 us
    all_to_all x3, starting transfers between devices, exchanged(): return lax.all_to_all(pieces, axis, 0, 0, tiled=True)  33.7 us
    ppermute x6, starting transfers between devices, turned(): lax.ppermute(block, axis, [(i, (i + step) % length) for i in range(length)])  17.1 us
    pallas_call x1, Pallas kernels, near_rows(): pl.pallas_call(lambda *refs: near_kernel(width, total, skip, *refs), out_...  5.4 us
    ppermute x6, waiting for transfers between devices, turned(): lax.ppermute(block, axis, [(i, (i + step) % length) for i in range(length)])  4.88 us
    pallas_call x1, Pallas kernels, far_rows(): pl.pallas_call(lambda *refs: far_kernel(width, total, *refs), out_shape=(...  3.7 us
    gather x3, local copies, waits for them, and re-layouts, local(): near_slots = owner_map[nearby]  3.65 us
  transfers between devices with their start and end apart: 9, of which 4 were waited for; matrix products, arithmetic and copies ran while one was open for 6% of the time, Pallas kernels for 7%

profile of v4, /device:TPU:1, one launch (start us, length us, event | category | flops | bytes accessed | tf_op | source)
XLA Modules:
  0.0 134.3 jit_solution(12856224277806552642)
XLA Ops:
  0.7 1.0 select_reduce_fusion
  2.5 0.8 select_reduce_fusion.4
  4.4 2.0 %fusion.4 = f32[2,2,768]{2,1,0:T(2,128)S(1)} fusion(f32[2,256,768]{2,1,0:T(8,128)} %vectors.1, pred[2,2,256]{2,0,1:T(4,128)(4,1)S(1)} %get-tuple-element.13), kind=kOutput, calls=%fused_computation.24 | convolution fusion | flops 9437184 | bytes 1586176 | tf_op jit(solution)/shard_map/kar,krd->kad/dot_general | solution.py:225
  8.8 1.5 %broadcast_in_dim.158 = f32[128,1,1664]{2,1,0:T(1,128)} reshape(f32[128,1664]{1,0:T(8,128)S(1)} %pad_maximum_fusion) | data formatting | bytes 1703936 | tf_op jit(solution)/shard_map/broadcast_in_dim | solution.py:245
  10.3 20.4 %all-to-all-start = ((f32[128,1,1664]{2,1,0:T(1,128)}), f32[128,1,1664]{2,1,0:T(1,128)S(1)}, u32[]{:S(2)}, u32[]{:S(2)}) async-start(f32[128,1,1664]{2,1,0:T(1,128)} %broadcast_in_dim.158), calls=%async_computation | async-start | bytes 1703936 | tf_op jit(solution)/shard_map/all_to_all | solution.py:17
  31.8 43.5 %all-to-all-done = f32[128,1,1664]{2,1,0:T(1,128)S(1)} async-done(((f32[128,1,1664]{2,1,0:T(1,128)}), f32[128,1,1664]{2,1,0:T(1,128)S(1)}, u32[]{:S(2)}, u32[]{:S(2)}) %all-to-all-start) | async-done | bytes 852000 | tf_op jit(solution)/shard_map/all_to_all | solution.py:17
  75.4 1.0 select.42
  76.4 4.2 %all-to-all-start.1 = ((f32[4,32,128]{2,1,0:T(8,128)}), f32[4,32,128]{2,1,0:T(8,128)S(1)}, u32[]{:S(2)}, u32[]{:S(2)}) async-start(f32[4,32,128]{2,1,0:T(8,128)} %select.42), calls=%async_computation.1 | async-start | bytes 131072 | tf_op jit(solution)/shard_map/all_to_all | solution.py:17
  80.6 4.5 %all-to-all-done.1.refs_1_ = f32[4,32,128]{2,1,0:T(8,128)S(1)} async-done(((f32[4,32,128]{2,1,0:T(8,128)}), f32[4,32,128]{2,1,0:T(8,128)S(1)}, u32[]{:S(2)}, u32[]{:S(2)}) %all-to-all-start.1) | async-done | bytes 65568 | tf_op jit(solution)/shard_map/all_to_all | solution.py:17
  85.9 9.1 %all-to-all-start.2 = ((f32[32,24,128]{2,1,0:T(8,128)}), f32[32,24,128]{2,1,0:T(8,128)S(1)}, u32[]{:S(2)}, u32[]{:S(2)}) async-start(f32[32,24,128]{2,1,0:T(8,128)} %broadcast_in_dim.159), calls=%async_computation.2 | async-start | bytes 786432 | tf_op jit(solution)/shard_map/all_to_all | solution.py:17
  95.0 1.2 fusion.14
  96.2 2.8 %collective-permute-start.3 = (f32[64,1,1536]{2,1,0:T(1,128)S(1)}, f32[64,1,1536]{2,1,0:T(1,128)}, u32[]{:S(2)}, u32[]{:S(2)}) collective-permute-start(f32[64,1,1536]{2,1,0:T(1,128)S(1)} %get-tuple-element.14.refs_3_), channel_id=1, source_target_pairs={{0,3},{1,0},{2,1},{3,2},{4,7},{5,4},{6,5},{7,6},{8,11},{9,8},{10,9... | collective-permute-start | bytes 1179656 | tf_op jit(solution)/shard_map/ppermute | solution.py:27
  99.0 2.5 %collective-permute-start = (f32[64,1,1536]{2,1,0:T(1,128)S(1)}, f32[64,1,1536]{2,1,0:T(1,128)}, u32[]{:S(2)}, u32[]{:S(2)}) collective-permute-start(f32[64,1,1536]{2,1,0:T(1,128)S(1)} %get-tuple-element.15.refs_2_), channel_id=1, source_target_pairs={{0,1},{1,2},{2,3},{3,0},{4,5},{5,6},{6,7},{7,4},{8,9},{9,10},{10,1... | collective-permute-start | bytes 1179656 | tf_op jit(solution)/shard_map/ppermute | solution.py:27
  101.5 3.5 %gather_fusion.3 = s32[512]{0:T(512)S(1)} fusion(s32[256]{0:T(256)S(1)} %copy-done.1, s32[1024]{0:T(1024)S(1)} %pad_clamp_fusion), kind=kCustom, calls=%fused_computation.3 | custom fusion | bytes 6144 | tf_op jit(solution)/shard_map/gather | solution.py:258
  105.3 1.4 %fusion.6 = f32[2,1,256]{2,1,0:T(1,128)S(1)} fusion(f32[2,256,768]{2,1,0:T(8,128)S(1)} %copy-done, f32[2,768,1]{1,0,2:T(2,128)S(1)} %bitcast.34), kind=kOutput, calls=%fused_computation.27 | convolution fusion | flops 4718592 | bytes 1581056 | tf_op jit(solution)/shard_map/krd,kd->kr/dot_general | solution.py:261
  106.7 2.2 %collective-permute-start.1 = (f32[64,1,1536]{2,1,0:T(1,128)S(1)}, f32[64,1,1536]{2,1,0:T(1,128)}, u32[]{:S(2)}, u32[]{:S(2)}) collective-permute-start(f32[64,1,1536]{2,1,0:T(1,128)S(1)} %get-tuple-element.14.refs_3_), channel_id=1, source_target_pairs={{0,1},{1,2},{2,3},{3,0},{4,5},{5,6},{6,7},{7,4},{8,9},{9,10},{10,1... | collective-permute-start | bytes 1179656 | tf_op jit(solution)/shard_map/ppermute | solution.py:27
  108.9 4.3 %collective-permute-start.2 = (f32[64,1,1536]{2,1,0:T(1,128)S(1)}, f32[64,1,1536]{2,1,0:T(1,128)}, u32[]{:S(2)}, u32[]{:S(2)}) collective-permute-start(f32[64,1,1536]{2,1,0:T(1,128)S(1)} %get-tuple-element.15.refs_2_), channel_id=1, source_target_pairs={{0,3},{1,0},{2,1},{3,2},{4,7},{5,4},{6,5},{7,6},{8,11},{9,8},{10,9... | collective-permute-start | bytes 1179656 | tf_op jit(solution)/shard_map/ppermute | solution.py:27
  113.2 2.8 %collective-permute-start.5 = (f32[64,1,1536]{2,1,0:T(1,128)}, f32[64,1,1536]{2,1,0:T(1,128)S(1)}, u32[]{:S(2)}, u32[]{:S(2)}) collective-permute-start(f32[64,1,1536]{2,1,0:T(1,128)} %collective-permute-done.3.refs_7_), channel_id=1, source_target_pairs={{0,3},{1,0},{2,1},{3,2},{4,7},{5,4},{6,5},{7,6},{8,11},{9,8},{10,9... | collective-permute-start | bytes 1179656 | tf_op jit(solution)/shard_map/ppermute | solution.py:27
  116.1 2.5 %collective-permute-start.4 = (f32[64,1,1536]{2,1,0:T(1,128)}, f32[64,1,1536]{2,1,0:T(1,128)}, u32[]{:S(2)}, u32[]{:S(2)}) collective-permute-start(f32[64,1,1536]{2,1,0:T(1,128)} %collective-permute-done.refs_4_), channel_id=1, source_target_pairs={{0,1},{1,2},{2,3},{3,0},{4,5},{5,6},{6,7},{7,4},{8,9},{9,10},{10,1... | collective-permute-start | bytes 1179656 | tf_op jit(solution)/shard_map/ppermute | solution.py:27
  118.9 2.2 %collective-permute-done.1.refs_5_ = f32[64,1,1536]{2,1,0:T(1,128)} collective-permute-done((f32[64,1,1536]{2,1,0:T(1,128)S(1)}, f32[64,1,1536]{2,1,0:T(1,128)}, u32[]{:S(2)}, u32[]{:S(2)}) %collective-permute-start.1) | collective-permute-done | bytes 393248 | tf_op jit(solution)/shard_map/ppermute | solution.py:27
  121.1 5.4 %near.1 = (f32[1032,768]{1,0:T(8,128)S(1)}, s32[8,128]{1,0:T(8,128)S(1)}) custom-call(s32[1]{0:T(128)} %bitcast.13.refs_0_, f32[4,32,128]{2,1,0:T(8,128)S(1)} %all-to-all-done.1.refs_1_, f32[64,1,1536]{2,1,0:T(1,128)S(1)} %get-tuple-element.15.refs_2_, f32[64,1,1536]{2,1,0:T(1,128)S(1)} %get-tuple-element.14.refs_3_, ...), custom_call_target="tpu_custom_call" | custom-call | tf_op jit(solution)/shard_map/near/pallas_call | solution.py:143
  126.5 2.7 %collective-permute-done.5.refs_3_ = f32[64,1,1536]{2,1,0:T(1,128)S(1)} collective-permute-done((f32[64,1,1536]{2,1,0:T(1,128)}, f32[64,1,1536]{2,1,0:T(1,128)S(1)}, u32[]{:S(2)}, u32[]{:S(2)}) %collective-permute-start.5) | collective-permute-done | bytes 393248 | tf_op jit(solution)/shard_map/ppermute | solution.py:27
  129.1 3.7 %far.1 = (f32[1032,768]{1,0:T(8,128)S(1)}, f32[1024,768]{1,0:T(8,128)}) custom-call(s32[1]{0:T(128)} %bitcast.13.refs_0_, s32[8,128]{1,0:T(8,128)S(1)} %get-tuple-element.5.refs_1_, f32[64,1,1536]{2,1,0:T(1,128)} %collective-permute-done.4.refs_2_, f32[64,1,1536]{2,1,0:T(1,128)S(1)} %collective-permute-done.5.refs_3_, ...), custom_call_target="tpu_custom_call", output_to_operand_aliasing={{0}: (4, {})} | custom-call | tf_op jit(solution)/shard_map/far/pallas_call | solution.py:173
  132.9 1.5 %score.1 = f32[2,256]{1,0:T(2,128)} custom-call(f32[2,256,768]{2,1,0:T(8,128)S(1)} %copy-done, f32[768,128]{1,0:T(8,128)S(1)} %bitcast.32, f32[2,128]{1,0:T(2,128)S(1)} %tile.23.penalty, f32[2,256]{1,0:T(2,128)S(1)} %fusion.10.own, f32[2,256]{1,0:T(2,128)S(1)} %get-tuple-element.18.live), custom_call_target="tpu_custom_call" | custom-call | tf_op jit(solution)/shard_map/score/pallas_call | solution.py:89
  (66 shorter events, 6.7 us)
Async XLA Ops:
  0.6 6.3 %copy-start = (f32[2,256,768]{2,1,0:T(8,128)S(1)}, f32[2,256,768]{2,1,0:T(8,128)}, u32[]{:S(2)}) copy-start(f32[2,256,768]{2,1,0:T(8,128)} %vectors.1) | copy-start | bytes 4718596
  8.8 21.9 %copy-start.5 = (s32[64]{0:T(128)S(1)}, s32[64]{0:T(128)}, u32[]{:S(2)}) copy-start(s32[64]{0:T(128)} %param.13) | copy-start | bytes 772
  8.8 21.9 %copy-start.1 = (s32[256]{0:T(256)S(1)}, s32[256]{0:T(256)}, u32[]{:S(2)}) copy-start(s32[256]{0:T(256)} %param.15) | copy-start | bytes 3076
  8.8 22.8 %copy-start.4 = (s32[64,8]{0,1:T(8,128)S(1)}, s32[64,8]{0,1:T(8,128)}, u32[]{:S(2)}) copy-start(s32[64,8]{0,1:T(8,128)} %param.14) | copy-start | bytes 6148
  10.3 65.1 %all-to-all-start = ((f32[128,1,1664]{2,1,0:T(1,128)}), f32[128,1,1664]{2,1,0:T(1,128)S(1)}, u32[]{:S(2)}, u32[]{:S(2)}) async-start(f32[128,1,1664]{2,1,0:T(1,128)} %broadcast_in_dim.158), calls=%async_computation | async-start | bytes 1703936 | tf_op jit(solution)/shard_map/all_to_all | solution.py:17
  75.3 10.5 %copy-start.2 = (f32[128,1,1664]{2,1,0:T(1,128)}, f32[128,1,1664]{2,1,0:T(1,128)S(1)}, u32[]{:S(2)}) copy-start(f32[128,1,1664]{2,1,0:T(1,128)S(1)} %all-to-all-done) | copy-start | bytes 2555908
  76.4 8.7 %all-to-all-start.1 = ((f32[4,32,128]{2,1,0:T(8,128)}), f32[4,32,128]{2,1,0:T(8,128)S(1)}, u32[]{:S(2)}, u32[]{:S(2)}) async-start(f32[4,32,128]{2,1,0:T(8,128)} %select.42), calls=%async_computation.1 | async-start | bytes 131072 | tf_op jit(solution)/shard_map/all_to_all | solution.py:17
  85.9 47.0 %all-to-all-start.2 = ((f32[32,24,128]{2,1,0:T(8,128)}), f32[32,24,128]{2,1,0:T(8,128)S(1)}, u32[]{:S(2)}, u32[]{:S(2)}) async-start(f32[32,24,128]{2,1,0:T(8,128)} %broadcast_in_dim.159), calls=%async_computation.2 | async-start | bytes 786432 | tf_op jit(solution)/shard_map/all_to_all | solution.py:17
  96.2 17.0 %collective-permute-start.3 = (f32[64,1,1536]{2,1,0:T(1,128)S(1)}, f32[64,1,1536]{2,1,0:T(1,128)}, u32[]{:S(2)}, u32[]{:S(2)}) collective-permute-start(f32[64,1,1536]{2,1,0:T(1,128)S(1)} %get-tuple-element.14.refs_3_), channel_id=1, source_target_pairs={{0,3},{1,0},{2,1},{3,2},{4,7},{5,4},{6,5},{7,6},{8,11},{9,8},{10,9... | collective-permute-start | bytes 1179656 | tf_op jit(solution)/shard_map/ppermute | solution.py:27
  99.0 17.0 %collective-permute-start = (f32[64,1,1536]{2,1,0:T(1,128)S(1)}, f32[64,1,1536]{2,1,0:T(1,128)}, u32[]{:S(2)}, u32[]{:S(2)}) collective-permute-start(f32[64,1,1536]{2,1,0:T(1,128)S(1)} %get-tuple-element.15.refs_2_), channel_id=1, source_target_pairs={{0,1},{1,2},{2,3},{3,0},{4,5},{5,6},{6,7},{7,4},{8,9},{9,10},{10,1... | collective-permute-start | bytes 1179656 | tf_op jit(solution)/shard_map/ppermute | solution.py:27
  101.5 3.8 %copy-start.3 = (f32[2,768]{1,0:T(2,128)S(1)}, f32[2,768]{1,0:T(2,128)}, u32[]{:S(2)}) copy-start(f32[2,768]{1,0:T(2,128)} %param.12) | copy-start | bytes 18436
  106.7 14.3 %collective-permute-start.1 = (f32[64,1,1536]{2,1,0:T(1,128)S(1)}, f32[64,1,1536]{2,1,0:T(1,128)}, u32[]{:S(2)}, u32[]{:S(2)}) collective-permute-start(f32[64,1,1536]{2,1,0:T(1,128)S(1)} %get-tuple-element.14.refs_3_), channel_id=1, source_target_pairs={{0,1},{1,2},{2,3},{3,0},{4,5},{5,6},{6,7},{7,4},{8,9},{9,10},{10,1... | collective-permute-start | bytes 1179656 | tf_op jit(solution)/shard_map/ppermute | solution.py:27
  108.9 12.1 %collective-permute-start.2 = (f32[64,1,1536]{2,1,0:T(1,128)S(1)}, f32[64,1,1536]{2,1,0:T(1,128)}, u32[]{:S(2)}, u32[]{:S(2)}) collective-permute-start(f32[64,1,1536]{2,1,0:T(1,128)S(1)} %get-tuple-element.15.refs_2_), channel_id=1, source_target_pairs={{0,3},{1,0},{2,1},{3,2},{4,7},{5,4},{6,5},{7,6},{8,11},{9,8},{10,9... | collective-permute-start | bytes 1179656 | tf_op jit(solution)/shard_map/ppermute | solution.py:27
  113.2 15.9 %collective-permute-start.5 = (f32[64,1,1536]{2,1,0:T(1,128)}, f32[64,1,1536]{2,1,0:T(1,128)S(1)}, u32[]{:S(2)}, u32[]{:S(2)}) collective-permute-start(f32[64,1,1536]{2,1,0:T(1,128)} %collective-permute-done.3.refs_7_), channel_id=1, source_target_pairs={{0,3},{1,0},{2,1},{3,2},{4,7},{5,4},{6,5},{7,6},{8,11},{9,8},{10,9... | collective-permute-start | bytes 1179656 | tf_op jit(solution)/shard_map/ppermute | solution.py:27
  116.1 13.1 %collective-permute-start.4 = (f32[64,1,1536]{2,1,0:T(1,128)}, f32[64,1,1536]{2,1,0:T(1,128)}, u32[]{:S(2)}, u32[]{:S(2)}) collective-permute-start(f32[64,1,1536]{2,1,0:T(1,128)} %collective-permute-done.refs_4_), channel_id=1, source_target_pairs={{0,1},{1,2},{2,3},{3,0},{4,5},{5,6},{6,7},{7,4},{8,9},{9,10},{10,1... | collective-permute-start | bytes 1179656 | tf_op jit(solution)/shard_map/ppermute | solution.py:27

commit v5 on v4

--- a/solution.py
+++ b/solution.py
@@ -59,6 +59,123 @@
         compiler_params=pltpu.CompilerParams(vmem_limit_bytes=4 * 2**20),
         name="select",
     )(key, tail)
+
+
+def build_kernel(cols, me, *refs):
+    away, (out, *held, spot, scalars, sem, sems) = refs[:6], refs[6:]
+    fetches = [
+        pltpu.make_async_copy(far, near, sems.at[i])
+        for i, (far, near) in enumerate(zip(away, held))
+    ]
+    for fetch in fetches:
+        fetch.start()
+    dest, owner, source, sizes, labels, vectors = held
+    for fetch in fetches[:3]:
+        fetch.wait()
+    f32, i32 = jnp.float32, jnp.int32
+    lists, rows = labels.shape
+    width = vectors.shape[1]
+    moves, ids = dest.shape[1], owner.shape[1]
+
+    def spread(shape, dim):
+        return lax.broadcasted_iota(i32, shape, dim)
+
+    def eight(row):
+        return jnp.broadcast_to(row, (8, row.shape[1])).astype(f32)
+
+    hit = (spread((ids, moves), 0) == dest[...]).astype(f32)
+    slot = jnp.dot(eight(owner[...]), hit, precision=HIGH, preferred_element_type=f32)[0:1]
+    slot = slot.astype(i32)
+    dev = jnp.where(dest[...] >= 0, lax.shift_right_logical(slot, 1), -1)
+    code = (jnp.bitwise_and(slot, 1) + 1).astype(f32)
+    square = (moves, moves)
+    to = (spread(square, 0) == dev).astype(f32)
+    sooner = (spread(square, 0) < spread(square, 1)).astype(f32)
+    before = jnp.dot(to, sooner, preferred_element_type=f32)
+    codes, takes = [], []
+    for r in range(2):
+        pick = jnp.where(before == float(r), to, 0.0)
+        codes.append(jnp.sum(pick * code, axis=1, keepdims=True))
+        take = lax.dot_general(
+            eight(source[...]), pick, (((1,), (1,)), ((), ())),
+            precision=HIGH, preferred_element_type=f32,
+        )
+        takes.append(take[0:1])
+    spot[...] = jnp.concatenate(takes * 4, axis=0).astype(i32)
+    copy = pltpu.make_async_copy(spot, scalars, sem)
+    copy.start()
+
+    for fetch in fetches[3:]:
+        fetch.wait()
+    row = spread((1, rows), 1) + me[0] * rows
+    kinds = [
+        jnp.where(row < sizes[k], labels[k : k + 1, :], 2).astype(f32) for k in range(lists)
+    ]
+    kinds = jnp.concatenate(kinds * 4, axis=0).T
+    chunks = width // cols
+    chunk = spread((chunks, width), 1) // cols == spread((chunks, width), 0)
+    lane = spread((chunks, LANES), 1)
+    pieces, counts = [], jnp.zeros((chunks, LANES), f32)
+    each = LANES // 4
+    for k in range(lists):
+        block = vectors[k * rows : (k + 1) * rows, :]
+        for a in range(2):
+            mark = kinds[:, k : k + 1] == float(a)
+            total = jnp.sum(jnp.where(mark, block, 0.0), axis=0, keepdims=True)
+            number = jnp.sum(mark.astype(f32), axis=0, keepdims=True)
+            pieces.append(jnp.where(chunk, total, 0.0))
+            counts = counts + jnp.where(lane == (2 * k + a) * each + cols, number, 0.0)
+    pieces = jnp.concatenate(pieces, axis=0)
+    first = pieces.astype(jnp.bfloat16)
+    rest = pieces - first.astype(f32)
+    second = rest.astype(jnp.bfloat16)
+    third = (rest - second.astype(f32)).astype(jnp.bfloat16)
+    fold = (spread((width, LANES), 0) % cols == spread((width, LANES), 1)).astype(jnp.bfloat16)
+    parts = jnp.concatenate([first, second, third], axis=0)
+    folded = jnp.dot(parts, fold, preferred_element_type=f32)
+    lines = 4 * chunks
+    folded = folded[:lines] + folded[lines : 2 * lines] + folded[2 * lines :]
+    tail = counts
+    for b in range(4):
+        piece = folded[b * chunks : (b + 1) * chunks]
+        tail = tail + (pltpu.roll(piece, b * each, 1) if b else piece)
+    tail = jnp.concatenate([tail] * (moves // chunks), axis=0)
+    lane = spread((moves, LANES), 1)
+    for r in range(2):
+        tail = jnp.where(lane == cols + 1 + r, codes[r], tail)
+    out[:, 0, 2 * width :] = tail
+
+    copy.wait()
+
+    def body(d, carry):
+        for r in range(2):
+            out[d, :, r * width : (r + 1) * width] = vectors[pl.ds(scalars[r, d], 1), :]
+        return carry
+
+    lax.fori_loop(0, moves, body, 0, unroll=4)
+
+
+def built(me, sizes, source, dest, owner, labels, vectors, cols):
+    smem = pl.BlockSpec(memory_space=pltpu.SMEM)
+    hbm = pl.BlockSpec(memory_space=pltpu.HBM)
+    moves = dest.shape[1]
+    away = [dest, owner, source, sizes, labels, vectors]
+    held = [(pltpu.SMEM if x is sizes else pltpu.VMEM)(x.shape, x.dtype) for x in away]
+    return pl.pallas_call(
+        lambda *refs: build_kernel(cols, *refs),
+        out_shape=jax.ShapeDtypeStruct((moves, 1, 2 * vectors.shape[1] + LANES), jnp.float32),
+        in_specs=[smem] + [hbm] * len(away),
+        out_specs=pl.BlockSpec(memory_space=pltpu.VMEM),
+        scratch_shapes=held
+        + [
+            pltpu.VMEM((8, LANES), jnp.int32),
+            pltpu.SMEM((8, LANES), jnp.int32),
+            pltpu.SemaphoreType.DMA,
+            pltpu.SemaphoreType.DMA((len(away),)),
+        ],
+        compiler_params=pltpu.CompilerParams(vmem_limit_bytes=16 * 2**20),
+        name="build",
+    )(me, *[pltpu.with_memory_space_constraint(x, pltpu.HBM) for x in away])
 
 
 def halved(values):
@@ -197,52 +314,16 @@
     start_row = my_help * rows
     splits = split_ids.shape[0]
     local_slots = first + jnp.arange(list_dev, dtype=jnp.int32)
-    row_index = start_row + jnp.arange(rows, dtype=jnp.int32)
-    valid = row_index[None, :] < list_sizes[:, None]
-    moves = mover_source.shape[0]
-    ids = jnp.arange(owner_map.shape[0], dtype=jnp.int32)
-    devs = jnp.arange(lists_count, dtype=jnp.int32)
     depth = 2
 
-    live = mover_dest >= 0
-    slot = jnp.sum(
-        jnp.where(mover_dest[:, None] == ids[None, :], owner_map[None, :], 0), axis=1
-    )
-    dev = jnp.where(live, slot // list_dev, -1)
-    order = jnp.arange(moves, dtype=jnp.int32)
-    same = (dev[:, None] == dev[None, :]) & (order[:, None] > order[None, :])
-    rank = jnp.sum(same.astype(jnp.int32), axis=1)
-    to = dev[:, None] == devs[None, :]
-    picked = [to & (rank == r)[:, None] for r in range(depth)]
-    codes = [
-        jnp.sum(jnp.where(p, (slot % list_dev + 1)[:, None], 0), axis=0) for p in picked
-    ]
-    takes = [jnp.sum(jnp.where(p, mover_source[:, None], 0), axis=0) for p in picked]
-    flat_rows = vectors.reshape(list_dev * rows, width)
-    sent = [flat_rows[t] for t in takes]
-
-    halves = jnp.stack([(labels == 0) & valid, (labels == 1) & valid], axis=1).astype(jnp.float32)
-    partial_value = jnp.einsum("kar,krd->kad", halves, vectors, precision=HIGH)
-    counts = jnp.sum(halves, axis=2)
     chunks = lax.axis_size(NEAR)
     cols = width // chunks
-    half = list_dev * 2
-    lanes = jnp.moveaxis(partial_value.reshape(half, chunks, cols), 1, 0)
-    lanes = jnp.concatenate(
-        [
-            lanes,
-            jnp.broadcast_to(counts.reshape(1, half, 1), (chunks, half, 1)),
-            jnp.zeros((chunks, half, LANES // half - cols - 1), jnp.float32),
-        ],
-        axis=2,
-    ).reshape(chunks, LANES)
-    lanes = jnp.tile(lanes, (lists_count // chunks, 1))
-    lane = jnp.arange(LANES, dtype=jnp.int32)
-    for r in range(depth):
-        lanes = jnp.where(
-            lane[None, :] == cols + 1 + r, codes[r].astype(jnp.float32)[:, None], lanes
-        )
-    bucket = jnp.concatenate([*sent, lanes], axis=1)[:, None, :]
+    flat_rows = vectors.reshape(list_dev * rows, width)
+    me = my_help[None]
+    bucket = built(
+        me, list_sizes, mover_source[None], mover_dest[None], owner_map[None], labels,
+        flat_rows, cols,
+    )
     got = exchanged(bucket, LISTS)
 
     split_slots = owner_map[split_ids]
@@ -257,10 +338,12 @@
 
     near_slots = owner_map[nearby]
     hit = jnp.any(near_slots[None, :, :] == local_slots[:, None, None], axis=2)
+    row_index = start_row + jnp.arange(rows, dtype=jnp.int32)
+    live = (row_index[None, :] < list_sizes[:, None]).astype(jnp.float32)
     penalty = jnp.tile(jnp.where(hit, 0.0, FAR), (1, 2))
     own_cross = jnp.einsum("krd,kd->kr", vectors, centroids, precision=HIGH)
     own_dist = jnp.sum(centroids * centroids, axis=1)[:, None] - 2.0 * own_cross
-    gains = scored(vectors, cents, penalty, own_dist, valid.astype(jnp.float32))
+    gains = scored(vectors, cents, penalty, own_dist, live)
 
     cut = lists_count // 2
     low, high = got[:cut, :, : depth * width], got[cut:, :, : depth * width]
@@ -272,7 +355,6 @@
     far_high = turned(above_high, "help", -1)
     arrive_cap = lists_count * help_count * ((depth + list_dev - 1) // list_dev)
     total = list_dev * arrive_cap
-    me = my_help[None]
     image, place = near_rows(me, over_help, [low, high, below_low, below_high, above_low, above_high], width, total, cols + 1)
     out = far_rows(me, place, [far_low, far_high], image, width, total)
     return gains, out.reshape(list_dev, arrive_cap, width)

time: 136 us -> 130 us (0.956)
  other arithmetic: 4.11 us -> 0.42 us
  Pallas kernels: 11.6 us -> 15.1 us
  local copies, waits for them, and re-layouts: 10.5 us -> 7.74 us
  matrix products: 3.43 us -> 1.42 us
    pallas_call x0 -> x1, Pallas kernels: none -> 4.26 us  [built(): pl.pallas_call(lambda *refs: build_kernel(cols, *refs), out_shape=jax.Sha...]
    ppermute x6, waiting for transfers between devices: 4.88 us -> 8.91 us  [turned(): lax.ppermute(block, axis, [(i, (i + step) % length) for i in range(length)])]
    all_to_all x3, waiting for transfers between devices: 48 us -> 44.2 us  [exchanged(): return lax.all_to_all(pieces, axis, 0, 0, tiled=True)]
    reduce_sum x4 -> x0, other arithmetic: 2.05 us -> none  [the longest x1 0.96 us: local(): jnp.sum(jnp.where(mover_dest[:, None] == ids[None, :], owner_map[None, :]...]
    dot_general x1 -> x0, matrix products: 2.01 us -> none  [local(): partial_value = jnp.einsum('kar,krd->kad', halves, vectors, precision=HIGH)]
    broadcast_in_dim x4 -> x0, local copies, waits for them, and re-layouts: 1.64 us -> none  [the longest x1 1.49 us: local(): bucket = jnp.concatenate([*sent, lanes], axis=1)[:, None, :]]
    gather x2 -> x0, local copies, waits for them, and re-layouts: 1.63 us -> none  [local(): sent = [flat_rows[t] for t in takes]]
  transfers between devices with their start and end apart: 9 -> 9, of which waited for: 4 -> 4; matrix products, arithmetic and copies ran while one was open for 6% -> 6% of each run, Pallas kernels for 7% -> 6%
where the time goes in v5:
time: 130 us
  waiting for transfers between devices  53.2 us (41%)
  starting transfers between devices  50.7 us (39%)
  Pallas kernels  15.1 us (12%)
  local copies, waits for them, and re-layouts  7.74 us (6%)
  matrix products  1.42 us (1%)
    all_to_all x3, waiting for transfers between devices, exchanged(): return lax.all_to_all(pieces, axis, 0, 0, tiled=True)  44.2 us
    all_to_all x3, starting transfers between devices, exchanged(): return lax.all_to_all(pieces, axis, 0, 0, tiled=True)  33.7 us
    ppermute x6, starting transfers between devices, turned(): lax.ppermute(block, axis, [(i, (i + step) % length) for i in range(length)])  17.1 us
    ppermute x6, waiting for transfers between devices, turned(): lax.ppermute(block, axis, [(i, (i + step) % length) for i in range(length)])  8.91 us
    pallas_call x1, Pallas kernels, near_rows(): pl.pallas_call(lambda *refs: near_kernel(width, total, skip, *refs), out_...  5.07 us
    pallas_call x1, Pallas kernels, built(): pl.pallas_call(lambda *refs: build_kernel(cols, *refs), out_shape=jax.Sha...  4.26 us
    gather x3, local copies, waits for them, and re-layouts, local(): near_slots = owner_map[nearby]  3.65 us
    pallas_call x1, Pallas kernels, far_rows(): pl.pallas_call(lambda *refs: far_kernel(width, total, *refs), out_shape=(...  3.3 us
  transfers between devices with their start and end apart: 9, of which 4 were waited for; matrix products, arithmetic and copies ran while one was open for 6% of the time, Pallas kernels for 6%

profile of v5, /device:TPU:1, one launch (start us, length us, event | category | flops | bytes accessed | tf_op | source)
XLA Modules:
  0.0 129.5 jit_solution(16184221537241207450)
XLA Ops:
  0.7 4.3 %build.1 = f32[128,1,1664]{2,1,0:T(1,128)} custom-call(s32[1]{0:T(128)} %bitcast.refs_0_, s32[1,128]{1,0:T(1,128)} %bitcast.19, s32[1,256]{1,0:T(1,128)} %bitcast.17, s32[1,128]{1,0:T(1,128)} %bitcast.20, s32[2]{0:T(128)} %refs_4_.1, s32[2,256]{1,0:T(2,128)} %refs_5_.1, f32[512,768]{1,0:T(8,128)} %bitcast.15), custom_call_target="tpu_custom_call" | custom-call | tf_op jit(solution)/shard_map/build/pallas_call | solution.py:164
  4.9 20.4 %all-to-all-start = ((f32[128,1,1664]{2,1,0:T(1,128)}), f32[128,1,1664]{2,1,0:T(1,128)S(1)}, u32[]{:S(2)}, u32[]{:S(2)}) async-start(f32[128,1,1664]{2,1,0:T(1,128)} %build.1), calls=%async_computation | async-start | bytes 1703936 | tf_op jit(solution)/shard_map/all_to_all | solution.py:17
  25.4 0.8 gather_fusion
  26.5 3.5 %gather_fusion.1 = s32[512]{0:T(512)S(1)} fusion(s32[256]{0:T(256)S(1)} %copy-done.1, s32[1024]{0:T(1024)S(1)} %pad_clamp_fusion), kind=kCustom, calls=%fused_computation.1 | custom fusion | bytes 6144 | tf_op jit(solution)/shard_map/gather | solution.py:339
  30.2 39.9 %all-to-all-done = f32[128,1,1664]{2,1,0:T(1,128)S(1)} async-done(((f32[128,1,1664]{2,1,0:T(1,128)}), f32[128,1,1664]{2,1,0:T(1,128)S(1)}, u32[]{:S(2)}, u32[]{:S(2)}) %all-to-all-start) | async-done | bytes 852000 | tf_op jit(solution)/shard_map/all_to_all | solution.py:17
  70.0 0.9 copy-done.2
  71.0 1.0 select.30
  72.0 4.2 %all-to-all-start.1 = ((f32[4,32,128]{2,1,0:T(8,128)}), f32[4,32,128]{2,1,0:T(8,128)S(1)}, u32[]{:S(2)}, u32[]{:S(2)}) async-start(f32[4,32,128]{2,1,0:T(8,128)} %select.30), calls=%async_computation.1 | async-start | bytes 131072 | tf_op jit(solution)/shard_map/all_to_all | solution.py:17
  76.3 4.4 %all-to-all-done.1.refs_1_ = f32[4,32,128]{2,1,0:T(8,128)S(1)} async-done(((f32[4,32,128]{2,1,0:T(8,128)}), f32[4,32,128]{2,1,0:T(8,128)S(1)}, u32[]{:S(2)}, u32[]{:S(2)}) %all-to-all-start.1) | async-done | bytes 65568 | tf_op jit(solution)/shard_map/all_to_all | solution.py:17
  80.7 0.8 broadcast_in_dim.59
  81.5 9.1 %all-to-all-start.2 = ((f32[32,24,128]{2,1,0:T(8,128)}), f32[32,24,128]{2,1,0:T(8,128)S(1)}, u32[]{:S(2)}, u32[]{:S(2)}) async-start(f32[32,24,128]{2,1,0:T(8,128)} %broadcast_in_dim.59), calls=%async_computation.2 | async-start | bytes 786432 | tf_op jit(solution)/shard_map/all_to_all | solution.py:17
  90.6 1.2 fusion.3
  91.8 2.8 %collective-permute-start.3 = (f32[64,1,1536]{2,1,0:T(1,128)S(1)}, f32[64,1,1536]{2,1,0:T(1,128)S(1)}, u32[]{:S(2)}, u32[]{:S(2)}) collective-permute-start(f32[64,1,1536]{2,1,0:T(1,128)S(1)} %get-tuple-element.8.refs_3_), channel_id=1, source_target_pairs={{0,3},{1,0},{2,1},{3,2},{4,7},{5,4},{6,5},{7,6},{8,11},{9,8},{10,9... | collective-permute-start | bytes 1179656 | tf_op jit(solution)/shard_map/ppermute | solution.py:27
  94.6 2.5 %collective-permute-start = (f32[64,1,1536]{2,1,0:T(1,128)S(1)}, f32[64,1,1536]{2,1,0:T(1,128)}, u32[]{:S(2)}, u32[]{:S(2)}) collective-permute-start(f32[64,1,1536]{2,1,0:T(1,128)S(1)} %get-tuple-element.9.refs_2_), channel_id=1, source_target_pairs={{0,1},{1,2},{2,3},{3,0},{4,5},{5,6},{6,7},{7,4},{8,9},{9,10},{10,1... | collective-permute-start | bytes 1179656 | tf_op jit(solution)/shard_map/ppermute | solution.py:27
  97.4 1.4 %fusion = f32[2,1,256]{2,1,0:T(1,128)S(1)} fusion(f32[2,256,768]{2,1,0:T(8,128)S(1)} %copy-done, f32[2,768,1]{1,0,2:T(2,128)S(1)} %bitcast.18), kind=kOutput, calls=%fused_computation.6 | convolution fusion | flops 4718592 | bytes 1581056 | tf_op jit(solution)/shard_map/krd,kd->kr/dot_general | solution.py:344
  98.8 2.2 %collective-permute-start.1 = (f32[64,1,1536]{2,1,0:T(1,128)S(1)}, f32[64,1,1536]{2,1,0:T(1,128)S(1)}, u32[]{:S(2)}, u32[]{:S(2)}) collective-permute-start(f32[64,1,1536]{2,1,0:T(1,128)S(1)} %get-tuple-element.8.refs_3_), channel_id=1, source_target_pairs={{0,1},{1,2},{2,3},{3,0},{4,5},{5,6},{6,7},{7,4},{8,9},{9,10},{10,1... | collective-permute-start | bytes 1179656 | tf_op jit(solution)/shard_map/ppermute | solution.py:27
  101.0 4.3 %collective-permute-start.2 = (f32[64,1,1536]{2,1,0:T(1,128)S(1)}, f32[64,1,1536]{2,1,0:T(1,128)S(1)}, u32[]{:S(2)}, u32[]{:S(2)}) collective-permute-start(f32[64,1,1536]{2,1,0:T(1,128)S(1)} %get-tuple-element.9.refs_2_), channel_id=1, source_target_pairs={{0,3},{1,0},{2,1},{3,2},{4,7},{5,4},{6,5},{7,6},{8,11},{9,8},{10,9... | collective-permute-start | bytes 1179656 | tf_op jit(solution)/shard_map/ppermute | solution.py:27
  105.3 2.9 %collective-permute-start.5 = (f32[64,1,1536]{2,1,0:T(1,128)S(1)}, f32[64,1,1536]{2,1,0:T(1,128)S(1)}, u32[]{:S(2)}, u32[]{:S(2)}) collective-permute-start(f32[64,1,1536]{2,1,0:T(1,128)S(1)} %collective-permute-done.3.refs_7_), channel_id=1, source_target_pairs={{0,3},{1,0},{2,1},{3,2},{4,7},{5,4},{6,5},{7,6},{8,11},{9,8},{10,9... | collective-permute-start | bytes 1179656 | tf_op jit(solution)/shard_map/ppermute | solution.py:27
  108.2 2.4 %collective-permute-start.4 = (f32[64,1,1536]{2,1,0:T(1,128)}, f32[64,1,1536]{2,1,0:T(1,128)S(1)}, u32[]{:S(2)}, u32[]{:S(2)}) collective-permute-start(f32[64,1,1536]{2,1,0:T(1,128)} %collective-permute-done.refs_4_), channel_id=1, source_target_pairs={{0,1},{1,2},{2,3},{3,0},{4,5},{5,6},{6,7},{7,4},{8,9},{9,10},{10,1... | collective-permute-start | bytes 1179656 | tf_op jit(solution)/shard_map/ppermute | solution.py:27
  110.8 5.6 %collective-permute-done.1.refs_5_ = f32[64,1,1536]{2,1,0:T(1,128)S(1)} collective-permute-done((f32[64,1,1536]{2,1,0:T(1,128)S(1)}, f32[64,1,1536]{2,1,0:T(1,128)S(1)}, u32[]{:S(2)}, u32[]{:S(2)}) %collective-permute-start.1) | collective-permute-done | bytes 393248 | tf_op jit(solution)/shard_map/ppermute | solution.py:27
  116.3 5.1 %near.1 = (f32[1032,768]{1,0:T(8,128)S(1)}, s32[8,128]{1,0:T(8,128)S(1)}) custom-call(s32[1]{0:T(128)} %bitcast.refs_0_, f32[4,32,128]{2,1,0:T(8,128)S(1)} %all-to-all-done.1.refs_1_, f32[64,1,1536]{2,1,0:T(1,128)S(1)} %get-tuple-element.9.refs_2_, f32[64,1,1536]{2,1,0:T(1,128)S(1)} %get-tuple-element.8.refs_3_, ...), custom_call_target="tpu_custom_call" | custom-call | tf_op jit(solution)/shard_map/near/pallas_call | solution.py:260
  121.4 3.3 %collective-permute-done.4.refs_2_ = f32[64,1,1536]{2,1,0:T(1,128)S(1)} collective-permute-done((f32[64,1,1536]{2,1,0:T(1,128)}, f32[64,1,1536]{2,1,0:T(1,128)S(1)}, u32[]{:S(2)}, u32[]{:S(2)}) %collective-permute-start.4) | collective-permute-done | bytes 393248 | tf_op jit(solution)/shard_map/ppermute | solution.py:27
  124.7 3.3 %far.1 = (f32[1032,768]{1,0:T(8,128)S(1)}, f32[1024,768]{1,0:T(8,128)}) custom-call(s32[1]{0:T(128)} %bitcast.refs_0_, s32[8,128]{1,0:T(8,128)S(1)} %get-tuple-element.5.refs_1_, f32[64,1,1536]{2,1,0:T(1,128)S(1)} %collective-permute-done.4.refs_2_, f32[64,1,1536]{2,1,0:T(1,128)S(1)} %collective-permute-done.5.refs_3_, ...), custom_call_target="tpu_custom_call", output_to_operand_aliasing={{0}: (4, {})} | custom-call | tf_op jit(solution)/shard_map/far/pallas_call | solution.py:290
  128.1 1.4 %score.1 = f32[2,256]{1,0:T(2,128)} custom-call(f32[2,256,768]{2,1,0:T(8,128)S(1)} %copy-done, f32[768,128]{1,0:T(8,128)S(1)} %bitcast.16, f32[2,128]{1,0:T(2,128)S(1)} %tile.10.penalty, f32[2,256]{1,0:T(2,128)S(1)} %fusion.2.own, f32[2,256]{1,0:T(2,128)S(1)} %compare_convert_fusion.live), custom_call_target="tpu_custom_call" | custom-call | tf_op jit(solution)/shard_map/score/pallas_call | solution.py:206
  (42 shorter events, 1.0 us)
Async XLA Ops:
  0.6 24.7 %copy-start.6 = (s32[64]{0:T(128)S(1)}, s32[64]{0:T(128)}, u32[]{:S(2)}) copy-start(s32[64]{0:T(128)} %param.13) | copy-start | bytes 772
  0.6 24.7 %copy-start.1 = (s32[256]{0:T(256)S(1)}, s32[256]{0:T(256)}, u32[]{:S(2)}) copy-start(s32[256]{0:T(256)} %param.15) | copy-start | bytes 3076
  4.9 21.4 %copy-start.4 = (s32[64,8]{0,1:T(8,128)S(1)}, s32[64,8]{0,1:T(8,128)}, u32[]{:S(2)}) copy-start(s32[64,8]{0,1:T(8,128)} %param.14) | copy-start | bytes 6148
  4.9 65.1 %all-to-all-start = ((f32[128,1,1664]{2,1,0:T(1,128)}), f32[128,1,1664]{2,1,0:T(1,128)S(1)}, u32[]{:S(2)}, u32[]{:S(2)}) async-start(f32[128,1,1664]{2,1,0:T(1,128)} %build.1), calls=%async_computation | async-start | bytes 1703936 | tf_op jit(solution)/shard_map/all_to_all | solution.py:17
  70.0 0.9 copy-start.2
  71.0 26.3 %copy-start.3 = (f32[2,768]{1,0:T(2,128)S(1)}, f32[2,768]{1,0:T(2,128)}, u32[]{:S(2)}) copy-start(f32[2,768]{1,0:T(2,128)} %param.12) | copy-start | bytes 18436
  71.0 26.4 %copy-start = (f32[2,256,768]{2,1,0:T(8,128)S(1)}, f32[2,256,768]{2,1,0:T(8,128)}, u32[]{:S(2)}) copy-start(f32[2,256,768]{2,1,0:T(8,128)} %vectors.1) | copy-start | bytes 4718596
  72.0 8.7 %all-to-all-start.1 = ((f32[4,32,128]{2,1,0:T(8,128)}), f32[4,32,128]{2,1,0:T(8,128)S(1)}, u32[]{:S(2)}, u32[]{:S(2)}) async-start(f32[4,32,128]{2,1,0:T(8,128)} %select.30), calls=%async_computation.1 | async-start | bytes 131072 | tf_op jit(solution)/shard_map/all_to_all | solution.py:17
  81.5 46.6 %all-to-all-start.2 = ((f32[32,24,128]{2,1,0:T(8,128)}), f32[32,24,128]{2,1,0:T(8,128)S(1)}, u32[]{:S(2)}, u32[]{:S(2)}) async-start(f32[32,24,128]{2,1,0:T(8,128)} %broadcast_in_dim.59), calls=%async_computation.2 | async-start | bytes 786432 | tf_op jit(solution)/shard_map/all_to_all | solution.py:17
  90.6 20.0 %copy-start.5 = (s32[2]{0:T(128)S(1)}, s32[2]{0:T(128)}, u32[]{:S(2)}) copy-start(s32[2]{0:T(128)} %refs_4_.1) | copy-start | bytes 28
  91.8 13.5 %collective-permute-start.3 = (f32[64,1,1536]{2,1,0:T(1,128)S(1)}, f32[64,1,1536]{2,1,0:T(1,128)S(1)}, u32[]{:S(2)}, u32[]{:S(2)}) collective-permute-start(f32[64,1,1536]{2,1,0:T(1,128)S(1)} %get-tuple-element.8.refs_3_), channel_id=1, source_target_pairs={{0,3},{1,0},{2,1},{3,2},{4,7},{5,4},{6,5},{7,6},{8,11},{9,8},{10,9... | collective-permute-start | bytes 1179656 | tf_op jit(solution)/shard_map/ppermute | solution.py:27
  94.6 13.5 %collective-permute-start = (f32[64,1,1536]{2,1,0:T(1,128)S(1)}, f32[64,1,1536]{2,1,0:T(1,128)}, u32[]{:S(2)}, u32[]{:S(2)}) collective-permute-start(f32[64,1,1536]{2,1,0:T(1,128)S(1)} %get-tuple-element.9.refs_2_), channel_id=1, source_target_pairs={{0,1},{1,2},{2,3},{3,0},{4,5},{5,6},{6,7},{7,4},{8,9},{9,10},{10,1... | collective-permute-start | bytes 1179656 | tf_op jit(solution)/shard_map/ppermute | solution.py:27
  98.8 17.5 %collective-permute-start.1 = (f32[64,1,1536]{2,1,0:T(1,128)S(1)}, f32[64,1,1536]{2,1,0:T(1,128)S(1)}, u32[]{:S(2)}, u32[]{:S(2)}) collective-permute-start(f32[64,1,1536]{2,1,0:T(1,128)S(1)} %get-tuple-element.8.refs_3_), channel_id=1, source_target_pairs={{0,1},{1,2},{2,3},{3,0},{4,5},{5,6},{6,7},{7,4},{8,9},{9,10},{10,1... | collective-permute-start | bytes 1179656 | tf_op jit(solution)/shard_map/ppermute | solution.py:27
  101.0 15.3 %collective-permute-start.2 = (f32[64,1,1536]{2,1,0:T(1,128)S(1)}, f32[64,1,1536]{2,1,0:T(1,128)S(1)}, u32[]{:S(2)}, u32[]{:S(2)}) collective-permute-start(f32[64,1,1536]{2,1,0:T(1,128)S(1)} %get-tuple-element.9.refs_2_), channel_id=1, source_target_pairs={{0,3},{1,0},{2,1},{3,2},{4,7},{5,4},{6,5},{7,6},{8,11},{9,8},{10,9... | collective-permute-start | bytes 1179656 | tf_op jit(solution)/shard_map/ppermute | solution.py:27
  105.3 16.1 %collective-permute-start.5 = (f32[64,1,1536]{2,1,0:T(1,128)S(1)}, f32[64,1,1536]{2,1,0:T(1,128)S(1)}, u32[]{:S(2)}, u32[]{:S(2)}) collective-permute-start(f32[64,1,1536]{2,1,0:T(1,128)S(1)} %collective-permute-done.3.refs_7_), channel_id=1, source_target_pairs={{0,3},{1,0},{2,1},{3,2},{4,7},{5,4},{6,5},{7,6},{8,11},{9,8},{10,9... | collective-permute-start | bytes 1179656 | tf_op jit(solution)/shard_map/ppermute | solution.py:27
  108.2 16.6 %collective-permute-start.4 = (f32[64,1,1536]{2,1,0:T(1,128)}, f32[64,1,1536]{2,1,0:T(1,128)S(1)}, u32[]{:S(2)}, u32[]{:S(2)}) collective-permute-start(f32[64,1,1536]{2,1,0:T(1,128)} %collective-permute-done.refs_4_), channel_id=1, source_target_pairs={{0,1},{1,2},{2,3},{3,0},{4,5},{5,6},{6,7},{7,4},{8,9},{9,10},{10,1... | collective-permute-start | bytes 1179656 | tf_op jit(solution)/shard_map/ppermute | solution.py:27

commit v6 on v5

--- a/solution.py
+++ b/solution.py
@@ -6,7 +6,8 @@
 from jax.sharding import Mesh
 from jax.sharding import PartitionSpec as P
 
-NEAR = ("z_lo", "x", "core")
+PAIR = ("x", "core")
+NEAR = ("z_lo", *PAIR)
 LISTS = ("z_hi", *NEAR)
 LANES = 128
 FAR = 1e30
@@ -61,7 +62,7 @@
     )(key, tail)
 
 
-def build_kernel(cols, me, *refs):
+def build_kernel(cols, pairs, me, *refs):
     away, (out, *held, spot, scalars, sem, sems) = refs[:6], refs[6:]
     fetches = [
         pltpu.make_async_copy(far, near, sems.at[i])
@@ -113,7 +114,9 @@
     ]
     kinds = jnp.concatenate(kinds * 4, axis=0).T
     chunks = width // cols
-    chunk = spread((chunks, width), 1) // cols == spread((chunks, width), 0)
+    line = spread((chunks, width), 0)
+    line = line % pairs * (chunks // pairs) + line // pairs
+    chunk = spread((chunks, width), 1) // cols == line
     lane = spread((chunks, LANES), 1)
     pieces, counts = [], jnp.zeros((chunks, LANES), f32)
     each = LANES // 4
@@ -155,14 +158,14 @@
     lax.fori_loop(0, moves, body, 0, unroll=4)
 
 
-def built(me, sizes, source, dest, owner, labels, vectors, cols):
+def built(me, sizes, source, dest, owner, labels, vectors, cols, pairs):
     smem = pl.BlockSpec(memory_space=pltpu.SMEM)
     hbm = pl.BlockSpec(memory_space=pltpu.HBM)
     moves = dest.shape[1]
     away = [dest, owner, source, sizes, labels, vectors]
     held = [(pltpu.SMEM if x is sizes else pltpu.VMEM)(x.shape, x.dtype) for x in away]
     return pl.pallas_call(
-        lambda *refs: build_kernel(cols, *refs),
+        lambda *refs: build_kernel(cols, pairs, *refs),
         out_shape=jax.ShapeDtypeStruct((moves, 1, 2 * vectors.shape[1] + LANES), jnp.float32),
         in_specs=[smem] + [hbm] * len(away),
         out_specs=pl.BlockSpec(memory_space=pltpu.VMEM),
@@ -226,7 +229,9 @@
 def near_kernel(width, total, skip, me, codes, *refs):
     *parts, image, place, spot, scalars, sem = refs
     lines = codes.shape[2]
-    code = jnp.concatenate([codes[y, skip : skip + 2, :] for y in range(4)], axis=0)
+    code = jnp.concatenate(
+        [codes[me[1] * 4 + y, skip : skip + 2, :] for y in range(4)], axis=0
+    )
     before = (
         lax.broadcasted_iota(jnp.int32, (lines, lines), 0)
         < lax.broadcasted_iota(jnp.int32, (lines, lines), 1)
@@ -322,7 +327,7 @@
     me = my_help[None]
     bucket = built(
         me, list_sizes, mover_source[None], mover_dest[None], owner_map[None], labels,
-        flat_rows, cols,
+        flat_rows, cols, lax.axis_size(PAIR),
     )
     got = exchanged(bucket, LISTS)
 
@@ -330,11 +335,16 @@
     k_ids = jnp.arange(list_dev, dtype=jnp.int32)[:, None]
     key = jnp.where(split_slots[None] % list_dev == k_ids, split_slots[None] // list_dev, -1)
     tail = got[:, :, depth * width :]
-    chosen = selected(key.reshape(1, list_dev * splits), tail, cols, depth, help_count)
-    over_help = exchanged(chosen, "help")
-    sums = jnp.sum(over_help[:, : cols + 1], axis=0)
-    means = sums[:cols] / sums[cols:]
-    cents = copies(means, NEAR).reshape(width, 2 * splits)
+    groups = lax.axis_size("z_lo")
+    chosen = selected(
+        key.reshape(1, list_dev * splits), tail, cols, depth, groups * help_count
+    )
+    over_help = exchanged(chosen, ("z_lo", "help"))
+    parts = over_help.reshape(groups, help_count, *over_help.shape[1:])
+    sums = jnp.sum(parts[:, :, : cols + 1], axis=1)
+    means = sums[:, :cols] / sums[:, cols:]
+    means = means.reshape(groups * cols, 2 * splits)
+    cents = copies(means, PAIR).reshape(width, 2 * splits)
 
     near_slots = owner_map[nearby]
     hit = jnp.any(near_slots[None, :, :] == local_slots[:, None, None], axis=2)
@@ -355,7 +365,8 @@
     far_high = turned(above_high, "help", -1)
     arrive_cap = lists_count * help_count * ((depth + list_dev - 1) // list_dev)
     total = list_dev * arrive_cap
-    image, place = near_rows(me, over_help, [low, high, below_low, below_high, above_low, above_high], width, total, cols + 1)
+    where = jnp.stack([my_help, lax.axis_index("z_lo")])
+    image, place = near_rows(where, over_help, [low, high, below_low, below_high, above_low, above_high], width, total, cols + 1)
     out = far_rows(me, place, [far_low, far_high], image, width, total)
     return gains, out.reshape(list_dev, arrive_cap, width)
 

time: 130 us -> 120 us (0.923)
  waiting for transfers between devices: 53.2 us -> 42.2 us
  starting transfers between devices: 50.7 us -> 52.9 us
  local copies, waits for them, and re-layouts: 7.74 us -> 5.73 us
    ppermute x6, waiting for transfers between devices: 8.91 us -> 2.44 us  [turned(): lax.ppermute(block, axis, [(i, (i + step) % length) for i in range(length)])]
    all_to_all x3, waiting for transfers between devices: 44.2 us -> 39.7 us  [exchanged(): return lax.all_to_all(pieces, axis, 0, 0, tiled=True)]
    ppermute x6, starting transfers between devices: 17.1 us -> 19.4 us  [turned(): lax.ppermute(block, axis, [(i, (i + step) % length) for i in range(length)])]
  transfers between devices with their start and end apart: 9 -> 9, of which waited for: 4 -> 3; matrix products, arithmetic and copies ran while one was open for 6% -> 6% of each run, Pallas kernels for 6% -> 8%
where the time goes in v6:
time: 120 us
  starting transfers between devices  52.9 us (44%)
  waiting for transfers between devices  42.2 us (35%)
  Pallas kernels  16 us (13%)
  local copies, waits for them, and re-layouts  5.73 us (5%)
  matrix products  1.42 us (1%)
    all_to_all x3, waiting for transfers between devices, exchanged(): return lax.all_to_all(pieces, axis, 0, 0, tiled=True)  39.7 us
    all_to_all x3, starting transfers between devices, exchanged(): return lax.all_to_all(pieces, axis, 0, 0, tiled=True)  33.5 us
    ppermute x6, starting transfers between devices, turned(): lax.ppermute(block, axis, [(i, (i + step) % length) for i in range(length)])  19.4 us
    pallas_call x1, Pallas kernels, near_rows(): pl.pallas_call(lambda *refs: near_kernel(width, total, skip, *refs), out_...  5.41 us
    pallas_call x1, Pallas kernels, built(): pl.pallas_call(lambda *refs: build_kernel(cols, pairs, *refs), out_shape=...  4.26 us
    pallas_call x1, Pallas kernels, far_rows(): pl.pallas_call(lambda *refs: far_kernel(width, total, *refs), out_shape=(...  3.7 us
    gather x3, local copies, waits for them, and re-layouts, local(): near_slots = owner_map[nearby]  3.65 us
    ppermute x6, waiting for transfers between devices, turned(): lax.ppermute(block, axis, [(i, (i + step) % length) for i in range(length)])  2.44 us
  transfers between devices with their start and end apart: 9, of which 3 were waited for; matrix products, arithmetic and copies ran while one was open for 6% of the time, Pallas kernels for 8%

profile of v6, /device:TPU:1, one launch (start us, length us, event | category | flops | bytes accessed | tf_op | source)
XLA Modules:
  0.0 119.7 jit_solution(683374811927950023)
XLA Ops:
  0.7 4.3 %build.1 = f32[128,1,1664]{2,1,0:T(1,128)} custom-call(s32[1]{0:T(128)} %bitcast.refs_0_, s32[1,128]{1,0:T(1,128)} %bitcast.24, s32[1,256]{1,0:T(1,128)} %bitcast.20, s32[1,128]{1,0:T(1,128)} %bitcast.25, s32[2]{0:T(128)} %refs_4_.1, s32[2,256]{1,0:T(2,128)} %refs_5_.1, f32[512,768]{1,0:T(8,128)} %bitcast.17), custom_call_target="tpu_custom_call" | custom-call | tf_op jit(solution)/shard_map/build/pallas_call | solution.py:167
  4.9 20.4 %all-to-all-start = ((f32[128,1,1664]{2,1,0:T(1,128)}), f32[128,1,1664]{2,1,0:T(1,128)S(1)}, u32[]{:S(2)}, u32[]{:S(2)}) async-start(f32[128,1,1664]{2,1,0:T(1,128)} %build.1), calls=%async_computation | async-start | bytes 1703936 | tf_op jit(solution)/shard_map/all_to_all | solution.py:18
  25.4 0.8 gather_fusion
  26.4 0.1 reshape.139
  26.5 3.5 %gather_fusion.1 = s32[512]{0:T(512)S(1)} fusion(s32[256]{0:T(256)S(1)} %copy-done.1, s32[1024]{0:T(1024)S(1)} %pad_clamp_fusion), kind=kCustom, calls=%fused_computation.1 | custom fusion | bytes 6144 | tf_op jit(solution)/shard_map/gather | solution.py:349
  30.3 39.7 %all-to-all-done = f32[128,1,1664]{2,1,0:T(1,128)S(1)} async-done(((f32[128,1,1664]{2,1,0:T(1,128)}), f32[128,1,1664]{2,1,0:T(1,128)S(1)}, u32[]{:S(2)}, u32[]{:S(2)}) %all-to-all-start) | async-done | bytes 852000 | tf_op jit(solution)/shard_map/all_to_all | solution.py:18
  70.1 1.1 select.30
  71.2 8.0 %all-to-all-start.1 = ((f32[16,32,128]{2,1,0:T(8,128)}), f32[16,32,128]{2,1,0:T(8,128)S(1)}, u32[]{:S(2)}, u32[]{:S(2)}) async-start(f32[16,32,128]{2,1,0:T(8,128)} %select.30), calls=%async_computation.1 | async-start | bytes 524288 | tf_op jit(solution)/shard_map/all_to_all | solution.py:18
  79.2 0.1 compare_reduce_fusion
  79.4 4.5 %collective-permute-start.3 = (f32[64,1,1536]{2,1,0:T(1,128)S(1)}, f32[64,1,1536]{2,1,0:T(1,128)}, u32[]{:S(2)}, u32[]{:S(2)}) collective-permute-start(f32[64,1,1536]{2,1,0:T(1,128)S(1)} %get-tuple-element.8.refs_3_), channel_id=1, source_target_pairs={{0,3},{1,0},{2,1},{3,2},{4,7},{5,4},{6,5},{7,6},{8,11},{9,8},{10,9... | collective-permute-start | bytes 1179656 | tf_op jit(solution)/shard_map/ppermute | solution.py:28
  83.9 1.9 %collective-permute-start = (f32[64,1,1536]{2,1,0:T(1,128)S(1)}, f32[64,1,1536]{2,1,0:T(1,128)}, u32[]{:S(2)}, u32[]{:S(2)}) collective-permute-start(f32[64,1,1536]{2,1,0:T(1,128)S(1)} %get-tuple-element.9.refs_2_), channel_id=1, source_target_pairs={{0,1},{1,2},{2,3},{3,0},{4,5},{5,6},{6,7},{7,4},{8,9},{9,10},{10,1... | collective-permute-start | bytes 1179656 | tf_op jit(solution)/shard_map/ppermute | solution.py:28
  85.9 1.4 %fusion = f32[2,1,256]{2,1,0:T(1,128)S(1)} fusion(f32[2,256,768]{2,1,0:T(8,128)S(1)} %copy-done, f32[2,768,1]{1,0,2:T(2,128)S(1)} %bitcast.22), kind=kOutput, calls=%fused_computation.6 | convolution fusion | flops 4718592 | bytes 1581056 | tf_op jit(solution)/shard_map/krd,kd->kr/dot_general | solution.py:354
  87.3 2.2 %collective-permute-start.1 = (f32[64,1,1536]{2,1,0:T(1,128)S(1)}, f32[64,1,1536]{2,1,0:T(1,128)}, u32[]{:S(2)}, u32[]{:S(2)}) collective-permute-start(f32[64,1,1536]{2,1,0:T(1,128)S(1)} %get-tuple-element.8.refs_3_), channel_id=1, source_target_pairs={{0,1},{1,2},{2,3},{3,0},{4,5},{5,6},{6,7},{7,4},{8,9},{9,10},{10,1... | collective-permute-start | bytes 1179656 | tf_op jit(solution)/shard_map/ppermute | solution.py:28
  89.4 4.3 %collective-permute-start.2 = (f32[64,1,1536]{2,1,0:T(1,128)S(1)}, f32[64,1,1536]{2,1,0:T(1,128)}, u32[]{:S(2)}, u32[]{:S(2)}) collective-permute-start(f32[64,1,1536]{2,1,0:T(1,128)S(1)} %get-tuple-element.9.refs_2_), channel_id=1, source_target_pairs={{0,3},{1,0},{2,1},{3,2},{4,7},{5,4},{6,5},{7,6},{8,11},{9,8},{10,9... | collective-permute-start | bytes 1179656 | tf_op jit(solution)/shard_map/ppermute | solution.py:28
  93.8 0.2 collective-permute-done.3.refs_7_
  94.0 4.5 %collective-permute-start.5 = (f32[64,1,1536]{2,1,0:T(1,128)}, f32[64,1,1536]{2,1,0:T(1,128)S(1)}, u32[]{:S(2)}, u32[]{:S(2)}) collective-permute-start(f32[64,1,1536]{2,1,0:T(1,128)} %collective-permute-done.3.refs_7_), channel_id=1, source_target_pairs={{0,3},{1,0},{2,1},{3,2},{4,7},{5,4},{6,5},{7,6},{8,11},{9,8},{10,9... | collective-permute-start | bytes 1179656 | tf_op jit(solution)/shard_map/ppermute | solution.py:28
  98.6 1.9 %collective-permute-start.4 = (f32[64,1,1536]{2,1,0:T(1,128)}, f32[64,1,1536]{2,1,0:T(1,128)}, u32[]{:S(2)}, u32[]{:S(2)}) collective-permute-start(f32[64,1,1536]{2,1,0:T(1,128)} %collective-permute-done.refs_4_), channel_id=1, source_target_pairs={{0,1},{1,2},{2,3},{3,0},{4,5},{5,6},{6,7},{7,4},{8,9},{9,10},{10,1... | collective-permute-start | bytes 1179656 | tf_op jit(solution)/shard_map/ppermute | solution.py:28
  100.6 0.8 broadcast_in_dim.61
  101.4 5.1 %all-to-all-start.2 = ((f32[8,96,128]{2,1,0:T(8,128)}), f32[8,96,128]{2,1,0:T(8,128)S(1)}, u32[]{:S(2)}, u32[]{:S(2)}) async-start(f32[8,96,128]{2,1,0:T(8,128)} %broadcast_in_dim.61), calls=%async_computation.2 | async-start | bytes 786432 | tf_op jit(solution)/shard_map/all_to_all | solution.py:18
  106.7 0.1 multiply_reduce_fusion
  106.9 5.4 %near.1 = (f32[1032,768]{1,0:T(8,128)S(1)}, s32[8,128]{1,0:T(8,128)S(1)}) custom-call(s32[2]{0:T(128)S(1)} %pad_add_fusion.refs_0_, f32[16,32,128]{2,1,0:T(8,128)S(1)} %all-to-all-done.1.refs_1_, f32[64,1,1536]{2,1,0:T(1,128)S(1)} %get-tuple-element.9.refs_2_, f32[64,1,1536]{2,1,0:T(1,128)S(1)} %get-tuple-element.8.refs_3_, ...), custom_call_target="tpu_custom_call" | custom-call | tf_op jit(solution)/shard_map/near/pallas_call | solution.py:265
  112.3 2.2 %collective-permute-done.4.refs_2_ = f32[64,1,1536]{2,1,0:T(1,128)} collective-permute-done((f32[64,1,1536]{2,1,0:T(1,128)}, f32[64,1,1536]{2,1,0:T(1,128)}, u32[]{:S(2)}, u32[]{:S(2)}) %collective-permute-start.4) | collective-permute-done | bytes 393248 | tf_op jit(solution)/shard_map/ppermute | solution.py:28
  114.5 3.7 %far.1 = (f32[1032,768]{1,0:T(8,128)S(1)}, f32[1024,768]{1,0:T(8,128)}) custom-call(s32[1]{0:T(128)} %bitcast.refs_0_, s32[8,128]{1,0:T(8,128)S(1)} %get-tuple-element.5.refs_1_, f32[64,1,1536]{2,1,0:T(1,128)} %collective-permute-done.4.refs_2_, f32[64,1,1536]{2,1,0:T(1,128)S(1)} %collective-permute-done.5.refs_3_, ...), custom_call_target="tpu_custom_call", output_to_operand_aliasing={{0}: (4, {})} | custom-call | tf_op jit(solution)/shard_map/far/pallas_call | solution.py:295
  118.2 1.5 %score.1 = f32[2,256]{1,0:T(2,128)} custom-call(f32[2,256,768]{2,1,0:T(8,128)S(1)} %copy-done, f32[768,128]{1,0:T(8,128)S(1)} %bitcast.19, f32[2,128]{1,0:T(2,128)S(1)} %tile.10.penalty, f32[2,256]{1,0:T(2,128)S(1)} %fusion.2.own, f32[2,256]{1,0:T(2,128)S(1)} %compare_convert_fusion.live), custom_call_target="tpu_custom_call" | custom-call | tf_op jit(solution)/shard_map/score/pallas_call | solution.py:209
  (41 shorter events, 0.9 us)
Async XLA Ops:
  0.6 24.7 %copy-start.5 = (s32[64]{0:T(128)S(1)}, s32[64]{0:T(128)}, u32[]{:S(2)}) copy-start(s32[64]{0:T(128)} %param.13) | copy-start | bytes 772
  0.6 24.7 %copy-start.1 = (s32[256]{0:T(256)S(1)}, s32[256]{0:T(256)}, u32[]{:S(2)}) copy-start(s32[256]{0:T(256)} %param.15) | copy-start | bytes 3076
  4.9 21.4 %copy-start.3 = (s32[64,8]{0,1:T(8,128)S(1)}, s32[64,8]{0,1:T(8,128)}, u32[]{:S(2)}) copy-start(s32[64,8]{0,1:T(8,128)} %param.14) | copy-start | bytes 6148
  4.9 65.1 %all-to-all-start = ((f32[128,1,1664]{2,1,0:T(1,128)}), f32[128,1,1664]{2,1,0:T(1,128)S(1)}, u32[]{:S(2)}, u32[]{:S(2)}) async-start(f32[128,1,1664]{2,1,0:T(1,128)} %build.1), calls=%async_computation | async-start | bytes 1703936 | tf_op jit(solution)/shard_map/all_to_all | solution.py:18
  26.5 3.7 %copy-start.4 = (s32[2]{0:T(128)S(1)}, s32[2]{0:T(128)}, u32[]{:S(2)}) copy-start(s32[2]{0:T(128)} %refs_4_.1) | copy-start | bytes 28
  30.0 55.8 %copy-start = (f32[2,256,768]{2,1,0:T(8,128)S(1)}, f32[2,256,768]{2,1,0:T(8,128)}, u32[]{:S(2)}) copy-start(f32[2,256,768]{2,1,0:T(8,128)} %vectors.1) | copy-start | bytes 4718596
  30.0 55.8 %copy-start.2 = (f32[2,768]{1,0:T(2,128)S(1)}, f32[2,768]{1,0:T(2,128)}, u32[]{:S(2)}) copy-start(f32[2,768]{1,0:T(2,128)} %param.12) | copy-start | bytes 18436
  71.2 29.3 %all-to-all-start.1 = ((f32[16,32,128]{2,1,0:T(8,128)}), f32[16,32,128]{2,1,0:T(8,128)S(1)}, u32[]{:S(2)}, u32[]{:S(2)}) async-start(f32[16,32,128]{2,1,0:T(8,128)} %select.30), calls=%async_computation.1 | async-start | bytes 524288 | tf_op jit(solution)/shard_map/all_to_all | solution.py:18
  79.4 14.6 %collective-permute-start.3 = (f32[64,1,1536]{2,1,0:T(1,128)S(1)}, f32[64,1,1536]{2,1,0:T(1,128)}, u32[]{:S(2)}, u32[]{:S(2)}) collective-permute-start(f32[64,1,1536]{2,1,0:T(1,128)S(1)} %get-tuple-element.8.refs_3_), channel_id=1, source_target_pairs={{0,3},{1,0},{2,1},{3,2},{4,7},{5,4},{6,5},{7,6},{8,11},{9,8},{10,9... | collective-permute-start | bytes 1179656 | tf_op jit(solution)/shard_map/ppermute | solution.py:28
  83.9 14.7 %collective-permute-start = (f32[64,1,1536]{2,1,0:T(1,128)S(1)}, f32[64,1,1536]{2,1,0:T(1,128)}, u32[]{:S(2)}, u32[]{:S(2)}) collective-permute-start(f32[64,1,1536]{2,1,0:T(1,128)S(1)} %get-tuple-element.9.refs_2_), channel_id=1, source_target_pairs={{0,1},{1,2},{2,3},{3,0},{4,5},{5,6},{6,7},{7,4},{8,9},{9,10},{10,1... | collective-permute-start | bytes 1179656 | tf_op jit(solution)/shard_map/ppermute | solution.py:28
  87.3 19.6 %collective-permute-start.1 = (f32[64,1,1536]{2,1,0:T(1,128)S(1)}, f32[64,1,1536]{2,1,0:T(1,128)}, u32[]{:S(2)}, u32[]{:S(2)}) collective-permute-start(f32[64,1,1536]{2,1,0:T(1,128)S(1)} %get-tuple-element.8.refs_3_), channel_id=1, source_target_pairs={{0,1},{1,2},{2,3},{3,0},{4,5},{5,6},{6,7},{7,4},{8,9},{9,10},{10,1... | collective-permute-start | bytes 1179656 | tf_op jit(solution)/shard_map/ppermute | solution.py:28
  89.4 17.4 %collective-permute-start.2 = (f32[64,1,1536]{2,1,0:T(1,128)S(1)}, f32[64,1,1536]{2,1,0:T(1,128)}, u32[]{:S(2)}, u32[]{:S(2)}) collective-permute-start(f32[64,1,1536]{2,1,0:T(1,128)S(1)} %get-tuple-element.9.refs_2_), channel_id=1, source_target_pairs={{0,3},{1,0},{2,1},{3,2},{4,7},{5,4},{6,5},{7,6},{8,11},{9,8},{10,9... | collective-permute-start | bytes 1179656 | tf_op jit(solution)/shard_map/ppermute | solution.py:28
  94.0 18.2 %collective-permute-start.5 = (f32[64,1,1536]{2,1,0:T(1,128)}, f32[64,1,1536]{2,1,0:T(1,128)S(1)}, u32[]{:S(2)}, u32[]{:S(2)}) collective-permute-start(f32[64,1,1536]{2,1,0:T(1,128)} %collective-permute-done.3.refs_7_), channel_id=1, source_target_pairs={{0,3},{1,0},{2,1},{3,2},{4,7},{5,4},{6,5},{7,6},{8,11},{9,8},{10,9... | collective-permute-start | bytes 1179656 | tf_op jit(solution)/shard_map/ppermute | solution.py:28
  98.6 15.9 %collective-permute-start.4 = (f32[64,1,1536]{2,1,0:T(1,128)}, f32[64,1,1536]{2,1,0:T(1,128)}, u32[]{:S(2)}, u32[]{:S(2)}) collective-permute-start(f32[64,1,1536]{2,1,0:T(1,128)} %collective-permute-done.refs_4_), channel_id=1, source_target_pairs={{0,1},{1,2},{2,3},{3,0},{4,5},{5,6},{6,7},{7,4},{8,9},{9,10},{10,1... | collective-permute-start | bytes 1179656 | tf_op jit(solution)/shard_map/ppermute | solution.py:28
  101.4 16.8 %all-to-all-start.2 = ((f32[8,96,128]{2,1,0:T(8,128)}), f32[8,96,128]{2,1,0:T(8,128)S(1)}, u32[]{:S(2)}, u32[]{:S(2)}) async-start(f32[8,96,128]{2,1,0:T(8,128)} %broadcast_in_dim.61), calls=%async_computation.2 | async-start | bytes 786432 | tf_op jit(solution)/shard_map/all_to_all | solution.py:18

commit v7 on v5

--- a/solution.py
+++ b/solution.py
@@ -62,7 +62,7 @@
 
 
 def build_kernel(cols, me, *refs):
-    away, (out, *held, spot, scalars, sem, sems) = refs[:6], refs[6:]
+    away, (final, *held, out, spot, scalars, sem, sems) = refs[:6], refs[6:]
     fetches = [
         pltpu.make_async_copy(far, near, sems.at[i])
         for i, (far, near) in enumerate(zip(away, held))
@@ -152,26 +152,37 @@
             out[d, :, r * width : (r + 1) * width] = vectors[pl.ds(scalars[r, d], 1), :]
         return carry
 
-    lax.fori_loop(0, moves, body, 0, unroll=4)
+    stores = []
+    for part in range(4):
+        lines = moves // 4
+        lax.fori_loop(part * lines, (part + 1) * lines, body, 0, unroll=8)
+        block = pl.ds(part * lines, lines)
+        stores.append(
+            pltpu.make_async_copy(out.at[block], final.at[block], sems.at[len(away) + part])
+        )
+        stores[-1].start()
+    for store in stores:
+        store.wait()
 
 
 def built(me, sizes, source, dest, owner, labels, vectors, cols):
     smem = pl.BlockSpec(memory_space=pltpu.SMEM)
     hbm = pl.BlockSpec(memory_space=pltpu.HBM)
-    moves = dest.shape[1]
+    shape = (dest.shape[1], 1, 2 * vectors.shape[1] + LANES)
     away = [dest, owner, source, sizes, labels, vectors]
     held = [(pltpu.SMEM if x is sizes else pltpu.VMEM)(x.shape, x.dtype) for x in away]
     return pl.pallas_call(
         lambda *refs: build_kernel(cols, *refs),
-        out_shape=jax.ShapeDtypeStruct((moves, 1, 2 * vectors.shape[1] + LANES), jnp.float32),
+        out_shape=jax.ShapeDtypeStruct(shape, jnp.float32),
         in_specs=[smem] + [hbm] * len(away),
-        out_specs=pl.BlockSpec(memory_space=pltpu.VMEM),
+        out_specs=hbm,
         scratch_shapes=held
         + [
+            pltpu.VMEM(shape, jnp.float32),
             pltpu.VMEM((8, LANES), jnp.int32),
             pltpu.SMEM((8, LANES), jnp.int32),
             pltpu.SemaphoreType.DMA,
-            pltpu.SemaphoreType.DMA((len(away),)),
+            pltpu.SemaphoreType.DMA((len(away) + 4,)),
         ],
         compiler_params=pltpu.CompilerParams(vmem_limit_bytes=16 * 2**20),
         name="build",
@@ -220,7 +231,7 @@
             image[pl.ds(p, 1), :] = ref[i, :, r * width : (r + 1) * width]
         return carry
 
-    lax.fori_loop(0, ref.shape[0], body, 0, unroll=4)
+    lax.fori_loop(0, ref.shape[0], body, 0, unroll=8)
 
 
 def near_kernel(width, total, skip, me, codes, *refs):
@@ -272,7 +283,7 @@
         ],
         compiler_params=pltpu.CompilerParams(vmem_limit_bytes=16 * 2**20),
         name="near",
-    )(me, codes, *parts)
+    )(me, codes, *[pltpu.with_memory_space_constraint(x, pltpu.VMEM) for x in parts])
 
 
 def far_kernel(width, total, me, place, low, high, old, image, out, sem):
@@ -299,7 +310,7 @@
         input_output_aliases={2 + len(parts): 0},
         compiler_params=pltpu.CompilerParams(vmem_limit_bytes=16 * 2**20),
         name="far",
-    )(me, place, *parts, image)[1]
+    )(me, place, *[pltpu.with_memory_space_constraint(x, pltpu.VMEM) for x in parts], image)[1]
 
 
 def local(

time: 130 us -> 130 us (level)
  no operation moved by 1% of the time
where the time goes in v7:
time: 130 us; the launch traced here: 129 us
  waiting for transfers between devices  53.3 us (41%)
  starting transfers between devices  50.7 us (39%)
  Pallas kernels  14.7 us (11%)
  local copies, waits for them, and re-layouts  7.74 us (6%)
  matrix products  1.42 us (1%)
    all_to_all x3, waiting for transfers between devices, exchanged(): return lax.all_to_all(pieces, axis, 0, 0, tiled=True)  44.2 us
    all_to_all x3, starting transfers between devices, exchanged(): return lax.all_to_all(pieces, axis, 0, 0, tiled=True)  33.7 us
    ppermute x6, starting transfers between devices, turned(): lax.ppermute(block, axis, [(i, (i + step) % length) for i in range(length)])  17.1 us
    ppermute x6, waiting for transfers between devices, turned(): lax.ppermute(block, axis, [(i, (i + step) % length) for i in range(length)])  9.01 us
    pallas_call x1, Pallas kernels, near_rows(): pl.pallas_call(lambda *refs: near_kernel(width, total, skip, *refs), out_...  4.96 us
    pallas_call x1, Pallas kernels, built(): pl.pallas_call(lambda *refs: build_kernel(cols, *refs), out_shape=jax.Sha...  3.98 us
    gather x3, local copies, waits for them, and re-layouts, local(): near_slots = owner_map[nearby]  3.65 us
    pallas_call x1, Pallas kernels, far_rows(): pl.pallas_call(lambda *refs: far_kernel(width, total, *refs), out_shape=(...  3.24 us
  transfers between devices with their start and end apart: 9, of which 4 were waited for; matrix products, arithmetic and copies ran while one was open for 6% of the time, Pallas kernels for 6%

profile of v7, /device:TPU:1, one launch (start us, length us, event | category | flops | bytes accessed | tf_op | source)
XLA Modules:
  0.0 129.2 jit_solution(7234233478919280982)
XLA Ops:
  0.7 4.0 %build.1 = f32[128,1,1664]{2,1,0:T(1,128)} custom-call(s32[1]{0:T(128)} %bitcast.refs_0_, s32[1,128]{1,0:T(1,128)} %bitcast.19, s32[1,256]{1,0:T(1,128)} %bitcast.17, s32[1,128]{1,0:T(1,128)} %bitcast.20, s32[2]{0:T(128)} %refs_4_.1, s32[2,256]{1,0:T(2,128)} %refs_5_.1, f32[512,768]{1,0:T(8,128)} %bitcast.15), custom_call_target="tpu_custom_call" | custom-call | tf_op jit(solution)/shard_map/build/pallas_call | solution.py:174
  4.7 20.4 %all-to-all-start = ((f32[128,1,1664]{2,1,0:T(1,128)}), f32[128,1,1664]{2,1,0:T(1,128)S(1)}, u32[]{:S(2)}, u32[]{:S(2)}) async-start(f32[128,1,1664]{2,1,0:T(1,128)} %build.1), calls=%async_computation | async-start | bytes 1703936 | tf_op jit(solution)/shard_map/all_to_all | solution.py:17
  25.1 0.8 gather_fusion
  26.2 3.5 %gather_fusion.1 = s32[512]{0:T(512)S(1)} fusion(s32[256]{0:T(256)S(1)} %copy-done.1, s32[1024]{0:T(1024)S(1)} %pad_clamp_fusion), kind=kCustom, calls=%fused_computation.1 | custom fusion | bytes 6144 | tf_op jit(solution)/shard_map/gather | solution.py:350
  29.9 39.9 %all-to-all-done = f32[128,1,1664]{2,1,0:T(1,128)S(1)} async-done(((f32[128,1,1664]{2,1,0:T(1,128)}), f32[128,1,1664]{2,1,0:T(1,128)S(1)}, u32[]{:S(2)}, u32[]{:S(2)}) %all-to-all-start) | async-done | bytes 852000 | tf_op jit(solution)/shard_map/all_to_all | solution.py:17
  69.7 0.9 copy-done.2
  70.7 1.0 select.30
  71.7 4.2 %all-to-all-start.1 = ((f32[4,32,128]{2,1,0:T(8,128)}), f32[4,32,128]{2,1,0:T(8,128)S(1)}, u32[]{:S(2)}, u32[]{:S(2)}) async-start(f32[4,32,128]{2,1,0:T(8,128)} %select.30), calls=%async_computation.1 | async-start | bytes 131072 | tf_op jit(solution)/shard_map/all_to_all | solution.py:17
  76.0 4.4 %all-to-all-done.1.refs_1_ = f32[4,32,128]{2,1,0:T(8,128)S(1)} async-done(((f32[4,32,128]{2,1,0:T(8,128)}), f32[4,32,128]{2,1,0:T(8,128)S(1)}, u32[]{:S(2)}, u32[]{:S(2)}) %all-to-all-start.1) | async-done | bytes 65568 | tf_op jit(solution)/shard_map/all_to_all | solution.py:17
  80.4 0.8 broadcast_in_dim.59
  81.2 9.1 %all-to-all-start.2 = ((f32[32,24,128]{2,1,0:T(8,128)}), f32[32,24,128]{2,1,0:T(8,128)S(1)}, u32[]{:S(2)}, u32[]{:S(2)}) async-start(f32[32,24,128]{2,1,0:T(8,128)} %broadcast_in_dim.59), calls=%async_computation.2 | async-start | bytes 786432 | tf_op jit(solution)/shard_map/all_to_all | solution.py:17
  90.3 1.2 fusion.3
  91.5 2.8 %collective-permute-start.3 = (f32[64,1,1536]{2,1,0:T(1,128)S(1)}, f32[64,1,1536]{2,1,0:T(1,128)S(1)}, u32[]{:S(2)}, u32[]{:S(2)}) collective-permute-start(f32[64,1,1536]{2,1,0:T(1,128)S(1)} %get-tuple-element.8.refs_3_), channel_id=1, source_target_pairs={{0,3},{1,0},{2,1},{3,2},{4,7},{5,4},{6,5},{7,6},{8,11},{9,8},{10,9... | collective-permute-start | bytes 1179656 | tf_op jit(solution)/shard_map/ppermute | solution.py:27
  94.3 2.5 %collective-permute-start = (f32[64,1,1536]{2,1,0:T(1,128)S(1)}, f32[64,1,1536]{2,1,0:T(1,128)}, u32[]{:S(2)}, u32[]{:S(2)}) collective-permute-start(f32[64,1,1536]{2,1,0:T(1,128)S(1)} %get-tuple-element.9.refs_2_), channel_id=1, source_target_pairs={{0,1},{1,2},{2,3},{3,0},{4,5},{5,6},{6,7},{7,4},{8,9},{9,10},{10,1... | collective-permute-start | bytes 1179656 | tf_op jit(solution)/shard_map/ppermute | solution.py:27
  97.1 1.4 %fusion = f32[2,1,256]{2,1,0:T(1,128)S(1)} fusion(f32[2,256,768]{2,1,0:T(8,128)S(1)} %copy-done, f32[2,768,1]{1,0,2:T(2,128)S(1)} %bitcast.18), kind=kOutput, calls=%fused_computation.6 | convolution fusion | flops 4718592 | bytes 1581056 | tf_op jit(solution)/shard_map/krd,kd->kr/dot_general | solution.py:355
  98.5 2.2 %collective-permute-start.1 = (f32[64,1,1536]{2,1,0:T(1,128)S(1)}, f32[64,1,1536]{2,1,0:T(1,128)S(1)}, u32[]{:S(2)}, u32[]{:S(2)}) collective-permute-start(f32[64,1,1536]{2,1,0:T(1,128)S(1)} %get-tuple-element.8.refs_3_), channel_id=1, source_target_pairs={{0,1},{1,2},{2,3},{3,0},{4,5},{5,6},{6,7},{7,4},{8,9},{9,10},{10,1... | collective-permute-start | bytes 1179656 | tf_op jit(solution)/shard_map/ppermute | solution.py:27
  100.7 4.3 %collective-permute-start.2 = (f32[64,1,1536]{2,1,0:T(1,128)S(1)}, f32[64,1,1536]{2,1,0:T(1,128)S(1)}, u32[]{:S(2)}, u32[]{:S(2)}) collective-permute-start(f32[64,1,1536]{2,1,0:T(1,128)S(1)} %get-tuple-element.9.refs_2_), channel_id=1, source_target_pairs={{0,3},{1,0},{2,1},{3,2},{4,7},{5,4},{6,5},{7,6},{8,11},{9,8},{10,9... | collective-permute-start | bytes 1179656 | tf_op jit(solution)/shard_map/ppermute | solution.py:27
  105.0 2.9 %collective-permute-start.5 = (f32[64,1,1536]{2,1,0:T(1,128)S(1)}, f32[64,1,1536]{2,1,0:T(1,128)S(1)}, u32[]{:S(2)}, u32[]{:S(2)}) collective-permute-start(f32[64,1,1536]{2,1,0:T(1,128)S(1)} %collective-permute-done.3.refs_7_), channel_id=1, source_target_pairs={{0,3},{1,0},{2,1},{3,2},{4,7},{5,4},{6,5},{7,6},{8,11},{9,8},{10,9... | collective-permute-start | bytes 1179656 | tf_op jit(solution)/shard_map/ppermute | solution.py:27
  107.9 2.4 %collective-permute-start.4 = (f32[64,1,1536]{2,1,0:T(1,128)}, f32[64,1,1536]{2,1,0:T(1,128)S(1)}, u32[]{:S(2)}, u32[]{:S(2)}) collective-permute-start(f32[64,1,1536]{2,1,0:T(1,128)} %collective-permute-done.refs_4_), channel_id=1, source_target_pairs={{0,1},{1,2},{2,3},{3,0},{4,5},{5,6},{6,7},{7,4},{8,9},{9,10},{10,1... | collective-permute-start | bytes 1179656 | tf_op jit(solution)/shard_map/ppermute | solution.py:27
  110.5 5.6 %collective-permute-done.1.refs_5_ = f32[64,1,1536]{2,1,0:T(1,128)S(1)} collective-permute-done((f32[64,1,1536]{2,1,0:T(1,128)S(1)}, f32[64,1,1536]{2,1,0:T(1,128)S(1)}, u32[]{:S(2)}, u32[]{:S(2)}) %collective-permute-start.1) | collective-permute-done | bytes 393248 | tf_op jit(solution)/shard_map/ppermute | solution.py:27
  116.0 5.0 %near.1 = (f32[1032,768]{1,0:T(8,128)S(1)}, s32[8,128]{1,0:T(8,128)S(1)}) custom-call(s32[1]{0:T(128)} %bitcast.refs_0_, f32[4,32,128]{2,1,0:T(8,128)S(1)} %all-to-all-done.1.refs_1_, f32[64,1,1536]{2,1,0:T(1,128)S(1)} %get-tuple-element.9.refs_2_, f32[64,1,1536]{2,1,0:T(1,128)S(1)} %get-tuple-element.8.refs_3_, ...), custom_call_target="tpu_custom_call" | custom-call | tf_op jit(solution)/shard_map/near/pallas_call | solution.py:271
  121.0 3.4 %collective-permute-done.4.refs_2_ = f32[64,1,1536]{2,1,0:T(1,128)S(1)} collective-permute-done((f32[64,1,1536]{2,1,0:T(1,128)}, f32[64,1,1536]{2,1,0:T(1,128)S(1)}, u32[]{:S(2)}, u32[]{:S(2)}) %collective-permute-start.4) | collective-permute-done | bytes 393248 | tf_op jit(solution)/shard_map/ppermute | solution.py:27
  124.5 3.2 %far.1 = (f32[1032,768]{1,0:T(8,128)S(1)}, f32[1024,768]{1,0:T(8,128)}) custom-call(s32[1]{0:T(128)} %bitcast.refs_0_, s32[8,128]{1,0:T(8,128)S(1)} %get-tuple-element.5.refs_1_, f32[64,1,1536]{2,1,0:T(1,128)S(1)} %collective-permute-done.4.refs_2_, f32[64,1,1536]{2,1,0:T(1,128)S(1)} %collective-permute-done.5.refs_3_, ...), custom_call_target="tpu_custom_call", output_to_operand_aliasing={{0}: (4, {})} | custom-call | tf_op jit(solution)/shard_map/far/pallas_call | solution.py:301
  127.7 1.4 %score.1 = f32[2,256]{1,0:T(2,128)} custom-call(f32[2,256,768]{2,1,0:T(8,128)S(1)} %copy-done, f32[768,128]{1,0:T(8,128)S(1)} %bitcast.16, f32[2,128]{1,0:T(2,128)S(1)} %tile.10.penalty, f32[2,256]{1,0:T(2,128)S(1)} %fusion.2.own, f32[2,256]{1,0:T(2,128)S(1)} %compare_convert_fusion.live), custom_call_target="tpu_custom_call" | custom-call | tf_op jit(solution)/shard_map/score/pallas_call | solution.py:217
  (42 shorter events, 1.0 us)
Async XLA Ops:
  0.6 24.4 %copy-start.6 = (s32[64]{0:T(128)S(1)}, s32[64]{0:T(128)}, u32[]{:S(2)}) copy-start(s32[64]{0:T(128)} %param.13) | copy-start | bytes 772
  0.6 24.5 %copy-start.1 = (s32[256]{0:T(256)S(1)}, s32[256]{0:T(256)}, u32[]{:S(2)}) copy-start(s32[256]{0:T(256)} %param.15) | copy-start | bytes 3076
  4.6 21.4 %copy-start.4 = (s32[64,8]{0,1:T(8,128)S(1)}, s32[64,8]{0,1:T(8,128)}, u32[]{:S(2)}) copy-start(s32[64,8]{0,1:T(8,128)} %param.14) | copy-start | bytes 6148
  4.7 65.1 %all-to-all-start = ((f32[128,1,1664]{2,1,0:T(1,128)}), f32[128,1,1664]{2,1,0:T(1,128)S(1)}, u32[]{:S(2)}, u32[]{:S(2)}) async-start(f32[128,1,1664]{2,1,0:T(1,128)} %build.1), calls=%async_computation | async-start | bytes 1703936 | tf_op jit(solution)/shard_map/all_to_all | solution.py:17
  69.7 0.9 copy-start.2
  70.7 26.3 %copy-start.3 = (f32[2,768]{1,0:T(2,128)S(1)}, f32[2,768]{1,0:T(2,128)}, u32[]{:S(2)}) copy-start(f32[2,768]{1,0:T(2,128)} %param.12) | copy-start | bytes 18436
  70.7 26.4 %copy-start = (f32[2,256,768]{2,1,0:T(8,128)S(1)}, f32[2,256,768]{2,1,0:T(8,128)}, u32[]{:S(2)}) copy-start(f32[2,256,768]{2,1,0:T(8,128)} %vectors.1) | copy-start | bytes 4718596
  71.7 8.7 %all-to-all-start.1 = ((f32[4,32,128]{2,1,0:T(8,128)}), f32[4,32,128]{2,1,0:T(8,128)S(1)}, u32[]{:S(2)}, u32[]{:S(2)}) async-start(f32[4,32,128]{2,1,0:T(8,128)} %select.30), calls=%async_computation.1 | async-start | bytes 131072 | tf_op jit(solution)/shard_map/all_to_all | solution.py:17
  81.2 46.5 %all-to-all-start.2 = ((f32[32,24,128]{2,1,0:T(8,128)}), f32[32,24,128]{2,1,0:T(8,128)S(1)}, u32[]{:S(2)}, u32[]{:S(2)}) async-start(f32[32,24,128]{2,1,0:T(8,128)} %broadcast_in_dim.59), calls=%async_computation.2 | async-start | bytes 786432 | tf_op jit(solution)/shard_map/all_to_all | solution.py:17
  90.3 20.0 %copy-start.5 = (s32[2]{0:T(128)S(1)}, s32[2]{0:T(128)}, u32[]{:S(2)}) copy-start(s32[2]{0:T(128)} %refs_4_.1) | copy-start | bytes 28
  91.5 13.5 %collective-permute-start.3 = (f32[64,1,1536]{2,1,0:T(1,128)S(1)}, f32[64,1,1536]{2,1,0:T(1,128)S(1)}, u32[]{:S(2)}, u32[]{:S(2)}) collective-permute-start(f32[64,1,1536]{2,1,0:T(1,128)S(1)} %get-tuple-element.8.refs_3_), channel_id=1, source_target_pairs={{0,3},{1,0},{2,1},{3,2},{4,7},{5,4},{6,5},{7,6},{8,11},{9,8},{10,9... | collective-permute-start | bytes 1179656 | tf_op jit(solution)/shard_map/ppermute | solution.py:27
  94.3 13.5 %collective-permute-start = (f32[64,1,1536]{2,1,0:T(1,128)S(1)}, f32[64,1,1536]{2,1,0:T(1,128)}, u32[]{:S(2)}, u32[]{:S(2)}) collective-permute-start(f32[64,1,1536]{2,1,0:T(1,128)S(1)} %get-tuple-element.9.refs_2_), channel_id=1, source_target_pairs={{0,1},{1,2},{2,3},{3,0},{4,5},{5,6},{6,7},{7,4},{8,9},{9,10},{10,1... | collective-permute-start | bytes 1179656 | tf_op jit(solution)/shard_map/ppermute | solution.py:27
  98.5 17.5 %collective-permute-start.1 = (f32[64,1,1536]{2,1,0:T(1,128)S(1)}, f32[64,1,1536]{2,1,0:T(1,128)S(1)}, u32[]{:S(2)}, u32[]{:S(2)}) collective-permute-start(f32[64,1,1536]{2,1,0:T(1,128)S(1)} %get-tuple-element.8.refs_3_), channel_id=1, source_target_pairs={{0,1},{1,2},{2,3},{3,0},{4,5},{5,6},{6,7},{7,4},{8,9},{9,10},{10,1... | collective-permute-start | bytes 1179656 | tf_op jit(solution)/shard_map/ppermute | solution.py:27
  100.7 15.3 %collective-permute-start.2 = (f32[64,1,1536]{2,1,0:T(1,128)S(1)}, f32[64,1,1536]{2,1,0:T(1,128)S(1)}, u32[]{:S(2)}, u32[]{:S(2)}) collective-permute-start(f32[64,1,1536]{2,1,0:T(1,128)S(1)} %get-tuple-element.9.refs_2_), channel_id=1, source_target_pairs={{0,3},{1,0},{2,1},{3,2},{4,7},{5,4},{6,5},{7,6},{8,11},{9,8},{10,9... | collective-permute-start | bytes 1179656 | tf_op jit(solution)/shard_map/ppermute | solution.py:27
  105.0 16.0 %collective-permute-start.5 = (f32[64,1,1536]{2,1,0:T(1,128)S(1)}, f32[64,1,1536]{2,1,0:T(1,128)S(1)}, u32[]{:S(2)}, u32[]{:S(2)}) collective-permute-start(f32[64,1,1536]{2,1,0:T(1,128)S(1)} %collective-permute-done.3.refs_7_), channel_id=1, source_target_pairs={{0,3},{1,0},{2,1},{3,2},{4,7},{5,4},{6,5},{7,6},{8,11},{9,8},{10,9... | collective-permute-start | bytes 1179656 | tf_op jit(solution)/shard_map/ppermute | solution.py:27
  107.9 16.6 %collective-permute-start.4 = (f32[64,1,1536]{2,1,0:T(1,128)}, f32[64,1,1536]{2,1,0:T(1,128)S(1)}, u32[]{:S(2)}, u32[]{:S(2)}) collective-permute-start(f32[64,1,1536]{2,1,0:T(1,128)} %collective-permute-done.refs_4_), channel_id=1, source_target_pairs={{0,1},{1,2},{2,3},{3,0},{4,5},{5,6},{6,7},{7,4},{8,9},{9,10},{10,1... | collective-permute-start | bytes 1179656 | tf_op jit(solution)/shard_map/ppermute | solution.py:27

commit v8 on v6

--- a/solution.py
+++ b/solution.py
@@ -63,7 +63,7 @@
 
 
 def build_kernel(cols, pairs, me, *refs):
-    away, (out, *held, spot, scalars, sem, sems) = refs[:6], refs[6:]
+    away, (final, *held, out, spot, scalars, sem, sems) = refs[:6], refs[6:]
     fetches = [
         pltpu.make_async_copy(far, near, sems.at[i])
         for i, (far, near) in enumerate(zip(away, held))
@@ -155,26 +155,37 @@
             out[d, :, r * width : (r + 1) * width] = vectors[pl.ds(scalars[r, d], 1), :]
         return carry
 
-    lax.fori_loop(0, moves, body, 0, unroll=4)
+    stores = []
+    for part in range(4):
+        lines = moves // 4
+        lax.fori_loop(part * lines, (part + 1) * lines, body, 0, unroll=8)
+        block = pl.ds(part * lines, lines)
+        stores.append(
+            pltpu.make_async_copy(out.at[block], final.at[block], sems.at[len(away) + part])
+        )
+        stores[-1].start()
+    for store in stores:
+        store.wait()
 
 
 def built(me, sizes, source, dest, owner, labels, vectors, cols, pairs):
     smem = pl.BlockSpec(memory_space=pltpu.SMEM)
     hbm = pl.BlockSpec(memory_space=pltpu.HBM)
-    moves = dest.shape[1]
+    shape = (dest.shape[1], 1, 2 * vectors.shape[1] + LANES)
     away = [dest, owner, source, sizes, labels, vectors]
     held = [(pltpu.SMEM if x is sizes else pltpu.VMEM)(x.shape, x.dtype) for x in away]
     return pl.pallas_call(
         lambda *refs: build_kernel(cols, pairs, *refs),
-        out_shape=jax.ShapeDtypeStruct((moves, 1, 2 * vectors.shape[1] + LANES), jnp.float32),
+        out_shape=jax.ShapeDtypeStruct(shape, jnp.float32),
         in_specs=[smem] + [hbm] * len(away),
-        out_specs=pl.BlockSpec(memory_space=pltpu.VMEM),
+        out_specs=hbm,
         scratch_shapes=held
         + [
+            pltpu.VMEM(shape, jnp.float32),
             pltpu.VMEM((8, LANES), jnp.int32),
             pltpu.SMEM((8, LANES), jnp.int32),
             pltpu.SemaphoreType.DMA,
-            pltpu.SemaphoreType.DMA((len(away),)),
+            pltpu.SemaphoreType.DMA((len(away) + 4,)),
         ],
         compiler_params=pltpu.CompilerParams(vmem_limit_bytes=16 * 2**20),
         name="build",
@@ -223,7 +234,7 @@
             image[pl.ds(p, 1), :] = ref[i, :, r * width : (r + 1) * width]
         return carry
 
-    lax.fori_loop(0, ref.shape[0], body, 0, unroll=4)
+    lax.fori_loop(0, ref.shape[0], body, 0, unroll=8)
 
 
 def near_kernel(width, total, skip, me, codes, *refs):
@@ -257,7 +268,7 @@
     copy.wait()
     for at, ref in enumerate(parts):
         base = lax.rem(me[0] + (0, 3, 1)[at // 2], 4) * 2
-        put_rows(image, scalars, ref, base, at % 2 * (lines // 2), width)
+        put_rows(image, scalars, ref, base, at % 2 * parts[0].shape[0], width)
 
 
 def near_rows(me, codes, parts, width, total, skip):
@@ -355,7 +366,7 @@
     own_dist = jnp.sum(centroids * centroids, axis=1)[:, None] - 2.0 * own_cross
     gains = scored(vectors, cents, penalty, own_dist, live)
 
-    cut = lists_count // 2
+    cut = lists_count * 9 // 16
     low, high = got[:cut, :, : depth * width], got[cut:, :, : depth * width]
     below_low = turned(low, "help", 1)
     above_high = turned(high, "help", -1)

time: 120 us -> 124 us (1.033)
  waiting for transfers between devices: 42.2 us -> 45.8 us
    all_to_all x3, waiting for transfers between devices: 39.7 us -> 43.5 us  [exchanged(): return lax.all_to_all(pieces, axis, 0, 0, tiled=True)]
    all_to_all x3, starting transfers between devices: 33.5 us -> 35.2 us  [exchanged(): return lax.all_to_all(pieces, axis, 0, 0, tiled=True)]
  transfers between devices with their start and end apart: 9 -> 9, of which waited for: 3 -> 3; matrix products, arithmetic and copies ran while one was open for 6% -> 6% of each run, Pallas kernels for 8% -> 7%
where the time goes in v8:
time: 124 us; the launch traced here: 123 us
  starting transfers between devices  53.5 us (43%)
  waiting for transfers between devices  45.8 us (37%)
  Pallas kernels  15.5 us (12%)
  local copies, waits for them, and re-layouts  5.74 us (5%)
  matrix products  1.42 us (1%)
    all_to_all x3, waiting for transfers between devices, exchanged(): return lax.all_to_all(pieces, axis, 0, 0, tiled=True)  43.5 us
    all_to_all x3, starting transfers between devices, exchanged(): return lax.all_to_all(pieces, axis, 0, 0, tiled=True)  35.2 us
    ppermute x6, starting transfers between devices, turned(): lax.ppermute(block, axis, [(i, (i + step) % length) for i in range(length)])  18.3 us
    pallas_call x1, Pallas kernels, near_rows(): pl.pallas_call(lambda *refs: near_kernel(width, total, skip, *refs), out_...  5.3 us
    pallas_call x1, Pallas kernels, built(): pl.pallas_call(lambda *refs: build_kernel(cols, pairs, *refs), out_shape=...  3.98 us
    gather x3, local copies, waits for them, and re-layouts, local(): near_slots = owner_map[nearby]  3.65 us
    pallas_call x1, Pallas kernels, far_rows(): pl.pallas_call(lambda *refs: far_kernel(width, total, *refs), out_shape=(...  3.62 us
  transfers between devices with their start and end apart: 9, of which 3 were waited for; matrix products, arithmetic and copies ran while one was open for 6% of the time, Pallas kernels for 7%

profile of v8, /device:TPU:1, one launch (start us, length us, event | category | flops | bytes accessed | tf_op | source)
XLA Modules:
  0.0 123.5 jit_solution(2806296528269272157)
XLA Ops:
  0.7 4.0 %build.1 = f32[128,1,1664]{2,1,0:T(1,128)} custom-call(s32[1]{0:T(128)} %bitcast.refs_0_, s32[1,128]{1,0:T(1,128)} %bitcast.24, s32[1,256]{1,0:T(1,128)} %bitcast.20, s32[1,128]{1,0:T(1,128)} %bitcast.25, s32[2]{0:T(128)} %refs_4_.1, s32[2,256]{1,0:T(2,128)} %refs_5_.1, f32[512,768]{1,0:T(8,128)} %bitcast.17), custom_call_target="tpu_custom_call" | custom-call | tf_op jit(solution)/shard_map/build/pallas_call | solution.py:177
  4.7 20.4 %all-to-all-start = ((f32[128,1,1664]{2,1,0:T(1,128)}), f32[128,1,1664]{2,1,0:T(1,128)S(1)}, u32[]{:S(2)}, u32[]{:S(2)}) async-start(f32[128,1,1664]{2,1,0:T(1,128)} %build.1), calls=%async_computation | async-start | bytes 1703936 | tf_op jit(solution)/shard_map/all_to_all | solution.py:18
  25.1 0.8 gather_fusion
  26.1 0.1 reshape.139
  26.2 43.5 %all-to-all-done = f32[128,1,1664]{2,1,0:T(1,128)S(1)} async-done(((f32[128,1,1664]{2,1,0:T(1,128)}), f32[128,1,1664]{2,1,0:T(1,128)S(1)}, u32[]{:S(2)}, u32[]{:S(2)}) %all-to-all-start) | async-done | bytes 852000 | tf_op jit(solution)/shard_map/all_to_all | solution.py:18
  69.8 1.1 select.30
  70.9 8.0 %all-to-all-start.1 = ((f32[16,32,128]{2,1,0:T(8,128)}), f32[16,32,128]{2,1,0:T(8,128)S(1)}, u32[]{:S(2)}, u32[]{:S(2)}) async-start(f32[16,32,128]{2,1,0:T(8,128)} %select.30), calls=%async_computation.1 | async-start | bytes 524288 | tf_op jit(solution)/shard_map/all_to_all | solution.py:18
  79.0 3.5 %gather_fusion.1 = s32[512]{0:T(512)S(1)} fusion(s32[256]{0:T(256)S(1)} %copy-done.1, s32[1024]{0:T(1024)S(1)} %pad_clamp_fusion), kind=kCustom, calls=%fused_computation.1 | custom fusion | bytes 6144 | tf_op jit(solution)/shard_map/gather | solution.py:360
  82.7 0.1 compare_reduce_fusion
  82.9 4.6 %collective-permute-start.3 = (f32[56,1,1536]{2,1,0:T(1,128)S(1)}, f32[56,1,1536]{2,1,0:T(1,128)}, u32[]{:S(2)}, u32[]{:S(2)}) collective-permute-start(f32[56,1,1536]{2,1,0:T(1,128)S(1)} %slice.33.refs_3_), channel_id=1, source_target_pairs={{0,3},{1,0},{2,1},{3,2},{4,7},{5,4},{6,5},{7,6},{8,11},{9,8},{10,9... | collective-permute-start | bytes 1032200 | tf_op jit(solution)/shard_map/ppermute | solution.py:28
  87.6 1.9 %collective-permute-start = (f32[72,1,1536]{2,1,0:T(1,128)S(1)}, f32[72,1,1536]{2,1,0:T(1,128)}, u32[]{:S(2)}, u32[]{:S(2)}) collective-permute-start(f32[72,1,1536]{2,1,0:T(1,128)S(1)} %slice.32.refs_2_), channel_id=1, source_target_pairs={{0,1},{1,2},{2,3},{3,0},{4,5},{5,6},{6,7},{7,4},{8,9},{9,10},{10,1... | collective-permute-start | bytes 1327112 | tf_op jit(solution)/shard_map/ppermute | solution.py:28
  89.5 1.4 %fusion = f32[2,1,256]{2,1,0:T(1,128)S(1)} fusion(f32[2,256,768]{2,1,0:T(8,128)S(1)} %copy-done, f32[2,768,1]{1,0,2:T(2,128)S(1)} %bitcast.22), kind=kOutput, calls=%fused_computation.6 | convolution fusion | flops 4718592 | bytes 1581056 | tf_op jit(solution)/shard_map/krd,kd->kr/dot_general | solution.py:365
  90.9 2.2 %collective-permute-start.1 = (f32[56,1,1536]{2,1,0:T(1,128)S(1)}, f32[56,1,1536]{2,1,0:T(1,128)}, u32[]{:S(2)}, u32[]{:S(2)}) collective-permute-start(f32[56,1,1536]{2,1,0:T(1,128)S(1)} %slice.33.refs_3_), channel_id=1, source_target_pairs={{0,1},{1,2},{2,3},{3,0},{4,5},{5,6},{6,7},{7,4},{8,9},{9,10},{10,1... | collective-permute-start | bytes 1032200 | tf_op jit(solution)/shard_map/ppermute | solution.py:28
  93.1 4.3 %collective-permute-start.2 = (f32[72,1,1536]{2,1,0:T(1,128)S(1)}, f32[72,1,1536]{2,1,0:T(1,128)}, u32[]{:S(2)}, u32[]{:S(2)}) collective-permute-start(f32[72,1,1536]{2,1,0:T(1,128)S(1)} %slice.32.refs_2_), channel_id=1, source_target_pairs={{0,3},{1,0},{2,1},{3,2},{4,7},{5,4},{6,5},{7,6},{8,11},{9,8},{10,9... | collective-permute-start | bytes 1327112 | tf_op jit(solution)/shard_map/ppermute | solution.py:28
  97.5 3.4 %collective-permute-start.5 = (f32[56,1,1536]{2,1,0:T(1,128)}, f32[56,1,1536]{2,1,0:T(1,128)}, u32[]{:S(2)}, u32[]{:S(2)}) collective-permute-start(f32[56,1,1536]{2,1,0:T(1,128)} %collective-permute-done.3.refs_7_), channel_id=1, source_target_pairs={{0,3},{1,0},{2,1},{3,2},{4,7},{5,4},{6,5},{7,6},{8,11},{9,8},{10,9... | collective-permute-start | bytes 1032200 | tf_op jit(solution)/shard_map/ppermute | solution.py:28
  100.8 0.8 collective-permute-done.refs_4_
  101.6 1.9 %collective-permute-start.4 = (f32[72,1,1536]{2,1,0:T(1,128)}, f32[72,1,1536]{2,1,0:T(1,128)S(1)}, u32[]{:S(2)}, u32[]{:S(2)}) collective-permute-start(f32[72,1,1536]{2,1,0:T(1,128)} %collective-permute-done.refs_4_), channel_id=1, source_target_pairs={{0,1},{1,2},{2,3},{3,0},{4,5},{5,6},{6,7},{7,4},{8,9},{9,10},{10,1... | collective-permute-start | bytes 1327112 | tf_op jit(solution)/shard_map/ppermute | solution.py:28
  103.6 0.8 broadcast_in_dim.61
  104.4 6.8 %all-to-all-start.2 = ((f32[8,96,128]{2,1,0:T(8,128)}), f32[8,96,128]{2,1,0:T(8,128)S(1)}, u32[]{:S(2)}, u32[]{:S(2)}) async-start(f32[8,96,128]{2,1,0:T(8,128)} %broadcast_in_dim.61), calls=%async_computation.2 | async-start | bytes 786432 | tf_op jit(solution)/shard_map/all_to_all | solution.py:18
  111.4 0.1 multiply_reduce_fusion
  111.6 5.3 %near.1 = (f32[1032,768]{1,0:T(8,128)S(1)}, s32[8,128]{1,0:T(8,128)S(1)}) custom-call(s32[2]{0:T(128)S(1)} %pad_add_fusion.refs_0_, f32[16,32,128]{2,1,0:T(8,128)S(1)} %all-to-all-done.1.refs_1_, f32[72,1,1536]{2,1,0:T(1,128)S(1)} %slice.32.refs_2_, f32[56,1,1536]{2,1,0:T(1,128)S(1)} %slice.33.refs_3_, f32[72,1,1536]{2,1,0:T(1,128)} %collective-permute-done.refs_4_, ...), custom_call_target="tpu_custom_call" | custom-call | tf_op jit(solution)/shard_map/near/pallas_call | solution.py:276
  116.9 1.5 %collective-permute-done.4.refs_2_ = f32[72,1,1536]{2,1,0:T(1,128)S(1)} collective-permute-done((f32[72,1,1536]{2,1,0:T(1,128)}, f32[72,1,1536]{2,1,0:T(1,128)S(1)}, u32[]{:S(2)}, u32[]{:S(2)}) %collective-permute-start.4) | collective-permute-done | bytes 442400 | tf_op jit(solution)/shard_map/ppermute | solution.py:28
  118.4 3.6 %far.1 = (f32[1032,768]{1,0:T(8,128)S(1)}, f32[1024,768]{1,0:T(8,128)}) custom-call(s32[1]{0:T(128)} %bitcast.refs_0_, s32[8,128]{1,0:T(8,128)S(1)} %get-tuple-element.5.refs_1_, f32[72,1,1536]{2,1,0:T(1,128)S(1)} %collective-permute-done.4.refs_2_, f32[56,1,1536]{2,1,0:T(1,128)} %collective-permute-done.5.refs_3_, ...), custom_call_target="tpu_custom_call", output_to_operand_aliasing={{0}: (4, {})} | custom-call | tf_op jit(solution)/shard_map/far/pallas_call | solution.py:306
  122.0 1.4 %score.1 = f32[2,256]{1,0:T(2,128)} custom-call(f32[2,256,768]{2,1,0:T(8,128)S(1)} %copy-done, f32[768,128]{1,0:T(8,128)S(1)} %bitcast.19, f32[2,128]{1,0:T(2,128)S(1)} %tile.10.penalty, f32[2,256]{1,0:T(2,128)S(1)} %fusion.2.own, f32[2,256]{1,0:T(2,128)S(1)} %compare_convert_fusion.live), custom_call_target="tpu_custom_call" | custom-call | tf_op jit(solution)/shard_map/score/pallas_call | solution.py:220
  (42 shorter events, 0.9 us)
Async XLA Ops:
  0.6 24.4 %copy-start.5 = (s32[64]{0:T(128)S(1)}, s32[64]{0:T(128)}, u32[]{:S(2)}) copy-start(s32[64]{0:T(128)} %param.13) | copy-start | bytes 772
  0.6 24.5 %copy-start.1 = (s32[256]{0:T(256)S(1)}, s32[256]{0:T(256)}, u32[]{:S(2)}) copy-start(s32[256]{0:T(256)} %param.15) | copy-start | bytes 3076
  4.6 21.4 %copy-start.3 = (s32[64,8]{0,1:T(8,128)S(1)}, s32[64,8]{0,1:T(8,128)}, u32[]{:S(2)}) copy-start(s32[64,8]{0,1:T(8,128)} %param.14) | copy-start | bytes 6148
  4.7 65.1 %all-to-all-start = ((f32[128,1,1664]{2,1,0:T(1,128)}), f32[128,1,1664]{2,1,0:T(1,128)S(1)}, u32[]{:S(2)}, u32[]{:S(2)}) async-start(f32[128,1,1664]{2,1,0:T(1,128)} %build.1), calls=%async_computation | async-start | bytes 1703936 | tf_op jit(solution)/shard_map/all_to_all | solution.py:18
  70.9 32.6 %all-to-all-start.1 = ((f32[16,32,128]{2,1,0:T(8,128)}), f32[16,32,128]{2,1,0:T(8,128)S(1)}, u32[]{:S(2)}, u32[]{:S(2)}) async-start(f32[16,32,128]{2,1,0:T(8,128)} %select.30), calls=%async_computation.1 | async-start | bytes 524288 | tf_op jit(solution)/shard_map/all_to_all | solution.py:18
  79.0 3.8 %copy-start.4 = (s32[2]{0:T(128)S(1)}, s32[2]{0:T(128)}, u32[]{:S(2)}) copy-start(s32[2]{0:T(128)} %refs_4_.1) | copy-start | bytes 28
  82.5 7.0 %copy-start = (f32[2,256,768]{2,1,0:T(8,128)S(1)}, f32[2,256,768]{2,1,0:T(8,128)}, u32[]{:S(2)}) copy-start(f32[2,256,768]{2,1,0:T(8,128)} %vectors.1) | copy-start | bytes 4718596
  82.5 7.0 %copy-start.2 = (f32[2,768]{1,0:T(2,128)S(1)}, f32[2,768]{1,0:T(2,128)}, u32[]{:S(2)}) copy-start(f32[2,768]{1,0:T(2,128)} %param.12) | copy-start | bytes 18436
  82.9 14.6 %collective-permute-start.3 = (f32[56,1,1536]{2,1,0:T(1,128)S(1)}, f32[56,1,1536]{2,1,0:T(1,128)}, u32[]{:S(2)}, u32[]{:S(2)}) collective-permute-start(f32[56,1,1536]{2,1,0:T(1,128)S(1)} %slice.33.refs_3_), channel_id=1, source_target_pairs={{0,3},{1,0},{2,1},{3,2},{4,7},{5,4},{6,5},{7,6},{8,11},{9,8},{10,9... | collective-permute-start | bytes 1032200 | tf_op jit(solution)/shard_map/ppermute | solution.py:28
  87.6 14.1 %collective-permute-start = (f32[72,1,1536]{2,1,0:T(1,128)S(1)}, f32[72,1,1536]{2,1,0:T(1,128)}, u32[]{:S(2)}, u32[]{:S(2)}) collective-permute-start(f32[72,1,1536]{2,1,0:T(1,128)S(1)} %slice.32.refs_2_), channel_id=1, source_target_pairs={{0,1},{1,2},{2,3},{3,0},{4,5},{5,6},{6,7},{7,4},{8,9},{9,10},{10,1... | collective-permute-start | bytes 1327112 | tf_op jit(solution)/shard_map/ppermute | solution.py:28
  90.9 20.6 %collective-permute-start.1 = (f32[56,1,1536]{2,1,0:T(1,128)S(1)}, f32[56,1,1536]{2,1,0:T(1,128)}, u32[]{:S(2)}, u32[]{:S(2)}) collective-permute-start(f32[56,1,1536]{2,1,0:T(1,128)S(1)} %slice.33.refs_3_), channel_id=1, source_target_pairs={{0,1},{1,2},{2,3},{3,0},{4,5},{5,6},{6,7},{7,4},{8,9},{9,10},{10,1... | collective-permute-start | bytes 1032200 | tf_op jit(solution)/shard_map/ppermute | solution.py:28
  93.1 18.5 %collective-permute-start.2 = (f32[72,1,1536]{2,1,0:T(1,128)S(1)}, f32[72,1,1536]{2,1,0:T(1,128)}, u32[]{:S(2)}, u32[]{:S(2)}) collective-permute-start(f32[72,1,1536]{2,1,0:T(1,128)S(1)} %slice.32.refs_2_), channel_id=1, source_target_pairs={{0,3},{1,0},{2,1},{3,2},{4,7},{5,4},{6,5},{7,6},{8,11},{9,8},{10,9... | collective-permute-start | bytes 1327112 | tf_op jit(solution)/shard_map/ppermute | solution.py:28
  97.5 19.4 %collective-permute-start.5 = (f32[56,1,1536]{2,1,0:T(1,128)}, f32[56,1,1536]{2,1,0:T(1,128)}, u32[]{:S(2)}, u32[]{:S(2)}) collective-permute-start(f32[56,1,1536]{2,1,0:T(1,128)} %collective-permute-done.3.refs_7_), channel_id=1, source_target_pairs={{0,3},{1,0},{2,1},{3,2},{4,7},{5,4},{6,5},{7,6},{8,11},{9,8},{10,9... | collective-permute-start | bytes 1032200 | tf_op jit(solution)/shard_map/ppermute | solution.py:28
  101.6 16.7 %collective-permute-start.4 = (f32[72,1,1536]{2,1,0:T(1,128)}, f32[72,1,1536]{2,1,0:T(1,128)S(1)}, u32[]{:S(2)}, u32[]{:S(2)}) collective-permute-start(f32[72,1,1536]{2,1,0:T(1,128)} %collective-permute-done.refs_4_), channel_id=1, source_target_pairs={{0,1},{1,2},{2,3},{3,0},{4,5},{5,6},{6,7},{7,4},{8,9},{9,10},{10,1... | collective-permute-start | bytes 1327112 | tf_op jit(solution)/shard_map/ppermute | solution.py:28
  104.4 17.6 %all-to-all-start.2 = ((f32[8,96,128]{2,1,0:T(8,128)}), f32[8,96,128]{2,1,0:T(8,128)S(1)}, u32[]{:S(2)}, u32[]{:S(2)}) async-start(f32[8,96,128]{2,1,0:T(8,128)} %broadcast_in_dim.61), calls=%async_computation.2 | async-start | bytes 786432 | tf_op jit(solution)/shard_map/all_to_all | solution.py:18
